TPU v7x, 32 devices: a whole 2x2x4 slice. The times are simulated.
32 devices in a mesh: doc: 8 (over y, x, core), ctx: 4 (over z).
Axes of the slice: x: 2, y: 2, z: 4, core: 2. Of those that a mesh axis runs over, the one named last changes fastest.
Arguments:
- layer_input: bfloat16 [16, 576, 1024], P('doc', 'ctx'), may hold values from -6 to 6
- text_count: int32 [16], P('doc'), may hold values from 51 to 512
- coords: int32 [16, 2, 576], P('doc'), may hold values from 0 to 31
- w_qkv: bfloat16 [2, 1024, 3072], P(None, ('doc', 'ctx')), may hold values from -0.1875 to 0.1875
- w_out: bfloat16 [2, 1024, 1024], P(None, ('doc', 'ctx')), may hold values from -0.5 to 0.5
- w_in: bfloat16 [2, 1024, 4096], P(None, ('doc', 'ctx')), may hold values from -0.1875 to 0.1875
- w_down: bfloat16 [2, 4096, 1024], P(None, ('doc', 'ctx')), may hold values from -0.09375 to 0.09375
- rel_tables: bfloat16 [2, 2, 128, 1024], P(None, None, None, ('doc', 'ctx')), may hold values from -6 to 6
- ln_gains: bfloat16 [2, 2, 1024], P(None, None, ('doc', 'ctx')), may hold values from 0.5 to 1.5
- biases: bfloat16 [2, 7, 1024], P(None, None, ('doc', 'ctx')), may hold values from -3 to 3
- b_in: bfloat16 [2, 4096], P(None, ('doc', 'ctx')), may hold values from -3 to 3
- cotangent: bfloat16 [16, 576, 1024], P('doc', 'ctx'), may hold values from -6 to 6
Outputs:
- out_first: float32 [16, 576, 1024], P('doc', 'ctx')
- out_second: float32 [16, 576, 1024], P('doc', 'ctx')
- grad_input: float32 [16, 576, 1024], P('doc', 'ctx')
- grad_w_qkv: float32 [2, 1024, 3072], P(None, ('doc', 'ctx'))
- grad_w_out: float32 [2, 1024, 1024], P(None, ('doc', 'ctx'))
- grad_w_in: float32 [2, 1024, 4096], P(None, ('doc', 'ctx'))
- grad_w_down: float32 [2, 4096, 1024], P(None, ('doc', 'ctx'))
- grad_rel_tables: float32 [2, 2, 128, 1024], P(None, None, None, ('doc', 'ctx'))
- grad_ln_gains: float32 [2, 2, 1024], P(None, None, ('doc', 'ctx'))
- grad_biases: float32 [2, 7, 1024], P(None, None, ('doc', 'ctx'))
- grad_b_in: float32 [2, 4096], P(None, ('doc', 'ctx'))
All inputs are finite; a program needn't handle non-finite values.
Results may differ from a plain program's by a relative error of at most 0.028.
Values may be sent and summed in bfloat16 or wider, within the bound.
No kernel may reach another device: no remote copies, remote signals or barrier semaphores. Data moves between devices by JAX's collectives and lax.ppermute only.
A program may use at most 384 MiB of HBM per device.

v0:
```python
import jax
import jax.numpy as jnp
from jax import lax
from jax.sharding import PartitionSpec as P

HEADS = 16
HEAD_DIM = 64
BUCKETS = 128
TEXT = 512
PATCH = 49
MICRO = 2


NORM_EPSILON = 1e-05
TOP_PRECISION = lax.Precision.HIGHEST


def norm_rows(values_in, scale_gain, offset):
    centered = values_in - jnp.mean(values_in, axis=-1, keepdims=True)
    spread = jnp.mean(centered * centered, axis=-1, keepdims=True)
    return centered * lax.rsqrt(spread + NORM_EPSILON) * scale_gain + offset


def exact_gelu(values_in):
    return jax.nn.gelu(values_in, approximate=False)


def bucket_tables(batch_coords, batch_counts, row_count, row_start):
    docs_here = batch_coords.shape[0]
    seq_len = batch_coords.shape[2]
    key_place = jnp.arange(seq_len, dtype=jnp.int32)
    query_place = row_start + jnp.arange(row_count, dtype=jnp.int32)
    half_range = BUCKETS // 2
    linear = (
        jnp.clip(query_place[:, None] - key_place[None, :], -half_range, half_range - 1)
        + half_range
    )
    query_cells = lax.dynamic_slice_in_dim(batch_coords, row_start, row_count, 2)
    across = jnp.clip(query_cells[:, 0, :, None] - batch_coords[:, 0, None, :], -8, 7) + 8
    upward = jnp.clip(query_cells[:, 1, :, None] - batch_coords[:, 1, None, :], -4, 3) + 4
    planar = across * 8 + upward
    levels = jnp.arange(BUCKETS, dtype=jnp.int32)
    linear_hot = (linear[:, :, None] == levels).astype(jnp.bfloat16)[None]
    planar_hot = (planar[:, :, :, None] == levels).astype(jnp.bfloat16)
    patch_rows = (key_place >= TEXT) & (key_place < TEXT + PATCH)
    key_valid = (key_place[None, :] < batch_counts[:, None]) | patch_rows[None, :]
    return ((linear_hot, planar_hot), key_valid)


def fetch_forward(shards):
    return (
        lax.all_gather(shards[0], ("doc", "ctx"), axis=0, tiled=True),
        lax.all_gather(shards[1], ("doc", "ctx"), axis=0, tiled=True),
        lax.all_gather(shards[2], ("doc", "ctx"), axis=0, tiled=True),
        lax.all_gather(shards[3], ("doc", "ctx"), axis=0, tiled=True),
        lax.all_gather(shards[4], ("doc", "ctx"), axis=2, tiled=True),
        lax.all_gather(shards[5], ("doc", "ctx"), axis=1, tiled=True),
        lax.all_gather(shards[6], ("doc", "ctx"), axis=1, tiled=True),
        lax.all_gather(shards[7], ("doc", "ctx"), axis=0, tiled=True),
    )


def fetch_backward(shards):
    return (
        lax.all_gather(shards[0], ("doc", "ctx"), axis=0, tiled=True),
        lax.all_gather(shards[1], ("doc", "ctx"), axis=0, tiled=True),
        lax.all_gather(shards[2], ("doc", "ctx"), axis=0, tiled=True),
        lax.all_gather(shards[3], ("doc", "ctx"), axis=0, tiled=True),
        lax.all_gather(shards[4], ("doc", "ctx"), axis=2, tiled=True),
        lax.all_gather(shards[5], ("doc", "ctx"), axis=1, tiled=True),
        lax.all_gather(shards[6], ("doc", "ctx"), axis=1, tiled=True),
        lax.all_gather(shards[7], ("doc", "ctx"), axis=0, tiled=True),
    )


def scatter_end(grad_terms):
    return (
        lax.psum_scatter(grad_terms[0], ("doc", "ctx"), scatter_dimension=0, tiled=True),
        lax.psum_scatter(grad_terms[1], ("doc", "ctx"), scatter_dimension=0, tiled=True),
        lax.psum_scatter(grad_terms[2], ("doc", "ctx"), scatter_dimension=0, tiled=True),
        lax.psum_scatter(grad_terms[3], ("doc", "ctx"), scatter_dimension=0, tiled=True),
        lax.psum_scatter(grad_terms[4], ("doc", "ctx"), scatter_dimension=2, tiled=True),
        lax.psum_scatter(grad_terms[5], ("doc", "ctx"), scatter_dimension=1, tiled=True),
        lax.psum_scatter(grad_terms[6], ("doc", "ctx"), scatter_dimension=1, tiled=True),
        lax.psum_scatter(grad_terms[7], ("doc", "ctx"), scatter_dimension=0, tiled=True),
    )


def add_terms(summed, grad_terms):
    if summed is None:
        return tuple(grad_terms)
    return tuple((left_term + right_term for left_term, right_term in zip(summed, grad_terms)))


def layer_forward(rows_in, full_weights, bucket_hots, key_valid):
    (
        w_qkv_full,
        w_out_full,
        w_in_full,
        w_down_full,
        tables_full,
        gains_full,
        biases_full,
        b_in_full,
    ) = full_weights
    doc_count, row_count, feature_width = rows_in.shape
    seq_len = key_valid.shape[1]
    gains_wide = gains_full.astype(jnp.float32)
    biases_wide = biases_full.astype(jnp.float32)
    rows_low = rows_in.astype(jnp.bfloat16)
    projected = jnp.einsum("nrd,de->nre", rows_low, w_qkv_full, preferred_element_type=jnp.float32)
    projected = projected + jnp.concatenate([biases_wide[0], biases_wide[1], biases_wide[2]])
    query_low = projected[:, :, :feature_width].astype(jnp.bfloat16)
    key_low = projected[:, :, feature_width : 2 * feature_width].astype(jnp.bfloat16)
    value_low = projected[:, :, 2 * feature_width :].astype(jnp.bfloat16)
    rel_key = (
        jnp.einsum(
            "tbd,de->tbe",
            tables_full,
            w_qkv_full[:, feature_width : 2 * feature_width],
            preferred_element_type=jnp.float32,
        )
        .astype(jnp.bfloat16)
        .reshape(2, BUCKETS, HEADS, HEAD_DIM)
    )
    rel_query = (
        jnp.einsum(
            "tbd,de->tbe",
            tables_full,
            w_qkv_full[:, :feature_width],
            preferred_element_type=jnp.float32,
        )
        .astype(jnp.bfloat16)
        .reshape(2, BUCKETS, HEADS, HEAD_DIM)
    )
    query_heads = query_low.reshape(doc_count, row_count, HEADS, HEAD_DIM)
    key_heads = key_low.reshape(doc_count, row_count, HEADS, HEAD_DIM)
    query_rel = jnp.einsum(
        "nihe,tbhe->nthib", query_heads, rel_key, preferred_element_type=jnp.float32
    ).astype(jnp.bfloat16)
    key_rel = jnp.einsum(
        "nihe,tbhe->nithb", key_heads, rel_query, preferred_element_type=jnp.float32
    ).astype(jnp.bfloat16)
    key_all, value_all, key_rel_all = (
        lax.all_gather(key_low, "ctx", axis=1, tiled=True),
        lax.all_gather(value_low, "ctx", axis=1, tiled=True),
        lax.all_gather(key_rel, "ctx", axis=1, tiled=True),
    )
    key_all_heads = key_all.reshape(doc_count, seq_len, HEADS, HEAD_DIM)
    value_all_heads = value_all.reshape(doc_count, seq_len, HEADS, HEAD_DIM)
    raw_scores = jnp.einsum(
        "nihe,njhe->nhij", query_heads, key_all_heads, preferred_element_type=jnp.float32
    )
    for kind_index in range(2):
        raw_scores = raw_scores + jnp.einsum(
            "nhib,nijb->nhij",
            query_rel[:, kind_index],
            bucket_hots[kind_index],
            preferred_element_type=jnp.float32,
        )
        raw_scores = raw_scores + jnp.einsum(
            "njhb,nijb->nhij",
            key_rel_all[:, :, kind_index],
            bucket_hots[kind_index],
            preferred_element_type=jnp.float32,
        )
    score_scale = (3.0 * HEAD_DIM) ** (-0.5)
    scaled = jnp.where(key_valid[:, None, None, :], raw_scores * score_scale, -jnp.inf)
    shifted = scaled - jnp.max(scaled, axis=-1, keepdims=True)
    exponent = jnp.exp(shifted)
    soft_weights = exponent / jnp.sum(exponent, axis=-1, keepdims=True)
    soft_low = soft_weights.astype(jnp.bfloat16)
    mixed_rows = jnp.einsum(
        "nhij,njhe->nihe", soft_low, value_all_heads, preferred_element_type=jnp.float32
    )
    mixed_low = mixed_rows.reshape(doc_count, row_count, feature_width).astype(jnp.bfloat16)
    attended = (
        jnp.einsum("nrd,de->nre", mixed_low, w_out_full, preferred_element_type=jnp.float32)
        + biases_wide[3]
    )
    first_sum = rows_in + attended
    first_norm = norm_rows(first_sum, gains_wide[0], biases_wide[5])
    norm_low = first_norm.astype(jnp.bfloat16)
    hidden_pre = jnp.einsum(
        "nrd,df->nrf", norm_low, w_in_full, preferred_element_type=jnp.float32
    ) + b_in_full.astype(jnp.float32)
    active_low = exact_gelu(hidden_pre).astype(jnp.bfloat16)
    down_rows = (
        jnp.einsum("nrf,fd->nrd", active_low, w_down_full, preferred_element_type=jnp.float32)
        + biases_wide[4]
    )
    second_sum = first_norm + down_rows
    result = norm_rows(second_sum, gains_wide[1], biases_wide[6])
    forward_kept = (
        rows_low,
        query_heads,
        key_heads,
        rel_key,
        rel_query,
        key_all_heads,
        value_all_heads,
        soft_weights,
        soft_low,
        mixed_low,
        first_sum,
        norm_low,
        hidden_pre,
        active_low,
        second_sum,
    )
    return (result, forward_kept)


def layer_backward(grad_out, forward_kept, full_weights, bucket_hots, key_valid):
    (
        rows_low,
        query_heads,
        key_heads,
        rel_key,
        rel_query,
        key_all_heads,
        value_all_heads,
        soft_weights,
        soft_low,
        mixed_low,
        first_sum,
        norm_low,
        hidden_pre,
        active_low,
        second_sum,
    ) = forward_kept
    (
        w_qkv_full,
        w_out_full,
        w_in_full,
        w_down_full,
        tables_full,
        gains_full,
        biases_full,
        b_in_full,
    ) = full_weights
    doc_count, row_count, feature_width = grad_out.shape
    seq_len = key_valid.shape[1]
    gains_wide = gains_full.astype(jnp.float32)
    biases_wide = biases_full.astype(jnp.float32)
    score_scale = (3.0 * HEAD_DIM) ** (-0.5)
    _, second_pull = jax.vjp(norm_rows, second_sum, gains_wide[1], biases_wide[6])
    grad_second, grad_gain_two, grad_offset_two = second_pull(grad_out)
    grad_down_low = grad_second.astype(jnp.bfloat16)
    grad_w_down = jnp.einsum(
        "nrf,nrd->fd", active_low, grad_down_low, preferred_element_type=jnp.float32
    )
    grad_b_down = jnp.sum(grad_down_low.astype(jnp.float32), axis=(0, 1))
    grad_active = jnp.einsum(
        "nrd,fd->nrf", grad_down_low, w_down_full, preferred_element_type=jnp.float32
    )
    _, gelu_pull = jax.vjp(exact_gelu, hidden_pre)
    grad_hidden_low = gelu_pull(grad_active)[0].astype(jnp.bfloat16)
    grad_w_in = jnp.einsum(
        "nrd,nrf->df", norm_low, grad_hidden_low, preferred_element_type=jnp.float32
    )
    grad_b_in = jnp.sum(grad_hidden_low.astype(jnp.float32), axis=(0, 1))
    grad_first_norm = grad_second + jnp.einsum(
        "nrf,df->nrd", grad_hidden_low, w_in_full, preferred_element_type=jnp.float32
    )
    _, first_pull = jax.vjp(norm_rows, first_sum, gains_wide[0], biases_wide[5])
    grad_first, grad_gain_one, grad_offset_one = first_pull(grad_first_norm)
    grad_att_low = grad_first.astype(jnp.bfloat16)
    grad_w_out = jnp.einsum(
        "nrd,nre->de", mixed_low, grad_att_low, preferred_element_type=jnp.float32
    )
    grad_b_out = jnp.sum(grad_att_low.astype(jnp.float32), axis=(0, 1))
    grad_mixed = jnp.einsum(
        "nre,de->nrd", grad_att_low, w_out_full, preferred_element_type=jnp.float32
    )
    grad_mixed_heads = grad_mixed.astype(jnp.bfloat16).reshape(
        doc_count, row_count, HEADS, HEAD_DIM
    )
    grad_soft = jnp.einsum(
        "nihe,njhe->nhij", grad_mixed_heads, value_all_heads, preferred_element_type=jnp.float32
    )
    grad_value_part = jnp.einsum(
        "nhij,nihe->njhe", soft_low, grad_mixed_heads, preferred_element_type=jnp.float32
    ).reshape(doc_count, seq_len, feature_width)
    grad_scaled = soft_weights * (
        grad_soft - jnp.sum(soft_weights * grad_soft, axis=-1, keepdims=True)
    )
    grad_raw_low = (grad_scaled * score_scale).astype(jnp.bfloat16)
    grad_query = jnp.einsum(
        "nhij,njhe->nihe", grad_raw_low, key_all_heads, preferred_element_type=jnp.float32
    )
    grad_key_part = jnp.einsum(
        "nhij,nihe->njhe", grad_raw_low, query_heads, preferred_element_type=jnp.float32
    )
    grad_query_rel = jnp.stack(
        [
            jnp.einsum(
                "nhij,nijb->nhib",
                grad_raw_low,
                bucket_hots[kind_index],
                preferred_element_type=jnp.float32,
            )
            for kind_index in range(2)
        ],
        axis=1,
    ).astype(jnp.bfloat16)
    grad_key_rel_part = jnp.stack(
        [
            jnp.einsum(
                "nhij,nijb->njhb",
                grad_raw_low,
                bucket_hots[kind_index],
                preferred_element_type=jnp.float32,
            )
            for kind_index in range(2)
        ],
        axis=2,
    )
    rel_query_wide = rel_query.astype(jnp.float32)
    grad_key_sum, grad_value_sum, grad_key_rel_sum = (
        lax.psum_scatter(
            grad_key_part.reshape(doc_count, seq_len, feature_width).astype(jnp.bfloat16),
            "ctx",
            scatter_dimension=1,
            tiled=True,
        ).astype(jnp.float32),
        lax.psum_scatter(
            grad_value_part.astype(jnp.bfloat16), "ctx", scatter_dimension=1, tiled=True
        ).astype(jnp.float32),
        lax.psum_scatter(
            grad_key_rel_part.astype(jnp.bfloat16), "ctx", scatter_dimension=1, tiled=True
        ).astype(jnp.float32),
    )
    grad_key = grad_key_sum.reshape(doc_count, row_count, HEADS, HEAD_DIM) + jnp.einsum(
        "nithb,tbhe->nihe", grad_key_rel_sum, rel_query_wide, precision=TOP_PRECISION
    )
    grad_rel_query = jnp.einsum(
        "nithb,nihe->tbhe", grad_key_rel_sum, key_heads.astype(jnp.float32), precision=TOP_PRECISION
    ).reshape(2, BUCKETS, feature_width)
    grad_query = grad_query + jnp.einsum(
        "nthib,tbhe->nihe", grad_query_rel, rel_key, preferred_element_type=jnp.float32
    )
    grad_qkv_low = jnp.concatenate(
        [
            grad_query.reshape(doc_count, row_count, feature_width),
            grad_key.reshape(doc_count, row_count, feature_width),
            grad_value_sum,
        ],
        axis=2,
    ).astype(jnp.bfloat16)
    grad_rel_key = jnp.einsum(
        "nthib,nihe->tbhe", grad_query_rel, query_heads, preferred_element_type=jnp.float32
    ).reshape(2, BUCKETS, feature_width)
    tables_wide = tables_full.astype(jnp.float32)
    query_block = w_qkv_full[:, :feature_width].astype(jnp.float32)
    key_block = w_qkv_full[:, feature_width : 2 * feature_width].astype(jnp.float32)
    grad_tables = jnp.einsum(
        "tbe,de->tbd", grad_rel_key, key_block, precision=TOP_PRECISION
    ) + jnp.einsum("tbe,de->tbd", grad_rel_query, query_block, precision=TOP_PRECISION)
    grad_w_qkv = jnp.einsum(
        "nrd,nre->de", rows_low, grad_qkv_low, preferred_element_type=jnp.float32
    )
    rel_columns = jnp.concatenate(
        [
            jnp.einsum("tbd,tbe->de", tables_wide, grad_rel_query, precision=TOP_PRECISION),
            jnp.einsum("tbd,tbe->de", tables_wide, grad_rel_key, precision=TOP_PRECISION),
            jnp.zeros((feature_width, feature_width), jnp.float32),
        ],
        axis=1,
    )
    grad_w_qkv = grad_w_qkv + rel_columns
    bias_sums = jnp.sum(grad_qkv_low.astype(jnp.float32), axis=(0, 1))
    grad_rows = grad_first + jnp.einsum(
        "nre,de->nrd", grad_qkv_low, w_qkv_full, preferred_element_type=jnp.float32
    )
    grad_gains = jnp.stack([grad_gain_one, grad_gain_two])
    grad_biases = jnp.stack(
        [
            bias_sums[:feature_width],
            bias_sums[feature_width : 2 * feature_width],
            bias_sums[2 * feature_width :],
            grad_b_out,
            grad_b_down,
            grad_offset_one,
            grad_offset_two,
        ]
    )
    grad_terms = (
        grad_w_qkv,
        grad_w_out,
        grad_w_in,
        grad_w_down,
        grad_tables,
        grad_gains,
        grad_biases,
        grad_b_in,
    )
    return (grad_rows, grad_terms)


def body(
    layer_input,
    text_count,
    coords,
    w_qkv,
    w_out,
    w_in,
    w_down,
    rel_tables,
    ln_gains,
    biases,
    b_in,
    cotangent,
):
    local_docs, row_count, feature_width = layer_input.shape
    layer_count = w_qkv.shape[0]
    group_docs = local_docs // MICRO
    row_start = lax.axis_index("ctx") * row_count
    batch_tables = []
    for batch_index in range(MICRO):
        first_doc = batch_index * group_docs
        batch_tables.append(
            bucket_tables(
                coords[first_doc : first_doc + group_docs],
                text_count[first_doc : first_doc + group_docs],
                row_count,
                row_start,
            )
        )
    layer_shards = [
        (
            w_qkv[layer_index],
            w_out[layer_index],
            w_in[layer_index],
            w_down[layer_index],
            rel_tables[layer_index],
            ln_gains[layer_index],
            biases[layer_index],
            b_in[layer_index],
        )
        for layer_index in range(layer_count)
    ]
    current = [
        layer_input[batch_index * group_docs : (batch_index + 1) * group_docs].astype(jnp.float32)
        for batch_index in range(MICRO)
    ]
    saved_forward = []
    layer_outputs = []
    for layer_index in range(layer_count):
        produced = []
        kept_here = []
        for batch_index in range(MICRO):
            full_weights = fetch_forward(layer_shards[layer_index])
            bucket_hots, key_valid = batch_tables[batch_index]
            result, forward_kept = layer_forward(
                current[batch_index], full_weights, bucket_hots, key_valid
            )
            produced.append(result)
            kept_here.append(forward_kept)
        saved_forward.append(kept_here)
        current = produced
        layer_outputs.append(jnp.concatenate(produced, axis=0))
    grad_batches = [
        cotangent[batch_index * group_docs : (batch_index + 1) * group_docs].astype(jnp.float32)
        for batch_index in range(MICRO)
    ]
    totals = [None] * layer_count
    for layer_index in reversed(range(layer_count)):
        summed = None
        next_grads = []
        for batch_index in range(MICRO):
            full_weights = fetch_backward(layer_shards[layer_index])
            bucket_hots, key_valid = batch_tables[batch_index]
            grad_rows, grad_terms = layer_backward(
                grad_batches[batch_index],
                saved_forward[layer_index][batch_index],
                full_weights,
                bucket_hots,
                key_valid,
            )
            next_grads.append(grad_rows)
            summed = add_terms(summed, grad_terms)
        summed = scatter_end(summed)
        totals[layer_index] = summed
        grad_batches = next_grads
    stacked = tuple(
        (
            jnp.stack([totals[layer_index][member] for layer_index in range(layer_count)])
            for member in range(8)
        )
    )
    return (layer_outputs[0], layer_outputs[-1], jnp.concatenate(grad_batches, axis=0)) + stacked


def solution(mesh):
    placed = (
        P("doc", "ctx", None),
        P("doc"),
        P("doc", None, None),
        P(None, ("doc", "ctx"), None),
        P(None, ("doc", "ctx"), None),
        P(None, ("doc", "ctx"), None),
        P(None, ("doc", "ctx"), None),
        P(None, None, None, ("doc", "ctx")),
        P(None, None, ("doc", "ctx")),
        P(None, None, ("doc", "ctx")),
        P(None, ("doc", "ctx")),
        P("doc", "ctx", None),
    )
    return jax.shard_map(
        body,
        mesh=mesh,
        in_specs=placed,
        out_specs=(
            P("doc", "ctx", None),
            P("doc", "ctx", None),
            P("doc", "ctx", None),
            P(None, ("doc", "ctx"), None),
            P(None, ("doc", "ctx"), None),
            P(None, ("doc", "ctx"), None),
            P(None, ("doc", "ctx"), None),
            P(None, None, None, ("doc", "ctx")),
            P(None, None, ("doc", "ctx")),
            P(None, None, ("doc", "ctx")),
            P(None, ("doc", "ctx")),
        ),
        check_vma=False,
    )
```

profile of v0, /device:TPU:0, one launch (start us, length us, event | category | flops | bytes accessed | tf_op | source)
XLA Modules:
  0.0 5040.2 jit_solution(3756881424795618879)
XLA Ops:
  10.0 77.9 %all-gather.1 = bf16[1,7,1024]{1,0,2:T(2,128)(2,1)S(1)} all-gather(bf16[1,7,32]{1,0,2:T(2,128)(2,1)S(1)} %copy.941), channel_id=3, replica_groups=mesh['doc'=8,'ctx'=4] {'doc','ctx'}, dimensions={2}, use_global_device_ids=true | all-gather | bytes 14784 | tf_op jit(solution)/shard_map/all_gather | solution.py:58
  88.4 22.6 slice_reduce_fusion.9
  122.9 72.6 %all-gather.2 = bf16[1,2,128,1024]{2,1,0,3:T(2,128)(2,1)S(1)} all-gather(bf16[1,2,128,32]{2,1,0,3:T(2,128)(2,1)S(1)} %copy.942), channel_id=4, replica_groups=mesh['doc'=8,'ctx'=4] {'doc','ctx'}, dimensions={3}, use_global_device_ids=true | all-gather | bytes 540672 | tf_op jit(solution)/shard_map/all_gather | solution.py:56
  209.1 17.6 iota_compare_fusion
  226.9 17.8 iota_compare_fusion.10
  246.6 77.2 %all-gather.4 = bf16[1,2,1024]{1,0,2:T(2,128)(2,1)S(1)} all-gather(bf16[1,2,32]{1,0,2:T(2,128)(2,1)S(1)} %copy.943), channel_id=6, replica_groups=mesh['doc'=8,'ctx'=4] {'doc','ctx'}, dimensions={2}, use_global_device_ids=true | all-gather | bytes 4224 | tf_op jit(solution)/shard_map/all_gather | solution.py:57
  331.7 65.8 %all-gather.6 = bf16[1,4096]{1,0:T(2,128)(2,1)S(1)} all-gather(bf16[1,128]{1,0:T(2,128)(2,1)S(1)} %get-tuple-element.235), channel_id=8, replica_groups=mesh['doc'=8,'ctx'=4] {'doc','ctx'}, dimensions={1}, use_global_device_ids=true | all-gather | bytes 8448 | tf_op jit(solution)/shard_map/all_gather | solution.py:59
  398.5 17.7 iota_compare_fusion.5
  417.6 70.1 %all-gather.9 = bf16[1,7,1024]{1,0,2:T(2,128)(2,1)S(1)} all-gather(bf16[1,7,32]{1,0,2:T(2,128)(2,1)S(1)} %copy.944), channel_id=11, replica_groups=mesh['doc'=8,'ctx'=4] {'doc','ctx'}, dimensions={2}, use_global_device_ids=true | all-gather | bytes 14784 | tf_op jit(solution)/shard_map/all_gather | solution.py:58
  488.2 22.6 slice_reduce_fusion
  521.3 16.2 fusion.489
  590.3 25.2 fusion.3
  626.8 18.9 fusion.13
  659.3 25.3 fusion.7
  684.7 25.3 fusion.15
  804.4 75.3 %all-gather.10 = bf16[1,2,128,1024]{2,1,0,3:T(2,128)(2,1)S(1)} all-gather(bf16[1,2,128,32]{2,1,0,3:T(2,128)(2,1)S(1)} %copy.945), channel_id=12, replica_groups=mesh['doc'=8,'ctx'=4] {'doc','ctx'}, dimensions={3}, use_global_device_ids=true | all-gather | bytes 540672 | tf_op jit(solution)/shard_map/all_gather | solution.py:56
  887.7 74.3 %all-gather.12 = bf16[1,2,1024]{1,0,2:T(2,128)(2,1)S(1)} all-gather(bf16[1,2,32]{1,0,2:T(2,128)(2,1)S(1)} %copy.946), channel_id=14, replica_groups=mesh['doc'=8,'ctx'=4] {'doc','ctx'}, dimensions={2}, use_global_device_ids=true | all-gather | bytes 4224 | tf_op jit(solution)/shard_map/all_gather | solution.py:57
  962.5 64.1 %all-gather.14 = bf16[1,4096]{1,0:T(2,128)(2,1)S(1)} all-gather(bf16[1,128]{1,0:T(2,128)(2,1)S(1)} %copy-done.331), channel_id=16, replica_groups=mesh['doc'=8,'ctx'=4] {'doc','ctx'}, dimensions={1}, use_global_device_ids=true | all-gather | bytes 8448 | tf_op jit(solution)/shard_map/all_gather | solution.py:59
  1048.3 16.5 fusion.46
  1108.6 25.3 fusion.5
  1134.0 25.3 fusion.11
  1205.3 35.7 all-gather.75.cloned.1.call-done
  1250.8 80.3 %all-gather.59.cloned.1.call-done = bf16[1,576,2,16,128]{4,1,2,3,0:T(8,128)(2,1)} async-done(((bf16[1,144,2,16,128]{4,1,2,3,0:T(8,128)(2,1)}), bf16[1,576,2,16,128]{4,1,2,3,0:T(8,128)(2,1)}) %all-gather.59.cloned.1.call-update) | async-done | bytes 4718608 | tf_op jit(solution)/shard_map/all_gather | solution.py:147
  1335.1 25.2 fusion.1
  1371.1 18.9 fusion.9
  1485.4 17.7 iota_compare_fusion.50
  1542.2 20.1 iota_compare_fusion.49
  1610.3 18.0 iota_compare_fusion.46
  1628.3 17.7 iota_compare_fusion.45
  1759.1 27.4 reduce-scatter.97.cloned.1.call-done
  1847.9 17.7 iota_compare_fusion.44
  1905.0 20.1 iota_compare_fusion.43
  1973.4 17.9 iota_compare_fusion.48
  1991.3 17.7 iota_compare_fusion.47
  2110.8 16.5 fusion.366
  2370.9 41.1 all-reduce.2
  2421.9 131.6 %reduce-scatter.117.cloned.1.call-done = f32[32,7]{1,0:T(8,128)} async-done(((f32[1024,7]{1,0:T(8,128)}), f32[32,7]{1,0:T(8,128)}) %reduce-scatter.117.cloned.1.call-update) | async-done | bytes 912
  2554.3 145.8 %reduce-scatter.69.cloned.1.call-done = f32[32,1024]{1,0:T(8,128)} async-done(((f32[1024,1024]{1,0:T(8,128)}), f32[32,1024]{1,0:T(8,128)}) %reduce-scatter.69.cloned.1.call-update) | async-done | bytes 131088 | tf_op jit(solution)/shard_map/reduce_scatter | solution.py:79
  2700.1 149.0 %reduce-scatter.67.cloned.1.call-done = f32[32,1024]{1,0:T(8,128)} async-done(((f32[1024,1024]{1,0:T(8,128)}), f32[32,1024]{1,0:T(8,128)}) %reduce-scatter.67.cloned.1.call-update) | async-done | bytes 131088 | tf_op jit(solution)/shard_map/reduce_scatter | solution.py:79
  2859.7 124.4 %reduce-scatter.115.cloned.1.call-done = f32[32,7]{1,0:T(8,128)} async-done(((f32[1024,7]{1,0:T(8,128)}), f32[32,7]{1,0:T(8,128)}) %reduce-scatter.115.cloned.1.call-update) | async-done | bytes 912
  2985.5 132.9 %reduce-scatter.81.cloned.1.call-done = f32[2,128,32]{1,2,0:T(8,128)} async-done(((f32[2,128,1024]{1,2,0:T(8,128)}), f32[2,128,32]{1,2,0:T(8,128)}) %reduce-scatter.81.cloned.1.call-update) | async-done | bytes 32784 | tf_op jit(solution)/shard_map/reduce_scatter | solution.py:82
  3118.4 134.1 %reduce-scatter.79.cloned.1.call-done = f32[2,128,32]{1,2,0:T(8,128)} async-done(((f32[2,128,1024]{1,2,0:T(8,128)}), f32[2,128,32]{1,2,0:T(8,128)}) %reduce-scatter.79.cloned.1.call-update) | async-done | bytes 32784 | tf_op jit(solution)/shard_map/reduce_scatter | solution.py:82
  3253.9 156.8 %reduce-scatter.109.cloned.1.call-done = f32[32,3072]{1,0:T(8,128)} async-done(((f32[1024,3072]{1,0:T(8,128)}), f32[32,3072]{1,0:T(8,128)}) %reduce-scatter.109.cloned.1.call-update) | async-done | bytes 393232
  3412.6 159.9 %reduce-scatter.107.cloned.1.call-done = f32[32,3072]{1,0:T(8,128)} async-done(((f32[1024,3072]{1,0:T(8,128)}), f32[32,3072]{1,0:T(8,128)}) %reduce-scatter.107.cloned.1.call-update) | async-done | bytes 393232
  3575.4 362.7 %reduce-scatter.77.cloned.1.call-done = f32[128,1024]{1,0:T(8,128)} async-done(((f32[4096,1024]{1,0:T(8,128)}), f32[128,1024]{1,0:T(8,128)}) %reduce-scatter.77.cloned.1.call-update) | async-done | bytes 524304 | tf_op jit(solution)/shard_map/reduce_scatter | solution.py:81
  3938.1 364.5 %reduce-scatter.75.cloned.1.call-done = f32[128,1024]{1,0:T(8,128)} async-done(((f32[4096,1024]{1,0:T(8,128)}), f32[128,1024]{1,0:T(8,128)}) %reduce-scatter.75.cloned.1.call-update) | async-done | bytes 524304 | tf_op jit(solution)/shard_map/reduce_scatter | solution.py:81
  4304.8 362.1 %reduce-scatter.73.cloned.1.call-done = f32[32,4096]{1,0:T(8,128)} async-done(((f32[1024,4096]{1,0:T(8,128)}), f32[32,4096]{1,0:T(8,128)}) %reduce-scatter.73.cloned.1.call-update) | async-done | bytes 524304 | tf_op jit(solution)/shard_map/reduce_scatter | solution.py:80
  4666.9 364.3 %reduce-scatter.71.cloned.1.call-done = f32[32,4096]{1,0:T(8,128)} async-done(((f32[1024,4096]{1,0:T(8,128)}), f32[32,4096]{1,0:T(8,128)}) %reduce-scatter.71.cloned.1.call-update) | async-done | bytes 524304 | tf_op jit(solution)/shard_map/reduce_scatter | solution.py:80
  (1322 shorter events, 1186.3 us)
Async XLA Ops:
  7.2 103.9 %all-gather.61.cloned.1.call-start = ((), (), s32[]{:S(2)}) async-start(), calls=%async_computation.46 | async-start | bytes 6488064 | tf_op jit(solution)/shard_map/all_gather | solution.py:52
  9.0 567.9 %all-gather.45.cloned.1.call-start = ((), (), s32[]{:S(2)}) async-start(), calls=%async_computation.30 | async-start | bytes 1474560 | tf_op jit(solution)/shard_map/all_gather | solution.py:145
  115.8 462.8 %all-gather.43.cloned.1.call-start = ((), (), s32[]{:S(2)}) async-start(), calls=%async_computation.29 | async-start | bytes 1474560 | tf_op jit(solution)/shard_map/all_gather | solution.py:146
  116.6 464.9 %all-gather.39.cloned.1.call-start = ((), (), s32[]{:S(2)}) async-start(), calls=%async_computation.27 | async-start | bytes 1474560 | tf_op jit(solution)/shard_map/all_gather | solution.py:145
  121.6 461.6 %all-gather.37.cloned.1.call-start = ((), (), s32[]{:S(2)}) async-start(), calls=%async_computation.26 | async-start | bytes 1474560 | tf_op jit(solution)/shard_map/all_gather | solution.py:146
  122.2 463.9 %all-gather.47.cloned.1.call-start = ((), (), s32[]{:S(2)}) async-start(), calls=%async_computation.31 | async-start | bytes 5898240 | tf_op jit(solution)/shard_map/all_gather | solution.py:147
  201.2 455.3 %all-gather.41.cloned.1.call-start = ((), (), s32[]{:S(2)}) async-start(), calls=%async_computation.28 | async-start | bytes 5898240 | tf_op jit(solution)/shard_map/all_gather | solution.py:147
  204.3 544.2 %all-gather.63.cloned.1.call-start = ((), (), s32[]{:S(2)}) async-start(), calls=%async_computation.47 | async-start | bytes 2162688 | tf_op jit(solution)/shard_map/all_gather | solution.py:53
  205.0 546.2 %all-gather.65.cloned.1.call-start = ((), (), s32[]{:S(2)}) async-start(), calls=%async_computation.48 | async-start | bytes 8650752 | tf_op jit(solution)/shard_map/all_gather | solution.py:54
  205.9 551.6 %all-gather.67.cloned.1.call-start = ((), (), s32[]{:S(2)}) async-start(), calls=%async_computation.49 | async-start | bytes 8650752 | tf_op jit(solution)/shard_map/all_gather | solution.py:55
  206.9 586.0 %all-gather.69.cloned.1.call-start = ((), (), s32[]{:S(2)}) async-start(), calls=%async_computation.50 | async-start | bytes 6488064 | tf_op jit(solution)/shard_map/all_gather | solution.py:52
  207.6 888.8 %all-gather.51.cloned.1.call-start = ((), (), s32[]{:S(2)}) async-start(), calls=%async_computation.33 | async-start | bytes 1474560 | tf_op jit(solution)/shard_map/all_gather | solution.py:145
  798.1 300.1 %all-gather.49.cloned.1.call-start = ((), (), s32[]{:S(2)}) async-start(), calls=%async_computation.32 | async-start | bytes 1474560 | tf_op jit(solution)/shard_map/all_gather | solution.py:146
  798.8 302.2 %all-gather.57.cloned.1.call-start = ((), (), s32[]{:S(2)}) async-start(), calls=%async_computation.36 | async-start | bytes 1474560 | tf_op jit(solution)/shard_map/all_gather | solution.py:145
  803.7 299.7 %all-gather.55.cloned.1.call-start = ((), (), s32[]{:S(2)}) async-start(), calls=%async_computation.35 | async-start | bytes 1474560 | tf_op jit(solution)/shard_map/all_gather | solution.py:146
  804.3 301.5 %all-gather.53.cloned.1.call-start = ((), (), s32[]{:S(2)}) async-start(), calls=%async_computation.34 | async-start | bytes 5898240 | tf_op jit(solution)/shard_map/all_gather | solution.py:147
  885.6 310.6 %all-gather.71.cloned.1.call-start = ((), (), s32[]{:S(2)}) async-start(), calls=%async_computation.51 | async-start | bytes 2162688 | tf_op jit(solution)/shard_map/all_gather | solution.py:53
  886.2 312.7 %all-gather.73.cloned.1.call-start = ((), (), s32[]{:S(2)}) async-start(), calls=%async_computation.52 | async-start | bytes 8650752 | tf_op jit(solution)/shard_map/all_gather | solution.py:54
  886.7 354.3 %all-gather.75.cloned.1.call-start = ((), (), s32[]{:S(2)}) async-start(), calls=%async_computation.53 | async-start | bytes 8650752 | tf_op jit(solution)/shard_map/all_gather | solution.py:55
  887.5 443.5 %all-gather.59.cloned.1.call-start = ((), (), s32[]{:S(2)}) async-start(), calls=%async_computation.37 | async-start | bytes 5898240 | tf_op jit(solution)/shard_map/all_gather | solution.py:147
  1096.4 646.3 %reduce-scatter.83.cloned.1.call-start = ((), (), s32[]{:S(2)}) async-start(), calls=%async_computation.54 | async-start | bytes 1474560
  1485.3 259.9 %reduce-scatter.87.cloned.1.call-start = ((), (), s32[]{:S(2)}) async-start(), calls=%async_computation.56 | async-start | bytes 1474560
  1522.9 224.8 %reduce-scatter.95.cloned.1.call-start = ((), (), s32[]{:S(2)}) async-start(), calls=%async_computation.60 | async-start | bytes 1474560
  1542.1 209.9 %reduce-scatter.99.cloned.1.call-start = ((), (), s32[]{:S(2)}) async-start(), calls=%async_computation.62 | async-start | bytes 1474560
  1583.6 172.9 %reduce-scatter.85.cloned.1.call-start = ((), (), s32[]{:S(2)}) async-start(), calls=%async_computation.55 | async-start | bytes 5898240
  1610.2 176.2 %reduce-scatter.97.cloned.1.call-start = ((), (), s32[]{:S(2)}) async-start(), calls=%async_computation.61 | async-start | bytes 5898240
  1690.9 464.3 %reduce-scatter.101.cloned.1.call-start = ((), (), s32[]{:S(2)}) async-start(), calls=%async_computation.63 | async-start | bytes 1474560
  1847.8 309.9 %reduce-scatter.105.cloned.1.call-start = ((), (), s32[]{:S(2)}) async-start(), calls=%async_computation.65 | async-start | bytes 1474560
  1885.4 274.0 %reduce-scatter.89.cloned.1.call-start = ((), (), s32[]{:S(2)}) async-start(), calls=%async_computation.57 | async-start | bytes 1474560
  1904.9 257.2 %reduce-scatter.93.cloned.1.call-start = ((), (), s32[]{:S(2)}) async-start(), calls=%async_computation.59 | async-start | bytes 1474560
  1946.4 218.1 %reduce-scatter.103.cloned.1.call-start = ((), (), s32[]{:S(2)}) async-start(), calls=%async_computation.64 | async-start | bytes 5898240
  1973.3 192.8 %reduce-scatter.91.cloned.1.call-start = ((), (), s32[]{:S(2)}) async-start(), calls=%async_computation.58 | async-start | bytes 5898240
  2046.8 323.3 %reduce-scatter.113.cloned.1.call-start = ((), (), s32[]{:S(2)}) async-start(), calls=%async_computation.69 | async-start | bytes 540672
  2052.5 368.1 %reduce-scatter.111.cloned.1.call-start = ((), (), s32[]{:S(2)}) async-start(), calls=%async_computation.68 | async-start | bytes 540672
  2057.2 496.3 %reduce-scatter.117.cloned.1.call-start = ((), (), s32[]{:S(2)}) async-start(), calls=%async_computation.71 | async-start | bytes 540672
  2058.6 641.5 %reduce-scatter.69.cloned.1.call-start = ((), (), s32[]{:S(2)}) async-start(), calls=%async_computation.39 | async-start | bytes 4325376 | tf_op jit(solution)/shard_map/reduce_scatter | solution.py:79
  2063.7 785.4 %reduce-scatter.67.cloned.1.call-start = ((), (), s32[]{:S(2)}) async-start(), calls=%async_computation.38 | async-start | bytes 4325376 | tf_op jit(solution)/shard_map/reduce_scatter | solution.py:79
  2110.7 873.4 %reduce-scatter.115.cloned.1.call-start = ((), (), s32[]{:S(2)}) async-start(), calls=%async_computation.70 | async-start | bytes 540672
  2176.0 942.4 %reduce-scatter.81.cloned.1.call-start = ((), (), s32[]{:S(2)}) async-start(), calls=%async_computation.45 | async-start | bytes 1081344 | tf_op jit(solution)/shard_map/reduce_scatter | solution.py:82
  2179.5 1073.0 %reduce-scatter.79.cloned.1.call-start = ((), (), s32[]{:S(2)}) async-start(), calls=%async_computation.44 | async-start | bytes 1081344 | tf_op jit(solution)/shard_map/reduce_scatter | solution.py:82
  2197.4 1213.3 %reduce-scatter.109.cloned.1.call-start = ((), (), s32[]{:S(2)}) async-start(), calls=%async_computation.67 | async-start | bytes 12976128
  2235.9 1336.6 %reduce-scatter.107.cloned.1.call-start = ((), (), s32[]{:S(2)}) async-start(), calls=%async_computation.66 | async-start | bytes 12976128
  2286.3 1651.8 %reduce-scatter.77.cloned.1.call-start = ((), (), s32[]{:S(2)}) async-start(), calls=%async_computation.43 | async-start | bytes 17301504 | tf_op jit(solution)/shard_map/reduce_scatter | solution.py:81
  2312.4 1990.1 %reduce-scatter.75.cloned.1.call-start = ((), (), s32[]{:S(2)}) async-start(), calls=%async_computation.42 | async-start | bytes 17301504 | tf_op jit(solution)/shard_map/reduce_scatter | solution.py:81
  2339.4 2327.5 %reduce-scatter.73.cloned.1.call-start = ((), (), s32[]{:S(2)}) async-start(), calls=%async_computation.41 | async-start | bytes 17301504 | tf_op jit(solution)/shard_map/reduce_scatter | solution.py:80
  2352.3 2678.9 %reduce-scatter.71.cloned.1.call-start = ((), (), s32[]{:S(2)}) async-start(), calls=%async_computation.40 | async-start | bytes 17301504 | tf_op jit(solution)/shard_map/reduce_scatter | solution.py:80
  2366.5 484.2 %copy-start.319 = (f32[144]{0:T(256)S(1)}, f32[144]{0:T(256)}, u32[]{:S(2)}) copy-start(f32[144]{0:T(256)} %copy-done.318) | copy-start | bytes 1732
  2366.5 489.7 %slice-start.8 = ((s8[6291456]{0:T(1024)(128)(4,1)}), s8[2097152]{0:T(1024)(128)(4,1)S(1)}, s32[]{:S(2)}) async-start(s8[6291456]{0:T(1024)(128)(4,1)} %bitcast.1308), calls=%async_computation.80 | async-start | bytes 4194304
  (383 other events, 7548.2 us)
Sparse Core Ops, SparseCore 0:
  11.5 74.2 all-gather.60
  116.0 29.6 all-gather.44
  147.2 32.9 all-gather.42
  182.2 29.1 all-gather.38
  212.8 29.7 all-gather.36
  244.6 97.0 all-gather.46
  343.7 90.5 all-gather.40
  437.2 54.9 all-gather.62
  495.2 76.5 all-gather.64
  574.6 76.0 all-gather.66
  653.5 68.3 all-gather.68
  798.2 31.5 all-gather.50
  831.3 33.2 all-gather.48
  866.1 30.9 all-gather.56
  898.5 33.0 all-gather.54
  933.7 89.7 all-gather.52
  1026.8 55.5 all-gather.70
  1085.2 76.2 all-gather.72
  1164.9 76.0 all-gather.74
  1243.0 87.9 all-gather.58
  1485.5 27.5 reduce-scatter.82
  1523.0 27.6 reduce-scatter.86
  1553.6 27.8 reduce-scatter.94
  1584.2 27.8 reduce-scatter.98
  1614.5 83.9 reduce-scatter.84
  1700.6 85.7 reduce-scatter.96
  1848.0 29.6 reduce-scatter.100
  1885.6 29.6 reduce-scatter.104
  1917.6 27.8 reduce-scatter.88
  1947.7 28.5 reduce-scatter.92
  1978.6 83.9 reduce-scatter.102
  2064.9 85.7 reduce-scatter.90
  2152.8 134.6 reduce-scatter.112
  2289.8 130.7 reduce-scatter.110
  2422.8 130.6 reduce-scatter.116
  2555.8 144.3 reduce-scatter.68
  2702.3 146.6 reduce-scatter.66
  2851.4 132.6 reduce-scatter.114
  2986.2 132.1 reduce-scatter.80
  3120.8 131.6 reduce-scatter.78
  3258.5 152.1 reduce-scatter.108
  3417.8 154.7 reduce-scatter.106
  3574.7 363.3 reduce-scatter.76
  3940.4 362.1 reduce-scatter.74
  4304.7 362.1 reduce-scatter.72
  4669.0 362.1 reduce-scatter.70
where the time goes:
time: 5050 us; the launch traced here: 5040 us
  waiting for transfers between devices  2740 us (54%)
  matrix products  931 us (18%)
  blocking collectives  618 us (12%)
  local copies, waits for them, and re-layouts  455 us (9%)
  other arithmetic  267 us (5%)
    reduce_scatter x2, waiting for transfers between devices, scatter_end(): lax.psum_scatter(grad_terms[3], ('doc', 'ctx'), scatter_dimension=0, tile...  727 us
    reduce_scatter x2, waiting for transfers between devices, scatter_end(): lax.psum_scatter(grad_terms[2], ('doc', 'ctx'), scatter_dimension=0, tile...  726 us
    unnamed x64, waiting for transfers between devices  614 us
    reduce_scatter x2, waiting for transfers between devices, scatter_end(): lax.psum_scatter(grad_terms[1], ('doc', 'ctx'), scatter_dimension=0, tile...  295 us
    reduce_scatter x2, waiting for transfers between devices, scatter_end(): lax.psum_scatter(grad_terms[4], ('doc', 'ctx'), scatter_dimension=2, tile...  267 us
    unnamed x833, local copies, waits for them, and re-layouts  207 us
    dot_general x8, matrix products, layer_forward(): jnp.einsum('njhb,nijb->nhij', key_rel_all[:, :, kind_index], bucket_hots[...  190 us
    all_gather x2, blocking collectives, fetch_forward(): lax.all_gather(shards[5], ('doc', 'ctx'), axis=1, tiled=True)  152 us
  transfers between devices with their start and end apart: 46, of which 16 were waited for; matrix products, arithmetic and copies ran while one was open for 28% of the time, Pallas kernels for 0%

commit v1 on v0

v1 whole, which is shorter than its diff:
```python
import functools

import jax
import jax.numpy as jnp
from jax import lax
from jax.experimental import pallas as pl
from jax.experimental.pallas import tpu as pltpu
from jax.sharding import PartitionSpec as P

HEADS = 16
HEAD_DIM = 64
BUCKETS = 128
TEXT = 512
PATCH = 49
GRID_SIDE = 32
CELLS = GRID_SIDE * GRID_SIDE
LANES = 128
PAIR = 2 * HEAD_DIM
NORM_EPSILON = 1e-05
SCORE_SCALE = (3.0 * HEAD_DIM) ** (-0.5)
MASKED = -1e30
BF16 = jnp.bfloat16
F32 = jnp.float32
BOTH = ("doc", "ctx")


def pad_lanes(count):
    return -(-count // LANES) * LANES


def norm_rows(values_in, scale_gain, offset):
    centered = values_in - jnp.mean(values_in, axis=-1, keepdims=True)
    spread = jnp.mean(centered * centered, axis=-1, keepdims=True)
    return centered * lax.rsqrt(spread + NORM_EPSILON) * scale_gain + offset


def exact_gelu(values_in):
    return jax.nn.gelu(values_in, approximate=False)


def dot(left, right, left_axis, right_axis):
    return lax.dot_general(
        left, right, (((left_axis,), (right_axis,)), ((), ())), preferred_element_type=F32
    )


def lookup(table, index):
    return jnp.take_along_axis(table, index, axis=1, mode="promise_in_bounds")


def head_lanes(head, rows):
    lane = lax.broadcasted_iota(jnp.int32, (rows, PAIR), 1)
    return (lane >= head * HEAD_DIM) & (lane < (head + 1) * HEAD_DIM)


def keep_head(values, head):
    return jnp.where(head_lanes(head, values.shape[0]), values, jnp.zeros_like(values))


def attend_kernel(
    chunks,
    q_ref,
    *refs,
):
    k_refs = refs[:chunks]
    v_refs = refs[chunks : 2 * chunks]
    (
        rel_key_ref,
        rel_query_ref,
        index_linear_ref,
        index_planar_ref,
        turned_linear_ref,
        turned_planar_ref,
        mask_ref,
        mixed_ref,
        prob_ref,
        left_scr,
        right_scr,
        value_scr,
        score_scr,
    ) = refs[2 * chunks :]
    rows = q_ref.shape[0]
    keys = rows * chunks
    keys_wide = score_scr.shape[1]
    rows_wide = left_scr.shape[1] - PAIR

    @pl.when(pl.program_id(0) == 0)
    def _():
        row_at = lax.broadcasted_iota(jnp.int32, (rows, rows_wide), 0)
        lane_at = lax.broadcasted_iota(jnp.int32, (rows, rows_wide), 1)
        left_scr[:, PAIR:] = jnp.where(row_at == lane_at, 1.0, 0.0).astype(BF16)
        right_scr[keys:, :] = jnp.zeros((keys_wide - keys, PAIR + rows_wide), BF16)
        value_scr[keys:, :] = jnp.zeros((keys_wide - keys, PAIR), BF16)

    for chunk in range(chunks):
        right_scr[chunk * rows : (chunk + 1) * rows, :PAIR] = k_refs[chunk][...]
        value_scr[chunk * rows : (chunk + 1) * rows, :] = v_refs[chunk][...]

    for head in range(2):
        left_scr[:, :PAIR] = keep_head(q_ref[...], head)
        rel_query = [keep_head(rel_query_ref[kind], head) for kind in range(2)]
        rel_key = [keep_head(rel_key_ref[kind], head) for kind in range(2)]

        key_step = 48

        def key_block(block, carry):
            at = pl.multiple_of(block * key_step, key_step)
            key_rows = right_scr[pl.ds(at, key_step), :PAIR]
            first = dot(key_rows, rel_query[0], 1, 1).astype(BF16).astype(F32)
            second = dot(key_rows, rel_query[1], 1, 1).astype(BF16).astype(F32)
            biased = lookup(first, turned_linear_ref[pl.ds(at, key_step), :]) + lookup(
                second, turned_planar_ref[pl.ds(at, key_step), :]
            )
            right_scr[pl.ds(at, key_step), PAIR:] = biased.astype(BF16)
            return carry

        lax.fori_loop(0, keys // key_step, key_block, 0)
        score_scr[...] = dot(left_scr[...], right_scr[...], 1, 1)

        row_step = 48

        def row_block(block, carry):
            at = pl.multiple_of(block * row_step, row_step)
            query_rows = left_scr[pl.ds(at, row_step), :PAIR]
            first = dot(query_rows, rel_key[0], 1, 1).astype(BF16).astype(F32)
            second = dot(query_rows, rel_key[1], 1, 1).astype(BF16).astype(F32)
            raw = score_scr[pl.ds(at, row_step), :]
            raw = raw + lookup(first, index_linear_ref[pl.ds(at, row_step), :])
            raw = raw + lookup(second, index_planar_ref[pl.ds(at, row_step), :])
            scaled = raw * SCORE_SCALE + mask_ref[...]
            shifted = scaled - jnp.max(scaled, axis=-1, keepdims=True)
            exponent = jnp.exp(shifted)
            inverse = 1.0 / jnp.sum(exponent, axis=-1, keepdims=True)
            prob_ref[head, pl.ds(at, row_step), :] = (exponent * inverse).astype(BF16)
            return carry

        lax.fori_loop(0, rows // row_step, row_block, 0)
        mixed = dot(prob_ref[head], value_scr[...], 1, 0)
        if head == 0:
            mixed_ref[...] = mixed.astype(BF16)
        else:
            mixed_ref[...] = jnp.where(head_lanes(1, rows), mixed, mixed_ref[...].astype(F32)).astype(BF16)


def whole_spec(array):
    return pl.BlockSpec(array.shape, lambda step: (0,) * array.ndim)


def attend(qkv, other_kv, rel_key, rel_query, lookups):
    rows = qkv.shape[0]
    width = qkv.shape[1] // 3
    pairs = width // PAIR
    chunks = 1 + len(other_kv)
    keys_wide = pad_lanes(rows * chunks)
    rows_wide = pad_lanes(rows)

    def column(offset):
        return pl.BlockSpec((rows, PAIR), lambda step: (0, offset + step))

    rel_spec = pl.BlockSpec((2, BUCKETS, PAIR), lambda step: (0, 0, step))
    small = (
        lookups["index_linear"],
        lookups["index_planar"],
        lookups["turned_linear"],
        lookups["turned_planar"],
        lookups["mask"],
    )
    return pl.pallas_call(
        functools.partial(attend_kernel, chunks),
        grid=(pairs,),
        in_specs=[column(0), column(pairs)]
        + [column(0)] * (chunks - 1)
        + [column(2 * pairs)]
        + [column(pairs)] * (chunks - 1)
        + [rel_spec, rel_spec]
        + [whole_spec(item) for item in small],
        out_specs=[
            pl.BlockSpec((rows, PAIR), lambda step: (0, step)),
            pl.BlockSpec((2, rows, keys_wide), lambda step: (step, 0, 0)),
        ],
        out_shape=[
            jax.ShapeDtypeStruct((rows, width), BF16),
            jax.ShapeDtypeStruct((2 * pairs, rows, keys_wide), BF16),
        ],
        scratch_shapes=[
            pltpu.VMEM((rows, PAIR + rows_wide), BF16),
            pltpu.VMEM((keys_wide, PAIR + rows_wide), BF16),
            pltpu.VMEM((keys_wide, PAIR), BF16),
            pltpu.VMEM((rows, keys_wide), F32),
        ],
        compiler_params=pltpu.CompilerParams(vmem_limit_bytes=40 << 20),
        cost_estimate=pl.CostEstimate(
            flops=20 * rows * rows * chunks * width,
            bytes_accessed=4 * pairs * rows * keys_wide + 8 * rows * width,
            transcendentals=2 * pairs * rows * keys_wide,
        ),
        name="attend",
    )(qkv, qkv, *other_kv, qkv, *other_kv, rel_key, rel_query, *small)


def bucket_sums(cells, pos, sums_out):
    spot = pos & (LANES - 1)
    part = pos >> 7
    total = jnp.zeros(spot.shape, F32)
    for chunk in range(CELLS // LANES):
        total = jnp.where(
            part == chunk, lookup(cells[:, chunk * LANES : (chunk + 1) * LANES], spot), total
        )
    lane = lax.broadcasted_iota(jnp.int32, total.shape, 1)
    total = total - jnp.where(lane < BUCKETS - 8, pltpu.roll(total, BUCKETS - 8, 1), 0.0)
    return total - jnp.where((lane & 7) < 7, pltpu.roll(total, BUCKETS - 1, 1), 0.0)


def band_sums(values, index, pos):
    spot = pos & (LANES - 1)
    part = pos >> 7
    total = jnp.zeros(spot.shape, F32)
    for chunk in range(values.shape[1] // LANES):
        total = jnp.where(
            part == chunk, lookup(values[:, chunk * LANES : (chunk + 1) * LANES], spot), total
        )
    low = jnp.sum(jnp.where(index == 0, values, 0.0), axis=-1, keepdims=True)
    high = jnp.sum(jnp.where(index == BUCKETS - 1, values, 0.0), axis=-1, keepdims=True)
    lane = lax.broadcasted_iota(jnp.int32, total.shape, 1)
    return jnp.where(lane == 0, low, jnp.where(lane == BUCKETS - 1, high, total))


def attend_back_kernel(
    chunks,
    q_ref,
    *refs,
):
    k_refs = refs[:chunks]
    v_refs = refs[chunks : 2 * chunks]
    (
        grad_ref,
        prob_ref,
        rel_key_ref,
        rel_query_ref,
        index_linear_ref,
        turned_linear_ref,
        key_cells_ref,
        row_cells_ref,
        planar_pos_ref,
        linear_pos_ref,
        turned_planar_pos_ref,
        turned_linear_pos_ref,
        grad_query_ref,
        grad_key_ref,
        grad_value_ref,
        grad_rel_key_ref,
        grad_rel_query_ref,
        key_scr,
        value_scr,
        raw_scr,
        low_scr,
        turned_scr,
        cell_scr,
        row_bucket_scr,
        key_bucket_scr,
    ) = refs[2 * chunks :]
    rows = q_ref.shape[0]
    keys = rows * chunks
    keys_wide = key_scr.shape[0]
    rows_wide = raw_scr.shape[0]

    @pl.when(pl.program_id(0) == 0)
    def _():
        key_scr[keys:, :] = jnp.zeros((keys_wide - keys, PAIR), BF16)
        value_scr[keys:, :] = jnp.zeros((keys_wide - keys, PAIR), BF16)
        raw_scr[rows:, :] = jnp.zeros((rows_wide - rows, keys_wide), F32)

    for chunk in range(chunks):
        key_scr[chunk * rows : (chunk + 1) * rows, :] = k_refs[chunk][...]
        value_scr[chunk * rows : (chunk + 1) * rows, :] = v_refs[chunk][...]

    for head in range(2):
        query = keep_head(q_ref[...], head)
        grad = keep_head(grad_ref[...], head)
        raw_scr[:rows, :] = dot(grad, value_scr[...], 1, 1)
        row_step = 48

        def row_block(block, carry):
            at = pl.multiple_of(block * row_step, row_step)
            prob = prob_ref[head, pl.ds(at, row_step), :].astype(F32)
            grad_prob = raw_scr[pl.ds(at, row_step), :]
            inner = jnp.sum(prob * grad_prob, axis=-1, keepdims=True)
            grad_raw = (prob * (grad_prob - inner) * SCORE_SCALE).astype(BF16)
            low_scr[pl.ds(at, row_step), :] = grad_raw
            raw_scr[pl.ds(at, row_step), :] = grad_raw.astype(F32)
            return carry

        lax.fori_loop(0, rows // row_step, row_block, 0)

        cell_scr[:rows, :] = dot(low_scr[...], key_cells_ref[...], 1, 0)
        step = 16

        def query_block(block, carry):
            at = pl.multiple_of(block * step, step)
            planar = bucket_sums(
                cell_scr[pl.ds(at, step), :], planar_pos_ref[pl.ds(at, step), :], None
            )
            linear = band_sums(
                raw_scr[pl.ds(at, step), :],
                index_linear_ref[pl.ds(at, step), :],
                linear_pos_ref[pl.ds(at, step), :],
            )
            row_bucket_scr[pl.ds(at, step), :BUCKETS] = linear.astype(BF16)
            row_bucket_scr[pl.ds(at, step), BUCKETS:] = planar.astype(BF16)
            return carry

        lax.fori_loop(0, rows // step, query_block, 0)
        row_bucket = row_bucket_scr[...]
        rel_key = keep_head(rel_key_ref[...].reshape(2 * BUCKETS, PAIR), head)
        rel_query = keep_head(rel_query_ref[...].reshape(2 * BUCKETS, PAIR), head)
        grad_query = dot(low_scr[...], key_scr[...], 1, 0) + dot(row_bucket, rel_key, 1, 0)
        grad_rel_key = dot(row_bucket, query, 0, 0)

        turned_scr[...] = raw_scr[...].T[:keys]
        turned_low = turned_scr[...].astype(BF16)
        cell_scr[...] = dot(turned_low, row_cells_ref[...], 1, 0)

        def key_block(block, carry):
            at = pl.multiple_of(block * step, step)
            planar = bucket_sums(
                cell_scr[pl.ds(at, step), :], turned_planar_pos_ref[pl.ds(at, step), :], None
            )
            linear = band_sums(
                turned_scr[pl.ds(at, step), :],
                turned_linear_ref[pl.ds(at, step), :],
                turned_linear_pos_ref[pl.ds(at, step), :],
            )
            key_bucket_scr[pl.ds(at, step), :BUCKETS] = linear.astype(BF16)
            key_bucket_scr[pl.ds(at, step), BUCKETS:] = planar.astype(BF16)
            return carry

        lax.fori_loop(0, keys // step, key_block, 0)
        key_bucket = key_bucket_scr[...]
        grad_key = dot(turned_low[:, :rows], query, 1, 0) + dot(key_bucket, rel_query, 1, 0)
        grad_value = dot(prob_ref[head], grad, 0, 0)[:keys]
        grad_rel_query = dot(key_bucket, key_scr[:keys, :], 0, 0)
        results = (
            (grad_query_ref, grad_query),
            (grad_key_ref, grad_key),
            (grad_value_ref, grad_value),
            (grad_rel_key_ref, grad_rel_key.reshape(2, BUCKETS, PAIR)),
            (grad_rel_query_ref, grad_rel_query.reshape(2, BUCKETS, PAIR)),
        )
        for target, found in results:
            if head == 0:
                target[...] = found
            else:
                lane = lax.broadcasted_iota(jnp.int32, found.shape, found.ndim - 1)
                target[...] = jnp.where(lane >= HEAD_DIM, found, target[...])


def attend_back(qkv, other_kv, grad_mixed, prob, rel_key, rel_query, lookups):
    rows = qkv.shape[0]
    width = qkv.shape[1] // 3
    pairs = width // PAIR
    chunks = 1 + len(other_kv)
    keys = rows * chunks
    keys_wide = pad_lanes(keys)
    rows_wide = pad_lanes(rows)

    def column(offset):
        return pl.BlockSpec((rows, PAIR), lambda step: (0, offset + step))

    rel_spec = pl.BlockSpec((2, BUCKETS, PAIR), lambda step: (0, 0, step))
    key_spec = pl.BlockSpec((keys, PAIR), lambda step: (0, step))
    small = (
        lookups["index_linear"],
        lookups["turned_linear"],
        lookups["key_cells"],
        lookups["row_cells"],
        lookups["planar_pos"],
        lookups["linear_pos"],
        lookups["turned_planar_pos"],
        lookups["turned_linear_pos"],
    )
    return pl.pallas_call(
        functools.partial(attend_back_kernel, chunks),
        grid=(pairs,),
        in_specs=[column(0), column(pairs)]
        + [column(0)] * (chunks - 1)
        + [column(2 * pairs)]
        + [column(pairs)] * (chunks - 1)
        + [
            column(0),
            pl.BlockSpec((2, rows, keys_wide), lambda step: (step, 0, 0)),
            rel_spec,
            rel_spec,
        ]
        + [whole_spec(item) for item in small],
        out_specs=[column(0), key_spec, key_spec, rel_spec, rel_spec],
        out_shape=[
            jax.ShapeDtypeStruct((rows, width), F32),
            jax.ShapeDtypeStruct((keys, width), F32),
            jax.ShapeDtypeStruct((keys, width), F32),
            jax.ShapeDtypeStruct((2, BUCKETS, width), F32),
            jax.ShapeDtypeStruct((2, BUCKETS, width), F32),
        ],
        scratch_shapes=[
            pltpu.VMEM((keys_wide, PAIR), BF16),
            pltpu.VMEM((keys_wide, PAIR), BF16),
            pltpu.VMEM((rows_wide, keys_wide), F32),
            pltpu.VMEM((rows, keys_wide), BF16),
            pltpu.VMEM((keys, rows_wide), F32),
            pltpu.VMEM((keys, CELLS), F32),
            pltpu.VMEM((rows, 2 * BUCKETS), BF16),
            pltpu.VMEM((keys, 2 * BUCKETS), BF16),
        ],
        compiler_params=pltpu.CompilerParams(vmem_limit_bytes=56 << 20),
        cost_estimate=pl.CostEstimate(
            flops=80 * rows * rows * chunks * width,
            bytes_accessed=4 * pairs * rows * keys_wide + 24 * rows * width,
            transcendentals=0,
        ),
        name="attend_back",
    )(qkv, qkv, *other_kv, qkv, *other_kv, grad_mixed, prob, rel_key, rel_query, *small)


def make_lookups(cells_x, cells_y, count, place, row_count):
    seq_len = place.shape[0]
    keys_wide = pad_lanes(seq_len)
    rows_wide = pad_lanes(row_count)
    half_range = BUCKETS // 2

    def wide(values, total):
        return jnp.pad(values, ((0, total - values.shape[0]),))

    key_place, key_x, key_y = (wide(item, keys_wide) for item in (place, cells_x, cells_y))
    row_place, row_x, row_y = (item[:row_count] for item in (place, cells_x, cells_y))
    wide_place, wide_x, wide_y = (wide(item, rows_wide) for item in (row_place, row_x, row_y))

    def linear(i, j):
        return jnp.clip(i - j, -half_range, half_range - 1) + half_range

    def planar(ix, iy, jx, jy):
        return (jnp.clip(ix - jx, -8, 7) + 8) * 8 + jnp.clip(iy - jy, -4, 3) + 4

    out = {}
    out["index_linear"] = linear(row_place[:, None], key_place[None, :])
    out["index_planar"] = planar(row_x[:, None], row_y[:, None], key_x[None, :], key_y[None, :])
    out["turned_linear"] = linear(wide_place[None, :], place[:, None])
    out["turned_planar"] = planar(
        wide_x[None, :], wide_y[None, :], cells_x[:, None], cells_y[:, None]
    )
    valid = (place < count) | ((place >= TEXT) & (place < TEXT + PATCH))
    out["mask"] = jnp.pad(
        jnp.where(valid, 0.0, MASKED).astype(F32),
        ((0, keys_wide - seq_len),),
        constant_values=MASKED,
    )[None]
    key_live = jnp.arange(keys_wide) < seq_len
    row_live = jnp.arange(rows_wide) < row_count
    cell = jnp.arange(CELLS, dtype=jnp.int32)
    cell_x, cell_y = cell // GRID_SIDE, cell % GRID_SIDE
    out["key_cells"] = (
        key_live[:, None] & (key_x[:, None] <= cell_x) & (key_y[:, None] <= cell_y)
    ).astype(BF16)
    out["row_cells"] = (
        row_live[:, None] & (wide_x[:, None] >= cell_x) & (wide_y[:, None] >= cell_y)
    ).astype(BF16)
    bucket = jnp.arange(BUCKETS, dtype=jnp.int32)
    bucket_x, bucket_y = bucket // 8, bucket % 8
    top = GRID_SIDE - 1
    to_x = jnp.where(bucket_x == 0, top, jnp.minimum(row_x[:, None] - bucket_x + 8, top))
    to_y = jnp.where(bucket_y == 0, top, jnp.minimum(row_y[:, None] - bucket_y + 4, top))
    out["planar_pos"] = jnp.where((to_x >= 0) & (to_y >= 0), to_x * GRID_SIDE + to_y, -1)
    from_x = jnp.where(bucket_x == 0, 0, jnp.maximum(cells_x[:, None] + bucket_x - 8, 0))
    from_y = jnp.where(bucket_y == 0, 0, jnp.maximum(cells_y[:, None] + bucket_y - 4, 0))
    out["turned_planar_pos"] = jnp.where(
        (from_x <= top) & (from_y <= top), from_x * GRID_SIDE + from_y, -1
    )
    first_place = place[0]
    target = row_place[:, None] - bucket + half_range
    out["linear_pos"] = jnp.where(
        (target >= 0) & (target < seq_len), (target - first_place) % seq_len, -1
    )
    source = place[:, None] + bucket - half_range - first_place
    out["turned_linear_pos"] = jnp.where((source >= 0) & (source < row_count), source, -1)
    return out


class Home:
    def __init__(self, mesh_shape, local_docs, block_rows):
        self.doc_size = mesh_shape["doc"]
        self.ctx_size = mesh_shape["ctx"]
        self.block = block_rows
        self.docs = 2 * local_docs
        self.span = self.ctx_size // self.docs
        self.group = 2 * self.span
        self.rows = 2 * block_rows
        self.seq = block_rows * self.ctx_size

    def flat(self, doc, ctx):
        return doc * self.ctx_size + ctx

    def move_pairs(self, turn):
        pairs = []
        for pair in range(self.doc_size // 2):
            for core in range(2):
                for block in range(self.ctx_size):
                    slot = (block + turn) % 2
                    doc = 2 * core + slot
                    place = block // 2
                    target = self.flat(
                        2 * pair + place // self.span, doc * self.span + place % self.span
                    )
                    pairs.append((self.flat(2 * pair + core, block), target))
        return pairs

    def to_home(self, local):
        ctx = lax.axis_index("ctx")
        doc_here = ctx // self.span
        pieces = []
        for turn in range(2):
            piece = lax.dynamic_index_in_dim(local, (ctx + turn) % 2, 0, keepdims=False)
            pieces.append(lax.ppermute(piece, BOTH, self.move_pairs(turn)))
        swap = (doc_here % 2) == 1
        low_half = jnp.where(swap, pieces[1], pieces[0])
        high_half = jnp.where(swap, pieces[0], pieces[1])
        return jnp.concatenate([low_half, high_half], axis=0)

    def from_home(self, rows):
        ctx = lax.axis_index("ctx")
        doc_here = ctx // self.span
        halves = rows.reshape(2, self.block, rows.shape[1])
        pieces = []
        for turn in range(2):
            piece = lax.dynamic_index_in_dim(halves, (doc_here + turn) % 2, 0, keepdims=False)
            back = [(target, source) for source, target in self.move_pairs(turn)]
            pieces.append(lax.ppermute(piece, BOTH, back))
        swap = (ctx % 2) == 1
        first = jnp.where(swap, pieces[1], pieces[0])
        second = jnp.where(swap, pieces[0], pieces[1])
        return jnp.stack([first, second])

    def position(self):
        core = lax.axis_index("doc") % 2
        return core * self.span + lax.axis_index("ctx") % self.span

    def ring_pairs(self, shift):
        pairs = []
        for doc in range(self.doc_size):
            for ctx in range(self.ctx_size):
                place = (doc % 2) * self.span + ctx % self.span
                other = (place + shift) % self.group
                pairs.append(
                    (
                        self.flat(doc, ctx),
                        self.flat(
                            doc - doc % 2 + other // self.span,
                            ctx - ctx % self.span + other % self.span,
                        ),
                    )
                )
        return pairs

    def fetch(self, values):
        return [
            lax.ppermute(values, BOTH, self.ring_pairs(-shift)) for shift in range(1, self.group)
        ]

    def give_back(self, pieces):
        return [
            lax.ppermute(piece, BOTH, self.ring_pairs(shift))
            for shift, piece in enumerate(pieces, 1)
        ]


def pack_layer(w_qkv, w_out, w_in, w_down, tables, gains, biases, b_in):
    shard = w_qkv.shape[0]
    down = w_down.reshape(-1, shard, w_down.shape[1])
    down = jnp.concatenate([down[part] for part in range(down.shape[0])], axis=1)
    small = jnp.concatenate(
        [tables.reshape(-1, shard).T, gains.T, biases.T, b_in.reshape(shard, -1)], axis=1
    )
    small = jnp.pad(small, ((0, 0), (0, pad_lanes(small.shape[1]) - small.shape[1])))
    return jnp.concatenate([w_qkv, w_out, w_in, down, small], axis=1)


def unpack_layer(packed, device_count):
    width = packed.shape[0]
    shard = width // device_count
    qkv = packed[:, : 3 * width]
    out = packed[:, 3 * width : 4 * width]
    rest = packed.shape[1] - 4 * width
    hidden = (rest // (2 * width)) * width
    w_in = packed[:, 4 * width : 4 * width + hidden]
    down = packed[:, 4 * width + hidden : 4 * width + 2 * hidden]
    down = (
        down.reshape(device_count, shard, hidden // width, width)
        .transpose(0, 2, 1, 3)
        .reshape(hidden, width)
    )
    small = packed[:, 4 * width + 2 * hidden :]
    table_cols = 2 * BUCKETS
    tables = small[:, :table_cols]
    gains = small[:, table_cols : table_cols + 2].T.astype(F32)
    biases = small[:, table_cols + 2 : table_cols + 9].T.astype(F32)
    b_in = small[:, table_cols + 9 : table_cols + 9 + hidden // width].astype(F32).reshape(hidden)
    return dict(
        qkv=qkv, out=out, w_in=w_in, down=down, tables=tables, gains=gains, biases=biases, b_in=b_in
    )


def doc_flip(doc_size, bit):
    return [(index, index ^ bit) for index in range(doc_size)]


def halve(values, axis, mine, send):
    kept = lax.dynamic_index_in_dim(values, mine, axis, keepdims=False)
    sent = lax.dynamic_index_in_dim(values, 1 - mine, axis, keepdims=False)
    return kept, send(sent.astype(BF16))


def scatter_sum(parts, doc_size, ctx_size):
    doc = lax.axis_index("doc")
    ctx = lax.axis_index("ctx")

    def doc_step(values, axis, bit):
        def send(half):
            return lax.ppermute(half, "doc", doc_flip(doc_size, bit))

        kept, got = halve(values, axis, (doc // bit) % 2, send)
        return (kept.astype(F32) + got.astype(F32)).astype(BF16)

    def ctx_step(values, axis, bit):
        def send(half):
            return lax.ppermute(half, "ctx", doc_flip(ctx_size, bit))

        kept, got = halve(values, axis, (ctx // bit) % 2, send)
        return kept.astype(F32) + got.astype(F32)

    high_bits = []
    bit = 2
    while bit < doc_size:
        high_bits.append(bit)
        bit *= 2
    results = []
    for part in parts:
        rows, columns = part.shape
        block = rows // (doc_size * ctx_size)
        values = part.reshape(doc_size // 2, 2, ctx_size * block, columns)
        values = doc_step(values, 1, 1)
        colored = []
        half_columns = columns // 2
        for color in range(2):
            piece = values[:, :, color * half_columns : (color + 1) * half_columns]
            order = list(reversed(high_bits)) if color == 0 else list(high_bits)
            left = sorted(high_bits, reverse=True)
            piece = piece.reshape((2,) * len(high_bits) + piece.shape[1:])
            for bit in order:
                axis = left.index(bit)
                piece = doc_step(piece, axis, bit)
                left.remove(bit)
            colored.append(piece)
        values = jnp.concatenate(colored, axis=1).reshape(ctx_size, block, columns)
        size = ctx_size
        while size > 1:
            values = values.reshape(2, size // 2, block, columns)
            values = ctx_step(values, 0, size // 2)
            size //= 2
        results.append(values.reshape(block, columns).astype(F32))
    return results


def layer_forward(home, rows_in, rows_low, weights, lookups):
    width = rows_in.shape[1]
    gains, biases = weights["gains"], weights["biases"]
    qkv = (dot(rows_low, weights["qkv"], 1, 0) + biases[:3].reshape(1, -1)).astype(BF16)
    other_kv = home.fetch(qkv[:, width:])
    tables = weights["tables"]
    rel_both = dot(tables, weights["qkv"][:, : 2 * width], 0, 0).astype(BF16)
    rel_query = rel_both[:, :width].reshape(2, BUCKETS, width)
    rel_key = rel_both[:, width:].reshape(2, BUCKETS, width)
    mixed, prob = attend(qkv, other_kv, rel_key, rel_query, lookups)
    first_sum = rows_in + (dot(mixed, weights["out"], 1, 0) + biases[3])
    first_norm = norm_rows(first_sum, gains[0], biases[5])
    norm_low = first_norm.astype(BF16)
    hidden_pre = dot(norm_low, weights["w_in"], 1, 0) + weights["b_in"]
    active = exact_gelu(hidden_pre).astype(BF16)
    second_sum = first_norm + (dot(active, weights["down"], 1, 0) + biases[4])
    result = norm_rows(second_sum, gains[1], biases[6])
    kept = dict(
        rows_low=rows_low,
        qkv=qkv,
        other_kv=other_kv,
        rel_key=rel_key,
        rel_query=rel_query,
        prob=prob,
        mixed=mixed,
        first_sum=first_sum,
        norm_low=norm_low,
        hidden_pre=hidden_pre,
        active=active,
        second_sum=second_sum,
    )
    return result, kept


def layer_backward(home, grad_out, kept, weights, lookups):
    width = grad_out.shape[1]
    gains, biases = weights["gains"], weights["biases"]
    _, second_pull = jax.vjp(norm_rows, kept["second_sum"], gains[1], biases[6])
    grad_second, grad_gain_two, grad_offset_two = second_pull(grad_out)
    grad_down = grad_second.astype(BF16)
    grad_w_down = dot(kept["active"], grad_down, 0, 0)
    grad_b_down = jnp.sum(grad_down.astype(F32), axis=0)
    grad_active = dot(grad_down, weights["down"], 1, 1)
    _, gelu_pull = jax.vjp(exact_gelu, kept["hidden_pre"])
    grad_hidden = gelu_pull(grad_active)[0].astype(BF16)
    grad_w_in = dot(kept["norm_low"], grad_hidden, 0, 0)
    grad_b_in = jnp.sum(grad_hidden.astype(F32), axis=0)
    grad_first_norm = grad_second + dot(grad_hidden, weights["w_in"], 1, 1)
    _, first_pull = jax.vjp(norm_rows, kept["first_sum"], gains[0], biases[5])
    grad_first, grad_gain_one, grad_offset_one = first_pull(grad_first_norm)
    grad_att = grad_first.astype(BF16)
    grad_w_out = dot(kept["mixed"], grad_att, 0, 0)
    grad_b_out = jnp.sum(grad_att.astype(F32), axis=0)
    grad_mixed = dot(grad_att, weights["out"], 1, 1).astype(BF16)
    grad_query, grad_key, grad_value, grad_rel_key, grad_rel_query = attend_back(
        kept["qkv"],
        kept["other_kv"],
        grad_mixed,
        kept["prob"],
        kept["rel_key"],
        kept["rel_query"],
        lookups,
    )
    rows = grad_out.shape[0]
    grad_kv = jnp.concatenate([grad_key, grad_value], axis=1)
    sent = [
        grad_kv[chunk * rows : (chunk + 1) * rows].astype(BF16)
        for chunk in range(1, grad_kv.shape[0] // rows)
    ]
    grad_own = grad_kv[:rows]
    for piece in home.give_back(sent):
        grad_own = grad_own + piece.astype(F32)
    grad_qkv = jnp.concatenate([grad_query, grad_own], axis=1).astype(BF16)
    tables = weights["tables"]
    rel_both = jnp.concatenate(
        [
            grad_rel_query.reshape(2 * BUCKETS, width),
            grad_rel_key.reshape(2 * BUCKETS, width),
        ],
        axis=1,
    ).astype(BF16)
    grad_tables = dot(weights["qkv"][:, :width], rel_both[:, :width], 1, 1) + dot(
        weights["qkv"][:, width : 2 * width], rel_both[:, width:], 1, 1
    )
    grad_w_qk = dot(kept["rows_low"], grad_qkv[:, : 2 * width], 0, 0) + dot(tables, rel_both, 1, 0)
    grad_w_v = dot(kept["rows_low"], grad_qkv[:, 2 * width :], 0, 0)
    grad_w_qkv = jnp.concatenate([grad_w_qk, grad_w_v], axis=1)
    bias_sums = jnp.sum(grad_qkv.astype(F32), axis=0).reshape(3, width)
    grad_rows = grad_first + dot(grad_qkv, weights["qkv"], 1, 1)
    small = jnp.concatenate(
        [
            grad_tables,
            grad_gain_one[:, None],
            grad_gain_two[:, None],
            bias_sums.T,
            grad_b_out[:, None],
            grad_b_down[:, None],
            grad_offset_one[:, None],
            grad_offset_two[:, None],
            grad_b_in.reshape(width, -1),
        ],
        axis=1,
    )
    small = jnp.pad(small, ((0, 0), (0, 2 * LANES * (-(-small.shape[1] // (2 * LANES))) - small.shape[1])))
    return grad_rows, (grad_w_down, grad_w_in, grad_w_out, grad_w_qkv, small)


def unpack_small(small, shard, hidden_shard):
    tables = small[:, : 2 * BUCKETS].T.reshape(2, BUCKETS, shard)
    gains = small[:, 2 * BUCKETS : 2 * BUCKETS + 2].T
    biases = small[:, 2 * BUCKETS + 2 : 2 * BUCKETS + 9].T
    b_in = small[:, 2 * BUCKETS + 9 : 2 * BUCKETS + 9 + hidden_shard // shard].reshape(hidden_shard)
    return tables, gains, biases, b_in


def body(
    mesh_shape,
    layer_input,
    text_count,
    coords,
    w_qkv,
    w_out,
    w_in,
    w_down,
    rel_tables,
    ln_gains,
    biases,
    b_in,
    cotangent,
):
    doc_size, ctx_size = mesh_shape["doc"], mesh_shape["ctx"]
    device_count = doc_size * ctx_size
    local_docs, block_rows, width = layer_input.shape
    layer_count = w_qkv.shape[0]
    home = Home(mesh_shape, local_docs, block_rows)

    packed = [
        pack_layer(
            w_qkv[layer],
            w_out[layer],
            w_in[layer],
            w_down[layer],
            rel_tables[layer],
            ln_gains[layer],
            biases[layer],
            b_in[layer],
        )
        for layer in range(layer_count)
    ]

    core = lax.axis_index("doc") % 2
    doc_here = lax.axis_index("ctx") // home.span
    swap = doc_flip(doc_size, 1)
    facts = jnp.concatenate(
        [coords.reshape(local_docs, -1), text_count[:, None]], axis=1
    )
    other_facts = lax.ppermute(facts, "doc", swap)
    mine = jnp.where(
        doc_here // local_docs == core,
        lax.dynamic_index_in_dim(facts, doc_here % local_docs, 0, keepdims=False),
        lax.dynamic_index_in_dim(other_facts, doc_here % local_docs, 0, keepdims=False),
    )
    place = (jnp.arange(home.seq, dtype=jnp.int32) + home.position() * home.rows) % home.seq

    def turned(values):
        twice = jnp.concatenate([values, values])
        return lax.dynamic_slice_in_dim(twice, home.position() * home.rows, home.seq)

    lookups = make_lookups(
        turned(mine[: home.seq]),
        turned(mine[home.seq : 2 * home.seq]),
        mine[2 * home.seq],
        place,
        home.rows,
    )

    rows_low = home.to_home(layer_input)
    current = rows_low.astype(F32)
    all_weights = []
    kept_all = []
    outputs = []
    gathered = None
    for layer in range(layer_count):
        shard = packed[layer]
        if gathered is not None:
            shard, gathered = lax.optimization_barrier((shard, gathered))
            all_weights[-1] = unpack_layer(gathered, device_count)
        gathered = lax.all_gather(shard, BOTH, axis=0, tiled=True)
        all_weights.append(unpack_layer(gathered, device_count))
    for layer in range(layer_count):
        current, kept = layer_forward(home, current, rows_low, all_weights[layer], lookups)
        rows_low = current.astype(BF16)
        outputs.append(home.from_home(rows_low).astype(F32))
        kept_all.append(kept)
    grad_rows = home.to_home(cotangent).astype(F32)
    totals = [None] * layer_count
    for layer in reversed(range(layer_count)):
        grad_rows, parts = layer_backward(
            home, grad_rows, kept_all[layer], all_weights[layer], lookups
        )
        totals[layer] = scatter_sum(parts, doc_size, ctx_size)
    grad_input = home.from_home(grad_rows.astype(BF16)).astype(F32)
    shard_rows = w_qkv.shape[1]
    smalls = [unpack_small(totals[layer][4], shard_rows, b_in.shape[1]) for layer in range(layer_count)]

    def stack(member):
        return jnp.stack([totals[layer][member] for layer in range(layer_count)])

    def stack_small(member):
        return jnp.stack([smalls[layer][member] for layer in range(layer_count)])

    return (
        outputs[0],
        outputs[-1],
        grad_input,
        stack(3),
        stack(2),
        stack(1),
        stack(0),
        stack_small(0),
        stack_small(1),
        stack_small(2),
        stack_small(3),
    )


def solution(mesh):
    placed = (
        P("doc", "ctx", None),
        P("doc"),
        P("doc", None, None),
        P(None, BOTH, None),
        P(None, BOTH, None),
        P(None, BOTH, None),
        P(None, BOTH, None),
        P(None, None, None, BOTH),
        P(None, None, BOTH),
        P(None, None, BOTH),
        P(None, BOTH),
        P("doc", "ctx", None),
    )
    return jax.shard_map(
        functools.partial(body, dict(mesh.shape)),
        mesh=mesh,
        in_specs=placed,
        out_specs=(
            P("doc", "ctx", None),
            P("doc", "ctx", None),
            P("doc", "ctx", None),
            P(None, BOTH, None),
            P(None, BOTH, None),
            P(None, BOTH, None),
            P(None, BOTH, None),
            P(None, None, None, BOTH),
            P(None, None, BOTH),
            P(None, None, BOTH),
            P(None, BOTH),
        ),
        check_vma=False,
    )
```

time: 5050 us -> 1840 us (0.36)
  waiting for transfers between devices: 2740 us -> 441 us
  Pallas kernels: 0 us -> 771 us
  matrix products: 931 us -> 186 us
  blocking collectives: 618 us -> 0 us
  local copies, waits for them, and re-layouts: 455 us -> 199 us
  other arithmetic: 267 us -> 102 us
  starting transfers between devices: 2.99 us -> 119 us
    reduce_scatter x8 -> x0, waiting for transfers between devices: 2020 us -> none  [the longest x2 727 us: scatter_end(): lax.psum_scatter(grad_terms[3], ('doc', 'ctx'), scatter_dimension=0, tile...]
    pallas_call x0 -> x4, Pallas kernels: none -> 771 us  [the longest x2 515 us: attend_back(): pl.pallas_call(functools.partial(attend_back_kernel, chunks), grid=(pairs...]
    dot_general x148 -> x34, matrix products: 931 us -> 186 us  [dot(): lax.dot_general(left, right, (((left_axis,), (right_axis,)), ((), ())), p...]
    unnamed x64 -> x2, waiting for transfers between devices: 614 us -> 0.03 us
    all_gather x8 -> x0, blocking collectives: 577 us -> none  [the longest x2 152 us: fetch_forward(): lax.all_gather(shards[5], ('doc', 'ctx'), axis=1, tiled=True)]
    ppermute x0 -> x85, waiting for transfers between devices: none -> 280 us  [the longest x50 155 us: send(): return lax.ppermute(half, 'doc', doc_flip(doc_size, bit))]
    unnamed x833 -> x282, local copies, waits for them, and re-layouts: 207 us -> 34.9 us
    dot_general x8 -> x0, other arithmetic: 147 us -> none  [layer_backward(): jnp.einsum('nhij,nijb->njhb', grad_raw_low, bucket_hots[kind_index], pref...]
  transfers between devices with their start and end apart: 46 -> 87, of which waited for: 16 -> 44; matrix products, arithmetic and copies ran while one was open for 28% -> 21% of each run, Pallas kernels for 0% -> 21%
where the time goes in v1:
time: 1840 us; the launch traced here: 1830 us
  Pallas kernels  771 us (42%)
  waiting for transfers between devices  441 us (24%)
  local copies, waits for them, and re-layouts  199 us (11%)
  matrix products  186 us (10%)
  starting transfers between devices  119 us (6%)
  other arithmetic  102 us (6%)
    pallas_call x2, Pallas kernels, attend_back(): pl.pallas_call(functools.partial(attend_back_kernel, chunks), grid=(pairs...  515 us
    pallas_call x2, Pallas kernels, attend(): pl.pallas_call(functools.partial(attend_kernel, chunks), grid=(pairs,), i...  255 us
    dot_general x34, matrix products, dot(): lax.dot_general(left, right, (((left_axis,), (right_axis,)), ((), ())), p...  186 us
    all_gather x2, waiting for transfers between devices, body(): gathered = lax.all_gather(shard, BOTH, axis=0, tiled=True)  161 us
    ppermute x50, waiting for transfers between devices, send(): return lax.ppermute(half, 'doc', doc_flip(doc_size, bit))  155 us
    ppermute x20, waiting for transfers between devices, send(): return lax.ppermute(half, 'ctx', doc_flip(ctx_size, bit))  124 us
    ppermute x50, starting transfers between devices, send(): return lax.ppermute(half, 'doc', doc_flip(doc_size, bit))  55.8 us
    convert_element_type x50, other arithmetic, doc_step(): return (kept.astype(F32) + got.astype(F32)).astype(BF16)  52.9 us
  transfers between devices with their start and end apart: 87, of which 44 were waited for; matrix products, arithmetic and copies ran while one was open for 21% of the time, Pallas kernels for 21%

profile of v1, /device:TPU:0, one launch (start us, length us, event | category | flops | bytes accessed | tf_op | source)
XLA Modules:
  0.0 1834.6 jit_solution(16192604288786173790)
XLA Ops:
  15.3 160.8 %all-gather.3.cloned.1.call-done = bf16[1024,12672]{1,0:T(8,128)(2,1)} async-done(((bf16[32,12672]{1,0:T(8,128)(2,1)}), bf16[1024,12672]{1,0:T(8,128)(2,1)}) %all-gather.3.cloned.1.call-update) | async-done | bytes 25952272 | tf_op jit(solution)/shard_map/all_gather | solution.py:857
  200.7 7.7 slice.431
  216.6 7.2 collective-permute-start.2
  227.5 14.5 reshape.598
  242.1 10.4 copy.94
  259.1 127.8 %attend.2 = (bf16[288,1024]{1,0:T(8,128)(2,1)S(1)}, bf16[16,288,640]{2,1,0:T(8,128)(2,1)S(1)}) custom-call(bf16[288,3072]{1,0:T(8,128)(2,1)S(1)} %fusion.57.q_ref.refs_0_.refs_2_, bf16[288,3072]{1,0:T(8,128)(2,1)S(1)} %fusion.57.q_ref.refs_0_.refs_2_, bf16[288,2048]{1,0:T(8,128)(2,1)} %collective-permute-done.2.refs_1_.refs_3_, ...), custom_call_target="tpu_custom_call" | custom-call | flops 3397386240 | bytes 8257536 | tf_op jit(solution)/shard_map/attend/pallas_call | solution.py:168
  391.7 16.2 multiply_convert_fusion.1
  429.5 13.6 collective-permute-start.6
  446.9 7.7 slice.523
  454.6 14.9 reshape.603
  469.5 10.4 copy.96
  486.4 127.6 %attend.3 = (bf16[288,1024]{1,0:T(8,128)(2,1)S(1)}, bf16[16,288,640]{2,1,0:T(8,128)(2,1)S(1)}) custom-call(bf16[288,3072]{1,0:T(8,128)(2,1)S(1)} %fusion.54.q_ref.refs_0_.refs_2_, bf16[288,3072]{1,0:T(8,128)(2,1)S(1)} %fusion.54.q_ref.refs_0_.refs_2_, bf16[288,2048]{1,0:T(8,128)(2,1)} %collective-permute-done.6.refs_1_.refs_3_, ...), custom_call_target="tpu_custom_call" | custom-call | flops 3397386240 | bytes 8257536 | tf_op jit(solution)/shard_map/attend/pallas_call | solution.py:168
  618.8 16.4 multiply_convert_fusion
  639.6 8.2 fusion.286
  647.8 7.8 convert_reduce_fusion
  655.7 10.5 fusion.253
  679.2 257.4 %attend_back.2 = (f32[288,1024]{1,0:T(8,128)}, f32[576,1024]{1,0:T(8,128)}, f32[576,1024]{1,0:T(8,128)}, f32[2,128,1024]{2,1,0:T(8,128)}, f32[2,128,1024]{2,1,0:T(8,128)}) custom-call(bf16[288,3072]{1,0:T(8,128)(2,1)} %copy-done.4, bf16[288,3072]{1,0:T(8,128)(2,1)} %copy-done.4, bf16[288,2048]{1,0:T(8,128)(2,1)} %collective-permute-done.6.refs_1_.refs_3_, ...), custom_call_target="tpu_custom_call" | custom-call | flops 13589544960 | bytes 12976128 | tf_op jit(solution)/shard_map/attend_back/pallas_call | solution.py:381
  942.5 6.3 fusion.43
  948.8 6.0 fusion.41
  994.1 8.2 fusion.285
  1002.3 8.0 convert_reduce_fusion.1
  1010.4 6.4 multiply_reduce_fusion.2
  1016.8 8.5 fusion.256
  1032.5 5.6 fusion.145
  1039.4 257.9 %attend_back.3 = (f32[288,1024]{1,0:T(8,128)}, f32[576,1024]{1,0:T(8,128)}, f32[576,1024]{1,0:T(8,128)}, f32[2,128,1024]{2,1,0:T(8,128)}, f32[2,128,1024]{2,1,0:T(8,128)}) custom-call(bf16[288,3072]{1,0:T(8,128)(2,1)} %copy-done.3, bf16[288,3072]{1,0:T(8,128)(2,1)} %copy-done.3, bf16[288,2048]{1,0:T(8,128)(2,1)} %collective-permute-done.2.refs_1_.refs_3_, ...), custom_call_target="tpu_custom_call" | custom-call | flops 13589544960 | bytes 12976128 | tf_op jit(solution)/shard_map/attend_back/pallas_call | solution.py:381
  1301.1 5.6 fusion.149
  1320.4 6.2 fusion.40
  1344.5 6.1 fusion.42
  1363.4 9.0 collective-permute-done.41
  1417.5 5.6 fusion.131
  1435.2 6.4 convolution_add_fusion.1
  1469.7 7.4 collective-permute-start.34
  1520.4 6.3 fusion
  1531.4 8.7 fusion.2
  1548.4 23.8 %collective-permute-done.23 = bf16[2,128,1536]{2,1,0:T(8,128)(2,1)S(1)} collective-permute-done((bf16[2,128,1536]{2,1,0:T(8,128)(2,1)S(1)}, bf16[2,128,1536]{2,1,0:T(8,128)(2,1)S(1)}, u32[]{:S(2)}, u32[]{:S(2)}) %collective-permute-start.23) | collective-permute-done | bytes 786464 | tf_op jit(solution)/shard_map/ppermute | solution.py:625
  1577.9 19.1 %collective-permute-done.67 = bf16[2,512,512]{2,1,0:T(8,128)(2,1)S(1)} collective-permute-done((bf16[2,512,512]{2,1,0:T(8,128)(2,1)S(1)}, bf16[2,512,512]{2,1,0:T(8,128)(2,1)S(1)}, u32[]{:S(2)}, u32[]{:S(2)}) %collective-permute-start.67) | collective-permute-done | bytes 1048608 | tf_op jit(solution)/shard_map/ppermute | solution.py:625
  1602.3 20.8 %collective-permute-done.53 = bf16[2,128,2048]{2,1,0:T(8,128)(2,1)S(1)} collective-permute-done((bf16[2,128,2048]{2,1,0:T(8,128)(2,1)S(1)}, bf16[2,128,2048]{2,1,0:T(8,128)(2,1)S(1)}, u32[]{:S(2)}, u32[]{:S(2)}) %collective-permute-start.53) | collective-permute-done | bytes 1048608 | tf_op jit(solution)/shard_map/ppermute | solution.py:625
  1626.6 6.3 fusion.1
  1637.6 6.1 fusion.3
  1657.9 8.0 collective-permute-done.54
  1672.0 19.7 %collective-permute-done.27 = bf16[2,32,3072]{2,1,0:T(8,128)(2,1)S(1)} collective-permute-done((bf16[2,32,3072]{2,1,0:T(8,128)(2,1)S(1)}, bf16[2,32,3072]{2,1,0:T(8,128)(2,1)S(1)}, u32[]{:S(2)}, u32[]{:S(2)}) %collective-permute-start.27) | collective-permute-done | bytes 393248 | tf_op jit(solution)/shard_map/ppermute | solution.py:632
  1692.0 6.0 collective-permute-done.28
  1700.5 18.7 %collective-permute-done.55 = bf16[2,32,4096]{2,1,0:T(8,128)(2,1)S(1)} collective-permute-done((bf16[2,32,4096]{2,1,0:T(8,128)(2,1)S(1)}, bf16[2,32,4096]{2,1,0:T(8,128)(2,1)S(1)}, u32[]{:S(2)}, u32[]{:S(2)}) %collective-permute-start.55) | collective-permute-done | bytes 524320 | tf_op jit(solution)/shard_map/ppermute | solution.py:632
  1719.2 14.7 collective-permute-done.69
  1736.6 17.8 collective-permute-done.18
  1760.2 14.8 collective-permute-done.46
  1791.7 11.2 collective-permute-done.20
  1806.1 9.9 collective-permute-done.21
  (788 shorter events, 432.6 us)
Async XLA Ops:
  7.2 168.9 %all-gather.3.cloned.1.call-start = ((), (), s32[]{:S(2)}) async-start(), calls=%async_computation | async-start | bytes 26763264 | tf_op jit(solution)/shard_map/all_gather | solution.py:857
  14.8 406.0 %all-gather.5.cloned.1.call-start = ((), (), s32[]{:S(2)}) async-start(), calls=%async_computation.1 | async-start | bytes 26763264 | tf_op jit(solution)/shard_map/all_gather | solution.py:857
  176.9 22.9 %collective-permute-start = (bf16[144,1024]{1,0:T(8,128)(2,1)}, bf16[144,1024]{1,0:T(8,128)(2,1)S(1)}, u32[]{:S(2)}, u32[]{:S(2)}) collective-permute-start(bf16[144,1024]{1,0:T(8,128)(2,1)} %get-tuple-element.156), channel_id=1, source_target_pairs={{0,1},{1,0},{2,5},{3,4},{4,3},{5,2},{6,7},{7,6},{8,9},{9,8},{10,13... | collective-permute-start | bytes 884744 | tf_op jit(solution)/shard_map/ppermute | solution.py:520
  176.9 22.9 %collective-permute-start.1 = (bf16[144,1024]{1,0:T(8,128)(2,1)S(1)}, bf16[144,1024]{1,0:T(8,128)(2,1)S(1)}, u32[]{:S(2)}, u32[]{:S(2)}) collective-permute-start(bf16[144,1024]{1,0:T(8,128)(2,1)S(1)} %get-tuple-element.157), channel_id=1, source_target_pairs={{0,0},{1,1},{2,4},{3,5},{4,2},{5,3},{6,6},{7,7},{8,8},{9,9},{10,12... | collective-permute-start | bytes 884744 | tf_op jit(solution)/shard_map/ppermute | solution.py:520
  181.5 235.6 %collective-permute-start.10 = (bf16[144,1024]{1,0:T(8,128)(2,1)}, bf16[144,1024]{1,0:T(8,128)(2,1)}, u32[]{:S(2)}, u32[]{:S(2)}) collective-permute-start(bf16[144,1024]{1,0:T(8,128)(2,1)} %get-tuple-element.145), channel_id=1, source_target_pairs={{0,0},{1,1},{2,4},{3,5},{4,2},{5,3},{6,6},{7,7},{8,8},{9,9},{10,12... | collective-permute-start | bytes 884744 | tf_op jit(solution)/shard_map/ppermute | solution.py:520
  185.2 231.9 %collective-permute-start.9 = (bf16[144,1024]{1,0:T(8,128)(2,1)}, bf16[144,1024]{1,0:T(8,128)(2,1)}, u32[]{:S(2)}, u32[]{:S(2)}) collective-permute-start(bf16[144,1024]{1,0:T(8,128)(2,1)} %get-tuple-element.144), channel_id=1, source_target_pairs={{0,1},{1,0},{2,5},{3,4},{4,3},{5,2},{6,7},{7,6},{8,9},{9,8},{10,13... | collective-permute-start | bytes 884744 | tf_op jit(solution)/shard_map/ppermute | solution.py:520
  216.6 42.5 %collective-permute-start.2 = (bf16[288,2048]{1,0:T(8,128)(2,1)}, bf16[288,2048]{1,0:T(8,128)(2,1)}, u32[]{:S(2)}, u32[]{:S(2)}) collective-permute-start(bf16[288,2048]{1,0:T(8,128)(2,1)} %slice.496), channel_id=1, source_target_pairs={{0,4},{1,5},{2,6},{3,7},{4,0},{5,1},{6,2},{7,3},{8,12},{9,13},{10,... | collective-permute-start | bytes 3538952 | tf_op jit(solution)/shard_map/ppermute | solution.py:563
  429.5 56.9 %collective-permute-start.6 = (bf16[288,2048]{1,0:T(8,128)(2,1)}, bf16[288,2048]{1,0:T(8,128)(2,1)}, u32[]{:S(2)}, u32[]{:S(2)}) collective-permute-start(bf16[288,2048]{1,0:T(8,128)(2,1)} %slice.511), channel_id=1, source_target_pairs={{0,4},{1,5},{2,6},{3,7},{4,0},{5,1},{6,2},{7,3},{8,12},{9,13},{10,... | collective-permute-start | bytes 3538952 | tf_op jit(solution)/shard_map/ppermute | solution.py:563
  940.5 34.8 %collective-permute-start.11 = (bf16[288,2048]{1,0:T(8,128)(2,1)}, bf16[288,2048]{1,0:T(8,128)(2,1)}, u32[]{:S(2)}, u32[]{:S(2)}) collective-permute-start(bf16[288,2048]{1,0:T(8,128)(2,1)} %slice.729), channel_id=1, source_target_pairs={{0,4},{1,5},{2,6},{3,7},{4,0},{5,1},{6,2},{7,3},{8,12},{9,13},{10,... | collective-permute-start | bytes 3538952 | tf_op jit(solution)/shard_map/ppermute | solution.py:568
  948.8 571.7 %collective-permute-start.64 = (bf16[4,512,1024]{2,1,0:T(8,128)(2,1)}, bf16[4,512,1024]{2,1,0:T(8,128)(2,1)}, u32[]{:S(2)}, u32[]{:S(2)}) collective-permute-start(bf16[4,512,1024]{2,1,0:T(8,128)(2,1)} %fusion.43), channel_id=1, source_target_pairs={{0,4},{4,0},{8,12},{12,8},{16,20},{20,16},{24,28},{28,24},{1,5},{5... | collective-permute-start | bytes 12582920 | tf_op jit(solution)/shard_map/ppermute | solution.py:625
  967.6 563.9 %collective-permute-start.50 = (bf16[4,128,4096]{2,1,0:T(8,128)(2,1)}, bf16[4,128,4096]{2,1,0:T(8,128)(2,1)}, u32[]{:S(2)}, u32[]{:S(2)}) collective-permute-start(bf16[4,128,4096]{2,1,0:T(8,128)(2,1)} %fusion.41), channel_id=1, source_target_pairs={{0,4},{4,0},{8,12},{12,8},{16,20},{20,16},{24,28},{28,24},{1,5},{5... | collective-permute-start | bytes 12582920 | tf_op jit(solution)/shard_map/ppermute | solution.py:625
  973.0 377.6 %collective-permute-start.37 = (bf16[2,128,512]{2,1,0:T(8,128)(2,1)}, bf16[2,128,512]{2,1,0:T(8,128)(2,1)}, u32[]{:S(2)}, u32[]{:S(2)}) collective-permute-start(bf16[2,128,512]{2,1,0:T(8,128)(2,1)} %dynamic-slice_bitcast_fusion.41), channel_id=1, source_target_pairs={{0,16},{4,20},{8,24},{12,28},{16,0},{20,4},{24,8},{28,12},{1,17},{... | collective-permute-start | bytes 786440 | tf_op jit(solution)/shard_map/ppermute | solution.py:625
  975.3 376.4 %collective-permute-start.39 = (bf16[2,128,512]{2,1,0:T(8,128)(2,1)}, bf16[2,128,512]{2,1,0:T(8,128)(2,1)}, u32[]{:S(2)}, u32[]{:S(2)}) collective-permute-start(bf16[2,128,512]{2,1,0:T(8,128)(2,1)} %dynamic-slice_bitcast_fusion.40), channel_id=1, source_target_pairs={{0,8},{4,12},{8,0},{12,4},{16,24},{20,28},{24,16},{28,20},{1,9},{5... | collective-permute-start | bytes 786440 | tf_op jit(solution)/shard_map/ppermute | solution.py:625
  1315.7 95.3 %collective-permute-start.12 = (bf16[288,2048]{1,0:T(8,128)(2,1)}, bf16[288,2048]{1,0:T(8,128)(2,1)}, u32[]{:S(2)}, u32[]{:S(2)}) collective-permute-start(bf16[288,2048]{1,0:T(8,128)(2,1)} %slice.728), channel_id=1, source_target_pairs={{0,4},{1,5},{2,6},{3,7},{4,0},{5,1},{6,2},{7,3},{8,12},{9,13},{10,... | collective-permute-start | bytes 3538952 | tf_op jit(solution)/shard_map/ppermute | solution.py:568
  1362.8 42.5 %collective-permute-start.29 = (bf16[4,128,1024]{2,1,0:T(8,128)(2,1)}, bf16[4,128,1024]{2,1,0:T(8,128)(2,1)}, u32[]{:S(2)}, u32[]{:S(2)}) collective-permute-start(bf16[4,128,1024]{2,1,0:T(8,128)(2,1)} %fusion.147), channel_id=1, source_target_pairs={{0,4},{4,0},{8,12},{12,8},{16,20},{20,16},{24,28},{28,24},{1,5},{5... | collective-permute-start | bytes 3145736 | tf_op jit(solution)/shard_map/ppermute | solution.py:625
  1404.9 221.2 %collective-permute-start.57 = (bf16[4,512,1024]{2,1,0:T(8,128)(2,1)}, bf16[4,512,1024]{2,1,0:T(8,128)(2,1)}, u32[]{:S(2)}, u32[]{:S(2)}) collective-permute-start(bf16[4,512,1024]{2,1,0:T(8,128)(2,1)} %fusion.42), channel_id=1, source_target_pairs={{0,4},{4,0},{8,12},{12,8},{16,20},{20,16},{24,28},{28,24},{1,5},{5... | collective-permute-start | bytes 12582920 | tf_op jit(solution)/shard_map/ppermute | solution.py:625
  1408.6 44.7 %collective-permute-start.30 = (bf16[2,128,512]{2,1,0:T(8,128)(2,1)}, bf16[2,128,512]{2,1,0:T(8,128)(2,1)}, u32[]{:S(2)}, u32[]{:S(2)}) collective-permute-start(bf16[2,128,512]{2,1,0:T(8,128)(2,1)} %dynamic-slice_bitcast_fusion.43), channel_id=1, source_target_pairs={{0,16},{4,20},{8,24},{12,28},{16,0},{20,4},{24,8},{28,12},{1,17},{... | collective-permute-start | bytes 786440 | tf_op jit(solution)/shard_map/ppermute | solution.py:625
  1411.0 43.4 %collective-permute-start.32 = (bf16[2,128,512]{2,1,0:T(8,128)(2,1)}, bf16[2,128,512]{2,1,0:T(8,128)(2,1)}, u32[]{:S(2)}, u32[]{:S(2)}) collective-permute-start(bf16[2,128,512]{2,1,0:T(8,128)(2,1)} %dynamic-slice_bitcast_fusion.42), channel_id=1, source_target_pairs={{0,8},{4,12},{8,0},{12,4},{16,24},{20,28},{24,16},{28,20},{1,9},{5... | collective-permute-start | bytes 786440 | tf_op jit(solution)/shard_map/ppermute | solution.py:625
  1467.6 16.6 collective-permute-start.71
  1480.6 155.3 %collective-permute-start.43 = (bf16[4,128,4096]{2,1,0:T(8,128)(2,1)}, bf16[4,128,4096]{2,1,0:T(8,128)(2,1)}, u32[]{:S(2)}, u32[]{:S(2)}) collective-permute-start(bf16[4,128,4096]{2,1,0:T(8,128)(2,1)} %fusion.40), channel_id=1, source_target_pairs={{0,4},{4,0},{8,12},{12,8},{16,20},{20,16},{24,28},{28,24},{1,5},{5... | collective-permute-start | bytes 12582920 | tf_op jit(solution)/shard_map/ppermute | solution.py:625
  1517.5 25.1 %collective-permute-start.22 = (bf16[4,128,3072]{2,1,0:T(8,128)(2,1)}, bf16[4,128,3072]{2,1,0:T(8,128)(2,1)}, u32[]{:S(2)}, u32[]{:S(2)}) collective-permute-start(bf16[4,128,3072]{2,1,0:T(8,128)(2,1)} %fusion.61), channel_id=1, source_target_pairs={{0,4},{4,0},{8,12},{12,8},{16,20},{20,16},{24,28},{28,24},{1,5},{5... | collective-permute-start | bytes 9437192 | tf_op jit(solution)/shard_map/ppermute | solution.py:625
  1529.7 46.6 %collective-permute-start.65 = (bf16[2,512,512]{2,1,0:T(8,128)(2,1)S(1)}, bf16[2,512,512]{2,1,0:T(8,128)(2,1)}, u32[]{:S(2)}, u32[]{:S(2)}) collective-permute-start(bf16[2,512,512]{2,1,0:T(8,128)(2,1)S(1)} %dynamic-slice_bitcast_fusion.1), channel_id=1, source_target_pairs={{0,16},{4,20},{8,24},{12,28},{16,0},{20,4},{24,8},{28,12},{1,17},{... | collective-permute-start | bytes 3145736 | tf_op jit(solution)/shard_map/ppermute | solution.py:625
  1545.9 26.3 %collective-permute-start.23 = (bf16[2,128,1536]{2,1,0:T(8,128)(2,1)S(1)}, bf16[2,128,1536]{2,1,0:T(8,128)(2,1)S(1)}, u32[]{:S(2)}, u32[]{:S(2)}) collective-permute-start(bf16[2,128,1536]{2,1,0:T(8,128)(2,1)S(1)} %dynamic-slice_bitcast_fusion.9), channel_id=1, source_target_pairs={{0,16},{4,20},{8,24},{12,28},{16,0},{20,4},{24,8},{28,12},{1,17},{... | collective-permute-start | bytes 2359304 | tf_op jit(solution)/shard_map/ppermute | solution.py:625
  1546.2 27.8 %collective-permute-start.25 = (bf16[2,128,1536]{2,1,0:T(8,128)(2,1)S(1)}, bf16[2,128,1536]{2,1,0:T(8,128)(2,1)S(1)}, u32[]{:S(2)}, u32[]{:S(2)}) collective-permute-start(bf16[2,128,1536]{2,1,0:T(8,128)(2,1)S(1)} %dynamic-slice_bitcast_fusion.8), channel_id=1, source_target_pairs={{0,8},{4,12},{8,0},{12,4},{16,24},{20,28},{24,16},{28,20},{1,9},{5... | collective-permute-start | bytes 2359304 | tf_op jit(solution)/shard_map/ppermute | solution.py:625
  1572.2 24.8 %collective-permute-start.67 = (bf16[2,512,512]{2,1,0:T(8,128)(2,1)S(1)}, bf16[2,512,512]{2,1,0:T(8,128)(2,1)S(1)}, u32[]{:S(2)}, u32[]{:S(2)}) collective-permute-start(bf16[2,512,512]{2,1,0:T(8,128)(2,1)S(1)} %dynamic-slice_bitcast_fusion), channel_id=1, source_target_pairs={{0,8},{4,12},{8,0},{12,4},{16,24},{20,28},{24,16},{28,20},{1,9},{5... | collective-permute-start | bytes 3145736 | tf_op jit(solution)/shard_map/ppermute | solution.py:625
  1574.0 26.5 %collective-permute-start.51 = (bf16[2,128,2048]{2,1,0:T(8,128)(2,1)S(1)}, bf16[2,128,2048]{2,1,0:T(8,128)(2,1)S(1)}, u32[]{:S(2)}, u32[]{:S(2)}) collective-permute-start(bf16[2,128,2048]{2,1,0:T(8,128)(2,1)S(1)} %dynamic-slice_bitcast_fusion.5), channel_id=1, source_target_pairs={{0,16},{4,20},{8,24},{12,28},{16,0},{20,4},{24,8},{28,12},{1,17},{... | collective-permute-start | bytes 3145736 | tf_op jit(solution)/shard_map/ppermute | solution.py:625
  1576.3 68.1 %collective-permute-start.15 = (bf16[4,128,3072]{2,1,0:T(8,128)(2,1)}, bf16[4,128,3072]{2,1,0:T(8,128)(2,1)}, u32[]{:S(2)}, u32[]{:S(2)}) collective-permute-start(bf16[4,128,3072]{2,1,0:T(8,128)(2,1)} %fusion.60), channel_id=1, source_target_pairs={{0,4},{4,0},{8,12},{12,8},{16,20},{20,16},{24,28},{28,24},{1,5},{5... | collective-permute-start | bytes 9437192 | tf_op jit(solution)/shard_map/ppermute | solution.py:625
  1597.0 26.1 %collective-permute-start.53 = (bf16[2,128,2048]{2,1,0:T(8,128)(2,1)S(1)}, bf16[2,128,2048]{2,1,0:T(8,128)(2,1)S(1)}, u32[]{:S(2)}, u32[]{:S(2)}) collective-permute-start(bf16[2,128,2048]{2,1,0:T(8,128)(2,1)S(1)} %dynamic-slice_bitcast_fusion.4), channel_id=1, source_target_pairs={{0,8},{4,12},{8,0},{12,4},{16,24},{20,28},{24,16},{28,20},{1,9},{5... | collective-permute-start | bytes 3145736 | tf_op jit(solution)/shard_map/ppermute | solution.py:625
  1600.5 49.7 %collective-permute-start.24 = (bf16[128,1536]{1,0:T(8,128)(2,1)}, bf16[128,1536]{1,0:T(8,128)(2,1)}, u32[]{:S(2)}, u32[]{:S(2)}) collective-permute-start(bf16[128,1536]{1,0:T(8,128)(2,1)} %dynamic-slice_bitcast_fusion.26), channel_id=1, source_target_pairs={{0,8},{4,12},{8,0},{12,4},{16,24},{20,28},{24,16},{28,20},{1,9},{5... | collective-permute-start | bytes 1179656 | tf_op jit(solution)/shard_map/ppermute | solution.py:625
  1623.1 30.2 %collective-permute-start.26 = (bf16[128,1536]{1,0:T(8,128)(2,1)}, bf16[128,1536]{1,0:T(8,128)(2,1)}, u32[]{:S(2)}, u32[]{:S(2)}) collective-permute-start(bf16[128,1536]{1,0:T(8,128)(2,1)} %dynamic-slice_bitcast_fusion.25), channel_id=1, source_target_pairs={{0,16},{4,20},{8,24},{12,28},{16,0},{20,4},{24,8},{28,12},{1,17},{... | collective-permute-start | bytes 1179656 | tf_op jit(solution)/shard_map/ppermute | solution.py:625
  1626.3 41.0 %collective-permute-start.66 = (bf16[512,512]{1,0:T(8,128)(2,1)}, bf16[512,512]{1,0:T(8,128)(2,1)}, u32[]{:S(2)}, u32[]{:S(2)}) collective-permute-start(bf16[512,512]{1,0:T(8,128)(2,1)} %dynamic-slice_bitcast_fusion.14), channel_id=1, source_target_pairs={{0,8},{4,12},{8,0},{12,4},{16,24},{20,28},{24,16},{28,20},{1,9},{5... | collective-permute-start | bytes 1572872 | tf_op jit(solution)/shard_map/ppermute | solution.py:625
  1635.9 33.5 %collective-permute-start.68 = (bf16[512,512]{1,0:T(8,128)(2,1)}, bf16[512,512]{1,0:T(8,128)(2,1)}, u32[]{:S(2)}, u32[]{:S(2)}) collective-permute-start(bf16[512,512]{1,0:T(8,128)(2,1)} %dynamic-slice_bitcast_fusion.13), channel_id=1, source_target_pairs={{0,16},{4,20},{8,24},{12,28},{16,0},{20,4},{24,8},{28,12},{1,17},{... | collective-permute-start | bytes 1572872 | tf_op jit(solution)/shard_map/ppermute | solution.py:625
  1651.0 14.9 collective-permute-start.54
  1653.4 101.4 %collective-permute-start.58 = (bf16[2,512,512]{2,1,0:T(8,128)(2,1)S(1)}, bf16[2,512,512]{2,1,0:T(8,128)(2,1)S(1)}, u32[]{:S(2)}, u32[]{:S(2)}) collective-permute-start(bf16[2,512,512]{2,1,0:T(8,128)(2,1)S(1)} %copy-done.85), channel_id=1, source_target_pairs={{0,16},{4,20},{8,24},{12,28},{16,0},{20,4},{24,8},{28,12},{1,17},{... | collective-permute-start | bytes 3145736 | tf_op jit(solution)/shard_map/ppermute | solution.py:625
  1657.2 101.7 %collective-permute-start.60 = (bf16[2,512,512]{2,1,0:T(8,128)(2,1)S(1)}, bf16[2,512,512]{2,1,0:T(8,128)(2,1)S(1)}, u32[]{:S(2)}, u32[]{:S(2)}) collective-permute-start(bf16[2,512,512]{2,1,0:T(8,128)(2,1)S(1)} %copy-done.84), channel_id=1, source_target_pairs={{0,8},{4,12},{8,0},{12,4},{16,24},{20,28},{24,16},{28,20},{1,9},{5... | collective-permute-start | bytes 3145736 | tf_op jit(solution)/shard_map/ppermute | solution.py:625
  1665.9 91.3 %collective-permute-start.44 = (bf16[2,128,2048]{2,1,0:T(8,128)(2,1)S(1)}, bf16[2,128,2048]{2,1,0:T(8,128)(2,1)S(1)}, u32[]{:S(2)}, u32[]{:S(2)}) collective-permute-start(bf16[2,128,2048]{2,1,0:T(8,128)(2,1)S(1)} %dynamic-slice_bitcast_fusion.7), channel_id=1, source_target_pairs={{0,16},{4,20},{8,24},{12,28},{16,0},{20,4},{24,8},{28,12},{1,17},{... | collective-permute-start | bytes 3145736 | tf_op jit(solution)/shard_map/ppermute | solution.py:625
  1667.3 68.1 %collective-permute-start.16 = (bf16[2,128,1536]{2,1,0:T(8,128)(2,1)S(1)}, bf16[2,128,1536]{2,1,0:T(8,128)(2,1)S(1)}, u32[]{:S(2)}, u32[]{:S(2)}) collective-permute-start(bf16[2,128,1536]{2,1,0:T(8,128)(2,1)S(1)} %dynamic-slice_bitcast_fusion.11), channel_id=1, source_target_pairs={{0,16},{4,20},{8,24},{12,28},{16,0},{20,4},{24,8},{28,12},{1,17},{... | collective-permute-start | bytes 2359304 | tf_op jit(solution)/shard_map/ppermute | solution.py:625
  1669.4 22.2 %collective-permute-start.27 = (bf16[2,32,3072]{2,1,0:T(8,128)(2,1)S(1)}, bf16[2,32,3072]{2,1,0:T(8,128)(2,1)S(1)}, u32[]{:S(2)}, u32[]{:S(2)}) collective-permute-start(bf16[2,32,3072]{2,1,0:T(8,128)(2,1)S(1)} %dynamic-slice_bitcast_fusion.24), channel_id=1, source_target_pairs={{0,2},{1,3},{2,0},{3,1},{4,6},{5,7},{6,4},{7,5},{8,10},{9,11},{10,... | collective-permute-start | bytes 1179656 | tf_op jit(solution)/shard_map/ppermute | solution.py:632
  1698.1 21.0 %collective-permute-start.55 = (bf16[2,32,4096]{2,1,0:T(8,128)(2,1)S(1)}, bf16[2,32,4096]{2,1,0:T(8,128)(2,1)S(1)}, u32[]{:S(2)}, u32[]{:S(2)}) collective-permute-start(bf16[2,32,4096]{2,1,0:T(8,128)(2,1)S(1)} %dynamic-slice_bitcast_fusion.18), channel_id=1, source_target_pairs={{0,2},{1,3},{2,0},{3,1},{4,6},{5,7},{6,4},{7,5},{8,10},{9,11},{10,... | collective-permute-start | bytes 1572872 | tf_op jit(solution)/shard_map/ppermute | solution.py:632
  1733.9 20.5 %collective-permute-start.18 = (bf16[2,128,1536]{2,1,0:T(8,128)(2,1)S(1)}, bf16[2,128,1536]{2,1,0:T(8,128)(2,1)S(1)}, u32[]{:S(2)}, u32[]{:S(2)}) collective-permute-start(bf16[2,128,1536]{2,1,0:T(8,128)(2,1)S(1)} %dynamic-slice_bitcast_fusion.10), channel_id=1, source_target_pairs={{0,8},{4,12},{8,0},{12,4},{16,24},{20,28},{24,16},{28,20},{1,9},{5... | collective-permute-start | bytes 2359304 | tf_op jit(solution)/shard_map/ppermute | solution.py:625
  1735.3 39.6 %collective-permute-start.46 = (bf16[2,128,2048]{2,1,0:T(8,128)(2,1)S(1)}, bf16[2,128,2048]{2,1,0:T(8,128)(2,1)S(1)}, u32[]{:S(2)}, u32[]{:S(2)}) collective-permute-start(bf16[2,128,2048]{2,1,0:T(8,128)(2,1)S(1)} %dynamic-slice_bitcast_fusion.6), channel_id=1, source_target_pairs={{0,8},{4,12},{8,0},{12,4},{16,24},{20,28},{24,16},{28,20},{1,9},{5... | collective-permute-start | bytes 3145736 | tf_op jit(solution)/shard_map/ppermute | solution.py:625
  1754.4 23.3 %collective-permute-start.70 = (bf16[1,128,1024]{2,1,0:T(8,128)(2,1)S(1)}, bf16[1,128,1024]{2,1,0:T(8,128)(2,1)S(1)}, u32[]{:S(2)}, u32[]{:S(2)}) collective-permute-start(bf16[1,128,1024]{2,1,0:T(8,128)(2,1)S(1)} %dynamic-slice_convert_fusion.8), channel_id=1, source_target_pairs={{0,1},{1,0},{2,3},{3,2},{4,5},{5,4},{6,7},{7,6},{8,9},{9,8},{10,11... | collective-permute-start | bytes 786440 | tf_op jit(solution)/shard_map/ppermute | solution.py:632
  1754.7 21.9 %collective-permute-start.56 = (bf16[1,32,4096]{2,1,0:T(8,128)(2,1)S(1)}, bf16[1,32,4096]{2,1,0:T(8,128)(2,1)S(1)}, u32[]{:S(2)}, u32[]{:S(2)}) collective-permute-start(bf16[1,32,4096]{2,1,0:T(8,128)(2,1)S(1)} %dynamic-slice_convert_fusion.10), channel_id=1, source_target_pairs={{0,1},{1,0},{2,3},{3,2},{4,5},{5,4},{6,7},{7,6},{8,9},{9,8},{10,11... | collective-permute-start | bytes 786440 | tf_op jit(solution)/shard_map/ppermute | solution.py:632
  1757.2 22.0 %collective-permute-start.17 = (bf16[128,1536]{1,0:T(8,128)(2,1)S(1)}, bf16[128,1536]{1,0:T(8,128)(2,1)S(1)}, u32[]{:S(2)}, u32[]{:S(2)}) collective-permute-start(bf16[128,1536]{1,0:T(8,128)(2,1)S(1)} %dynamic-slice_bitcast_fusion.29), channel_id=1, source_target_pairs={{0,8},{4,12},{8,0},{12,4},{16,24},{20,28},{24,16},{28,20},{1,9},{5... | collective-permute-start | bytes 1179656 | tf_op jit(solution)/shard_map/ppermute | solution.py:625
  1758.9 21.6 %collective-permute-start.19 = (bf16[128,1536]{1,0:T(8,128)(2,1)S(1)}, bf16[128,1536]{1,0:T(8,128)(2,1)S(1)}, u32[]{:S(2)}, u32[]{:S(2)}) collective-permute-start(bf16[128,1536]{1,0:T(8,128)(2,1)S(1)} %dynamic-slice_bitcast_fusion.28), channel_id=1, source_target_pairs={{0,16},{4,20},{8,24},{12,28},{16,0},{20,4},{24,8},{28,12},{1,17},{... | collective-permute-start | bytes 1179656 | tf_op jit(solution)/shard_map/ppermute | solution.py:625
  1780.7 22.2 %collective-permute-start.20 = (bf16[2,32,3072]{2,1,0:T(8,128)(2,1)S(1)}, bf16[2,32,3072]{2,1,0:T(8,128)(2,1)S(1)}, u32[]{:S(2)}, u32[]{:S(2)}) collective-permute-start(bf16[2,32,3072]{2,1,0:T(8,128)(2,1)S(1)} %dynamic-slice_bitcast_fusion.27), channel_id=1, source_target_pairs={{0,2},{1,3},{2,0},{3,1},{4,6},{5,7},{6,4},{7,5},{8,10},{9,11},{10,... | collective-permute-start | bytes 1179656 | tf_op jit(solution)/shard_map/ppermute | solution.py:632
  1786.2 30.7 %collective-permute-start.62 = (bf16[2,128,1024]{2,1,0:T(8,128)(2,1)S(1)}, bf16[2,128,1024]{2,1,0:T(8,128)(2,1)S(1)}, u32[]{:S(2)}, u32[]{:S(2)}) collective-permute-start(bf16[2,128,1024]{2,1,0:T(8,128)(2,1)S(1)} %dynamic-slice_bitcast_fusion.15), channel_id=1, source_target_pairs={{0,2},{1,3},{2,0},{3,1},{4,6},{5,7},{6,4},{7,5},{8,10},{9,11},{10,... | collective-permute-start | bytes 1572872 | tf_op jit(solution)/shard_map/ppermute | solution.py:632
  1803.2 16.6 collective-permute-start.48
  (173 other events, 4536.8 us)
Sparse Core Ops, SparseCore 0:
  14.9 161.0 all-gather.2
  179.4 166.3 all-gather.4

commit v2 on v1

v2 whole, which is shorter than its diff:
```python
import functools

import jax
import jax.numpy as jnp
from jax import lax
from jax.experimental import pallas as pl
from jax.experimental.pallas import tpu as pltpu
from jax.sharding import PartitionSpec as P

HEADS = 16
HEAD_DIM = 64
BUCKETS = 128
TEXT = 512
PATCH = 49
GRID_SIDE = 32
CELLS = GRID_SIDE * GRID_SIDE
LANES = 128
PAIR = 2 * HEAD_DIM
NORM_EPSILON = 1e-05
SCORE_SCALE = (3.0 * HEAD_DIM) ** (-0.5)
MASKED = -1e30
FIXED_TOP = 16000.0
BF16 = jnp.bfloat16
F32 = jnp.float32
BOTH = ("doc", "ctx")


def pad_lanes(count):
    return -(-count // LANES) * LANES


def norm_rows(values_in, scale_gain, offset):
    centered = values_in - jnp.mean(values_in, axis=-1, keepdims=True)
    spread = jnp.mean(centered * centered, axis=-1, keepdims=True)
    return centered * lax.rsqrt(spread + NORM_EPSILON) * scale_gain + offset


def exact_gelu(values_in):
    return jax.nn.gelu(values_in, approximate=False)


def dot(left, right, left_axis, right_axis):
    return lax.dot_general(
        left, right, (((left_axis,), (right_axis,)), ((), ())), preferred_element_type=F32
    )


def lookup(table, index):
    return jnp.take_along_axis(table, index, axis=1, mode="promise_in_bounds")


def head_lanes(head, rows):
    lane = lax.broadcasted_iota(jnp.int32, (rows, PAIR), 1)
    return (lane >= head * HEAD_DIM) & (lane < (head + 1) * HEAD_DIM)


def keep_head(values, head):
    return jnp.where(head_lanes(head, values.shape[0]), values, jnp.zeros_like(values))


def keep_both(table):
    return jnp.concatenate([keep_head(table, 0), keep_head(table, 1)], axis=0)


def paired_lookup(tables, indices):
    top = [jnp.max(jnp.abs(table)) for table in tables]
    top = jnp.maximum(jnp.maximum(top[0], top[1]), 1e-30)
    fine = FIXED_TOP / top
    total = None
    for table, index in zip(tables, indices):
        steps = jnp.round(table * fine).astype(jnp.int32)
        both = steps[:, :BUCKETS] * 65536 + steps[:, BUCKETS:]
        found = lookup(both, index)
        total = found if total is None else total + found
    coarse = top / FIXED_TOP
    first = (total + 32768) >> 16
    second = (total << 16) >> 16
    return first.astype(F32) * coarse, second.astype(F32) * coarse


def attend_kernel(
    chunks,
    q_ref,
    *refs,
):
    k_refs = refs[:chunks]
    v_refs = refs[chunks : 2 * chunks]
    (
        rel_key_ref,
        rel_query_ref,
        index_linear_ref,
        index_planar_ref,
        turned_linear_ref,
        turned_planar_ref,
        mask_ref,
        mixed_ref,
        prob_ref,
        left_scr,
        right_scr,
        value_scr,
    ) = refs[2 * chunks :]
    rows = q_ref.shape[0]
    keys = rows * chunks
    keys_wide = right_scr.shape[0]
    rows_wide = left_scr.shape[1] - PAIR

    @pl.when(pl.program_id(0) == 0)
    def _():
        row_at = lax.broadcasted_iota(jnp.int32, (rows, rows_wide), 0)
        lane_at = lax.broadcasted_iota(jnp.int32, (rows, rows_wide), 1)
        left_scr[:, PAIR:] = jnp.where(row_at == lane_at, 1.0, 0.0).astype(BF16)
        right_scr[keys:, :] = jnp.zeros((keys_wide - keys, PAIR + rows_wide), BF16)
        value_scr[keys:, :] = jnp.zeros((keys_wide - keys, PAIR), BF16)

    for chunk in range(chunks):
        right_scr[chunk * rows : (chunk + 1) * rows, :PAIR] = k_refs[chunk][...]
        value_scr[chunk * rows : (chunk + 1) * rows, :] = v_refs[chunk][...]

    query = q_ref[...]
    key = right_scr[:keys, :PAIR]
    key_bias = paired_lookup(
        [dot(key, keep_both(rel_query_ref[kind]), 1, 1) for kind in range(2)],
        [turned_linear_ref[...], turned_planar_ref[...]],
    )
    query_bias = paired_lookup(
        [dot(query, keep_both(rel_key_ref[kind]), 1, 1) for kind in range(2)],
        [index_linear_ref[...], index_planar_ref[...]],
    )
    mixed = []
    for head in range(2):
        left_scr[:, :PAIR] = keep_head(query, head)
        right_scr[:keys, PAIR:] = key_bias[head].astype(BF16)
        raw = dot(left_scr[...], right_scr[...], 1, 1) + query_bias[head]
        scaled = raw * SCORE_SCALE + mask_ref[...]
        shifted = scaled - jnp.max(scaled, axis=-1, keepdims=True)
        exponent = jnp.exp(shifted)
        inverse = 1.0 / jnp.sum(exponent, axis=-1, keepdims=True)
        prob = (exponent * inverse).astype(BF16)
        prob_ref[head] = prob
        mixed.append(dot(prob, value_scr[...], 1, 0))
    mixed_ref[...] = jnp.where(head_lanes(1, rows), mixed[1], mixed[0]).astype(BF16)


def whole_spec(array):
    return pl.BlockSpec(array.shape, lambda step: (0,) * array.ndim)


def attend(qkv, other_kv, rel_key, rel_query, lookups):
    rows = qkv.shape[0]
    width = qkv.shape[1] // 3
    pairs = width // PAIR
    chunks = 1 + len(other_kv)
    keys_wide = pad_lanes(rows * chunks)
    rows_wide = pad_lanes(rows)

    def column(offset):
        return pl.BlockSpec((rows, PAIR), lambda step: (0, offset + step))

    rel_spec = pl.BlockSpec((2, BUCKETS, PAIR), lambda step: (0, 0, step))
    small = (
        lookups["index_linear"],
        lookups["index_planar"],
        lookups["turned_linear"],
        lookups["turned_planar"],
        lookups["mask"],
    )
    return pl.pallas_call(
        functools.partial(attend_kernel, chunks),
        grid=(pairs,),
        in_specs=[column(0), column(pairs)]
        + [column(0)] * (chunks - 1)
        + [column(2 * pairs)]
        + [column(pairs)] * (chunks - 1)
        + [rel_spec, rel_spec]
        + [whole_spec(item) for item in small],
        out_specs=[
            pl.BlockSpec((rows, PAIR), lambda step: (0, step)),
            pl.BlockSpec((2, rows, keys_wide), lambda step: (step, 0, 0)),
        ],
        out_shape=[
            jax.ShapeDtypeStruct((rows, width), BF16),
            jax.ShapeDtypeStruct((2 * pairs, rows, keys_wide), BF16),
        ],
        scratch_shapes=[
            pltpu.VMEM((rows, PAIR + rows_wide), BF16),
            pltpu.VMEM((keys_wide, PAIR + rows_wide), BF16),
            pltpu.VMEM((keys_wide, PAIR), BF16),
        ],
        compiler_params=pltpu.CompilerParams(vmem_limit_bytes=40 << 20),
        cost_estimate=pl.CostEstimate(
            flops=20 * rows * rows * chunks * width,
            bytes_accessed=4 * pairs * rows * keys_wide + 8 * rows * width,
            transcendentals=2 * pairs * rows * keys_wide,
        ),
        name="attend",
    )(qkv, qkv, *other_kv, qkv, *other_kv, rel_key, rel_query, *small)


def bucket_sums(cells, pos):
    spot = pos & (LANES - 1)
    part = pos >> 7
    total = jnp.zeros(spot.shape, F32)
    for chunk in range(CELLS // LANES):
        total = jnp.where(
            part == chunk, lookup(cells[:, chunk * LANES : (chunk + 1) * LANES], spot), total
        )
    lane = lax.broadcasted_iota(jnp.int32, total.shape, 1)
    total = total - jnp.where(lane < BUCKETS - 8, pltpu.roll(total, BUCKETS - 8, 1), 0.0)
    return total - jnp.where((lane & 7) < 7, pltpu.roll(total, BUCKETS - 1, 1), 0.0)


def band_sums(values, index, pos):
    spot = pos & (LANES - 1)
    part = pos >> 7
    total = jnp.zeros(spot.shape, F32)
    for chunk in range(values.shape[1] // LANES):
        total = jnp.where(
            part == chunk, lookup(values[:, chunk * LANES : (chunk + 1) * LANES], spot), total
        )
    low = jnp.sum(jnp.where(index == 0, values, 0.0), axis=-1, keepdims=True)
    high = jnp.sum(jnp.where(index == BUCKETS - 1, values, 0.0), axis=-1, keepdims=True)
    lane = lax.broadcasted_iota(jnp.int32, total.shape, 1)
    return jnp.where(lane == 0, low, jnp.where(lane == BUCKETS - 1, high, total))


def attend_back_kernel(
    chunks,
    q_ref,
    *refs,
):
    k_refs = refs[:chunks]
    v_refs = refs[chunks : 2 * chunks]
    (
        grad_ref,
        prob_ref,
        rel_key_ref,
        rel_query_ref,
        index_linear_ref,
        turned_linear_ref,
        key_cells_ref,
        row_cells_ref,
        planar_pos_ref,
        linear_pos_ref,
        turned_planar_pos_ref,
        turned_linear_pos_ref,
        grad_query_ref,
        grad_kv_ref,
        grad_rel_ref,
        key_scr,
        value_scr,
        raw_scr,
        low_scr,
        turned_scr,
        cell_scr,
    ) = refs[2 * chunks :]
    rows = q_ref.shape[0]
    keys = rows * chunks
    keys_wide = key_scr.shape[0]
    rows_wide = raw_scr.shape[0]

    @pl.when(pl.program_id(0) == 0)
    def _():
        key_scr[keys:, :] = jnp.zeros((keys_wide - keys, PAIR), BF16)
        value_scr[keys:, :] = jnp.zeros((keys_wide - keys, PAIR), BF16)
        raw_scr[rows:, :] = jnp.zeros((rows_wide - rows, keys_wide), F32)

    for chunk in range(chunks):
        key_scr[chunk * rows : (chunk + 1) * rows, :] = k_refs[chunk][...]
        value_scr[chunk * rows : (chunk + 1) * rows, :] = v_refs[chunk][...]

    found = []
    for head in range(2):
        query = keep_head(q_ref[...], head)
        grad = keep_head(grad_ref[...], head)
        raw_scr[:rows, :] = dot(grad, value_scr[...], 1, 1)
        prob = prob_ref[head].astype(F32)
        grad_prob = raw_scr[:rows, :]
        inner = jnp.sum(prob * grad_prob, axis=-1, keepdims=True)
        grad_raw = (prob * (grad_prob - inner) * SCORE_SCALE).astype(BF16)
        low_scr[...] = grad_raw
        raw_scr[:rows, :] = grad_raw.astype(F32)

        cell_scr[:rows, :] = dot(low_scr[...], key_cells_ref[...], 1, 0)
        planar = bucket_sums(cell_scr[:rows, :], planar_pos_ref[...])
        linear = band_sums(raw_scr[:rows, :], index_linear_ref[...], linear_pos_ref[...])
        row_bucket = jnp.concatenate([linear.astype(BF16), planar.astype(BF16)], axis=1)
        rel_key = keep_head(rel_key_ref[...].reshape(2 * BUCKETS, PAIR), head)
        rel_query = keep_head(rel_query_ref[...].reshape(2 * BUCKETS, PAIR), head)
        grad_query = dot(low_scr[...], key_scr[...], 1, 0) + dot(row_bucket, rel_key, 1, 0)
        grad_rel_key = dot(row_bucket, query, 0, 0)

        turned_scr[...] = raw_scr[...].T[:keys]
        turned_low = turned_scr[...].astype(BF16)
        cell_scr[...] = dot(turned_low, row_cells_ref[...], 1, 0)
        planar = bucket_sums(cell_scr[...], turned_planar_pos_ref[...])
        linear = band_sums(turned_scr[...], turned_linear_ref[...], turned_linear_pos_ref[...])
        key_bucket = jnp.concatenate([linear.astype(BF16), planar.astype(BF16)], axis=1)
        grad_key = dot(turned_low[:, :rows], query, 1, 0) + dot(key_bucket, rel_query, 1, 0)
        grad_value = dot(prob_ref[head], grad, 0, 0)[:keys]
        grad_rel_query = dot(key_bucket, key_scr[:keys, :], 0, 0)
        found.append((grad_query, grad_key, grad_value, grad_rel_query, grad_rel_key))

    def joined(member):
        first, second = found[0][member], found[1][member]
        return jnp.where(head_lanes(1, first.shape[0]), second, first).astype(BF16)

    grad_query_ref[...] = joined(0)
    grad_key, grad_value = joined(1), joined(2)
    for chunk in range(chunks):
        grad_kv_ref[chunk, 0] = grad_key[chunk * rows : (chunk + 1) * rows]
        grad_kv_ref[chunk, 1] = grad_value[chunk * rows : (chunk + 1) * rows]
    grad_rel_ref[0] = joined(3)
    grad_rel_ref[1] = joined(4)


def attend_back(qkv, other_kv, grad_mixed, prob, rel_key, rel_query, lookups, first, count):
    rows = qkv.shape[0]
    width = qkv.shape[1] // 3
    pairs = width // PAIR
    chunks = 1 + len(other_kv)
    keys = rows * chunks
    keys_wide = pad_lanes(keys)
    rows_wide = pad_lanes(rows)
    part = count * PAIR

    def column(offset):
        return pl.BlockSpec((rows, PAIR), lambda step: (0, offset + first + step))

    rel_spec = pl.BlockSpec((2, BUCKETS, PAIR), lambda step: (0, 0, first + step))
    small = (
        lookups["index_linear"],
        lookups["turned_linear"],
        lookups["key_cells"],
        lookups["row_cells"],
        lookups["planar_pos"],
        lookups["linear_pos"],
        lookups["turned_planar_pos"],
        lookups["turned_linear_pos"],
    )
    return pl.pallas_call(
        functools.partial(attend_back_kernel, chunks),
        grid=(count,),
        in_specs=[column(0), column(pairs)]
        + [column(0)] * (chunks - 1)
        + [column(2 * pairs)]
        + [column(pairs)] * (chunks - 1)
        + [
            column(0),
            pl.BlockSpec((2, rows, keys_wide), lambda step: (first + step, 0, 0)),
            rel_spec,
            rel_spec,
        ]
        + [whole_spec(item) for item in small],
        out_specs=[
            pl.BlockSpec((rows, PAIR), lambda step: (0, step)),
            pl.BlockSpec((chunks, 2, rows, PAIR), lambda step: (0, 0, 0, step)),
            pl.BlockSpec((2, 2 * BUCKETS, PAIR), lambda step: (0, 0, step)),
        ],
        out_shape=[
            jax.ShapeDtypeStruct((rows, part), BF16),
            jax.ShapeDtypeStruct((chunks, 2, rows, part), BF16),
            jax.ShapeDtypeStruct((2, 2 * BUCKETS, part), BF16),
        ],
        scratch_shapes=[
            pltpu.VMEM((keys_wide, PAIR), BF16),
            pltpu.VMEM((keys_wide, PAIR), BF16),
            pltpu.VMEM((rows_wide, keys_wide), F32),
            pltpu.VMEM((rows, keys_wide), BF16),
            pltpu.VMEM((keys, rows_wide), F32),
            pltpu.VMEM((keys, CELLS), F32),
        ],
        compiler_params=pltpu.CompilerParams(vmem_limit_bytes=56 << 20),
        cost_estimate=pl.CostEstimate(
            flops=80 * rows * rows * chunks * part,
            bytes_accessed=4 * count * rows * keys_wide + 24 * rows * part,
            transcendentals=0,
        ),
        name="attend_back",
    )(qkv, qkv, *other_kv, qkv, *other_kv, grad_mixed, prob, rel_key, rel_query, *small)


def make_lookups(cells_x, cells_y, count, place, row_count):
    seq_len = place.shape[0]
    keys_wide = pad_lanes(seq_len)
    rows_wide = pad_lanes(row_count)
    half_range = BUCKETS // 2

    def wide(values, total):
        return jnp.pad(values, ((0, total - values.shape[0]),))

    key_place, key_x, key_y = (wide(item, keys_wide) for item in (place, cells_x, cells_y))
    row_place, row_x, row_y = (item[:row_count] for item in (place, cells_x, cells_y))
    wide_place, wide_x, wide_y = (wide(item, rows_wide) for item in (row_place, row_x, row_y))

    def linear(i, j):
        return jnp.clip(i - j, -half_range, half_range - 1) + half_range

    def planar(ix, iy, jx, jy):
        return (jnp.clip(ix - jx, -8, 7) + 8) * 8 + jnp.clip(iy - jy, -4, 3) + 4

    out = {}
    out["index_linear"] = linear(row_place[:, None], key_place[None, :])
    out["index_planar"] = planar(row_x[:, None], row_y[:, None], key_x[None, :], key_y[None, :])
    out["turned_linear"] = linear(wide_place[None, :], place[:, None])
    out["turned_planar"] = planar(
        wide_x[None, :], wide_y[None, :], cells_x[:, None], cells_y[:, None]
    )
    valid = (place < count) | ((place >= TEXT) & (place < TEXT + PATCH))
    out["mask"] = jnp.pad(
        jnp.where(valid, 0.0, MASKED).astype(F32),
        ((0, keys_wide - seq_len),),
        constant_values=MASKED,
    )[None]
    key_live = jnp.arange(keys_wide) < seq_len
    row_live = jnp.arange(rows_wide) < row_count
    cell = jnp.arange(CELLS, dtype=jnp.int32)
    cell_x, cell_y = cell // GRID_SIDE, cell % GRID_SIDE
    out["key_cells"] = (
        key_live[:, None] & (key_x[:, None] <= cell_x) & (key_y[:, None] <= cell_y)
    ).astype(BF16)
    out["row_cells"] = (
        row_live[:, None] & (wide_x[:, None] >= cell_x) & (wide_y[:, None] >= cell_y)
    ).astype(BF16)
    bucket = jnp.arange(BUCKETS, dtype=jnp.int32)
    bucket_x, bucket_y = bucket // 8, bucket % 8
    top = GRID_SIDE - 1
    to_x = jnp.where(bucket_x == 0, top, jnp.minimum(row_x[:, None] - bucket_x + 8, top))
    to_y = jnp.where(bucket_y == 0, top, jnp.minimum(row_y[:, None] - bucket_y + 4, top))
    out["planar_pos"] = jnp.where((to_x >= 0) & (to_y >= 0), to_x * GRID_SIDE + to_y, -1)
    from_x = jnp.where(bucket_x == 0, 0, jnp.maximum(cells_x[:, None] + bucket_x - 8, 0))
    from_y = jnp.where(bucket_y == 0, 0, jnp.maximum(cells_y[:, None] + bucket_y - 4, 0))
    out["turned_planar_pos"] = jnp.where(
        (from_x <= top) & (from_y <= top), from_x * GRID_SIDE + from_y, -1
    )
    first_place = place[0]
    target = row_place[:, None] - bucket + half_range
    out["linear_pos"] = jnp.where(
        (target >= 0) & (target < seq_len), (target - first_place) % seq_len, -1
    )
    source = place[:, None] + bucket - half_range - first_place
    out["turned_linear_pos"] = jnp.where((source >= 0) & (source < row_count), source, -1)
    return out


class Home:
    def __init__(self, mesh_shape, local_docs, block_rows, width):
        self.width = width
        self.doc_size = mesh_shape["doc"]
        self.ctx_size = mesh_shape["ctx"]
        self.block = block_rows
        self.docs = 2 * local_docs
        self.span = self.ctx_size // self.docs
        self.group = 2 * self.span
        self.rows = 2 * block_rows
        self.seq = block_rows * self.ctx_size

    def flat(self, doc, ctx):
        return doc * self.ctx_size + ctx

    def move_pairs(self, turn):
        pairs = []
        for pair in range(self.doc_size // 2):
            for core in range(2):
                for block in range(self.ctx_size):
                    slot = (block + turn) % 2
                    doc = 2 * core + slot
                    place = block // 2
                    target = self.flat(
                        2 * pair + place // self.span, doc * self.span + place % self.span
                    )
                    pairs.append((self.flat(2 * pair + core, block), target))
        return pairs

    def to_home(self, local):
        ctx = lax.axis_index("ctx")
        doc_here = ctx // self.span
        pieces = []
        for turn in range(2):
            piece = lax.dynamic_index_in_dim(local, (ctx + turn) % 2, 0, keepdims=False)
            pieces.append(lax.ppermute(piece, BOTH, self.move_pairs(turn)))
        swap = (doc_here % 2) == 1
        low_half = jnp.where(swap, pieces[1], pieces[0])
        high_half = jnp.where(swap, pieces[0], pieces[1])
        return jnp.concatenate([low_half, high_half], axis=0)

    def from_home(self, rows):
        ctx = lax.axis_index("ctx")
        doc_here = ctx // self.span
        halves = rows.reshape(2, self.block, rows.shape[1])
        pieces = []
        for turn in range(2):
            piece = lax.dynamic_index_in_dim(halves, (doc_here + turn) % 2, 0, keepdims=False)
            back = [(target, source) for source, target in self.move_pairs(turn)]
            pieces.append(lax.ppermute(piece, BOTH, back))
        swap = (ctx % 2) == 1
        first = jnp.where(swap, pieces[1], pieces[0])
        second = jnp.where(swap, pieces[0], pieces[1])
        return jnp.stack([first, second])

    def core_half(self, values, core):
        block = self.width // self.doc_size
        pieces = []
        for start in range(0, values.shape[1], 2 * block):
            first = values[:, start : start + block]
            second = values[:, start + block : start + 2 * block]
            pieces.append(jnp.where(core == 0, first, second))
        return jnp.concatenate(pieces, axis=1)

    def position(self):
        core = lax.axis_index("doc") % 2
        return core * self.span + lax.axis_index("ctx") % self.span

    def ring_pairs(self, shift):
        pairs = []
        for doc in range(self.doc_size):
            for ctx in range(self.ctx_size):
                place = (doc % 2) * self.span + ctx % self.span
                other = (place + shift) % self.group
                pairs.append(
                    (
                        self.flat(doc, ctx),
                        self.flat(
                            doc - doc % 2 + other // self.span,
                            ctx - ctx % self.span + other % self.span,
                        ),
                    )
                )
        return pairs

    def fetch(self, values):
        return [
            lax.ppermute(values, BOTH, self.ring_pairs(-shift)) for shift in range(1, self.group)
        ]

    def give_back(self, pieces):
        return [
            lax.ppermute(piece, BOTH, self.ring_pairs(shift))
            for shift, piece in enumerate(pieces, 1)
        ]


def to_part_order(columns, devices, shard):
    rows, hidden = columns.shape
    split = columns.reshape(rows, devices, hidden // (devices * shard), shard)
    return split.transpose(0, 2, 1, 3).reshape(rows, hidden)


def to_device_order(columns, devices, shard):
    rows, hidden = columns.shape
    split = columns.reshape(rows, hidden // (devices * shard), devices, shard)
    return split.transpose(0, 2, 1, 3).reshape(rows, hidden)


def pack_layer(devices, w_qkv, w_out, w_in, w_down, tables, gains, biases, b_in):
    shard = w_qkv.shape[0]
    down = w_down.reshape(-1, shard, w_down.shape[1])
    down = [down[part] for part in range(down.shape[0])]
    small = jnp.concatenate(
        [tables.reshape(-1, shard).T, gains.T, biases.T, b_in.reshape(-1, shard).T], axis=1
    )
    small = jnp.pad(small, ((0, 0), (0, pad_lanes(small.shape[1]) - small.shape[1])))
    return jnp.concatenate(
        [w_qkv, w_out, to_part_order(w_in, devices, shard), *down, small], axis=1
    )


def unpack_layer(packed):
    width = packed.shape[0]
    hidden = ((packed.shape[1] - 4 * width) // (2 * width)) * width
    start = 4 * width + hidden
    small = packed[:, start + hidden :]
    table_cols = 2 * BUCKETS
    rows = small[:, table_cols:].astype(F32).T
    return dict(
        qkv=packed[:, : 3 * width],
        out=packed[:, 3 * width : 4 * width],
        w_in=packed[:, 4 * width : start],
        down=[packed[:, start + at : start + at + width] for at in range(0, hidden, width)],
        tables=small[:, :table_cols],
        gains=rows[:2],
        biases=rows[2:9],
        b_in=rows[9 : 9 + hidden // width].reshape(hidden),
    )


def flips(size, bit):
    return [(index, index ^ bit) for index in range(size)]


class Scatter:
    def __init__(self, shape, order):
        self.doc_size, self.ctx_size = shape
        self.order = order
        self.bits = [1 << at for at in range(self.doc_size.bit_length() - 2, 0, -1)]
        self.value = None
        self.got = None
        self.steps = None

    def begin(self, leading, half):
        columns = half.shape[-1]
        block = half.size // (columns * leading * (self.doc_size // 2) * self.ctx_size)
        self.value = half.reshape((leading,) + (2,) * len(self.bits) + (self.ctx_size, block, columns))
        self.left = list(self.bits)
        steps = [("doc", bit) for bit in (self.bits if self.order == 0 else reversed(self.bits))]
        size = self.ctx_size // 2
        while size:
            steps.append(("ctx", size))
            size //= 2
        self.steps = steps
        self.send()

    def send(self):
        self.kept = self.got = None
        if not self.steps:
            return
        axis_name, bit = self.steps.pop(0)
        value = self.value
        if axis_name == "doc":
            axis = 1 + self.left.index(bit)
            self.left.remove(bit)
            size = self.doc_size
        else:
            axis = 1
            value = value.reshape((value.shape[0], 2, value.shape[1] // 2) + value.shape[2:])
            size = self.ctx_size
        mine = (lax.axis_index(axis_name) // bit) % 2
        self.kept = lax.dynamic_index_in_dim(value, mine, axis, keepdims=False)
        sent = lax.dynamic_index_in_dim(value, 1 - mine, axis, keepdims=False)
        self.got = lax.ppermute(sent, axis_name, flips(size, bit))

    def advance(self):
        total = self.kept.astype(F32) + self.got.astype(F32)
        self.value = total.astype(BF16)
        if not self.steps:
            self.value = total
        self.send()

    def result(self):
        value = self.value
        return value.reshape((value.shape[0],) + value.shape[-2:])


class Flight:
    def __init__(self):
        self.moving = []

    def add(self, scatter):
        self.moving.append(scatter)

    def tick(self, values):
        got = [item.got for item in self.moving]
        values, got = lax.optimization_barrier((values, got))
        for item, piece in zip(self.moving, got):
            item.got = piece
            item.advance()
        self.moving = [item for item in self.moving if item.got is not None]
        return values


def layer_forward(home, rows_in, rows_low, weights, lookups):
    width = rows_in.shape[1]
    gains, biases = weights["gains"], weights["biases"]
    qkv = (dot(rows_low, weights["qkv"], 1, 0) + biases[:3].reshape(1, -1)).astype(BF16)
    other_kv = home.fetch(qkv[:, width:])
    rel_both = dot(weights["tables"], weights["qkv"][:, : 2 * width], 0, 0).astype(BF16)
    rel_query = rel_both[:, :width].reshape(2, BUCKETS, width)
    rel_key = rel_both[:, width:].reshape(2, BUCKETS, width)
    mixed, prob = attend(qkv, other_kv, rel_key, rel_query, lookups)
    first_sum = rows_in + (dot(mixed, weights["out"], 1, 0) + biases[3])
    first_norm = norm_rows(first_sum, gains[0], biases[5])
    norm_low = first_norm.astype(BF16)
    hidden_pre = dot(norm_low, weights["w_in"], 1, 0) + weights["b_in"]
    active = exact_gelu(hidden_pre).astype(BF16)
    down_rows = biases[4]
    for part, panel in enumerate(weights["down"]):
        down_rows = down_rows + dot(active[:, part * width : (part + 1) * width], panel, 1, 0)
    second_sum = first_norm + down_rows
    result = norm_rows(second_sum, gains[1], biases[6])
    kept = dict(
        rows_low=rows_low,
        qkv=qkv,
        other_kv=other_kv,
        rel_key=rel_key,
        rel_query=rel_query,
        prob=prob,
        mixed=mixed,
        first_sum=first_sum,
        norm_low=norm_low,
        hidden_pre=hidden_pre,
        active=active,
        second_sum=second_sum,
    )
    return result, kept


class CoreSum:
    def __init__(self, home, terms):
        self.home = home
        self.terms = terms
        core = lax.axis_index("doc") % 2
        self.core = core
        sent = self.product(1 - core).astype(BF16)
        self.got = lax.ppermute(sent, "doc", flips(home.doc_size, 1))

    def product(self, core):
        total = None
        for left, right in self.terms:
            piece = dot(self.home.core_half(left, core), right, 0, 0)
            total = piece if total is None else total + piece
        return total

    def finish(self):
        return (self.product(self.core) + self.got.astype(F32)).astype(BF16)


def layer_backward(home, flight, grad_out, kept, weights, lookups):
    width = grad_out.shape[1]
    shape = (home.doc_size, home.ctx_size)
    gains, biases = weights["gains"], weights["biases"]
    rows = grad_out.shape[0]
    parts = len(weights["down"])

    _, second_pull = jax.vjp(norm_rows, kept["second_sum"], gains[1], biases[6])
    grad_second, grad_gain_two, grad_offset_two = second_pull(grad_out)
    grad_down = grad_second.astype(BF16)
    sum_down = CoreSum(home, [(kept["active"], grad_down)])
    grad_active = jnp.concatenate(
        [dot(grad_down, panel, 1, 1) for panel in weights["down"]], axis=1
    )
    _, gelu_pull = jax.vjp(exact_gelu, kept["hidden_pre"])
    grad_hidden = gelu_pull(grad_active)[0].astype(BF16)
    grad_hidden, grad_down, sum_down.got = flight.tick((grad_hidden, grad_down, sum_down.got))

    sum_in = CoreSum(home, [(kept["norm_low"], grad_hidden)])
    grad_first_norm = grad_second + dot(grad_hidden, weights["w_in"], 1, 1)
    _, first_pull = jax.vjp(norm_rows, kept["first_sum"], gains[0], biases[5])
    grad_first, grad_gain_one, grad_offset_one = first_pull(grad_first_norm)
    grad_att = grad_first.astype(BF16)
    sum_out = CoreSum(home, [(kept["mixed"], grad_att)])
    grad_mixed = dot(grad_att, weights["out"], 1, 1).astype(BF16)
    half_down = sum_down.finish()
    grad_mixed, half_down, sum_in.got, sum_out.got = flight.tick(
        (grad_mixed, half_down, sum_in.got, sum_out.got)
    )
    scatter_down, scatter_in = Scatter(shape, 0), Scatter(shape, 1)
    scatter_down.begin(parts, half_down)
    half_in = jnp.concatenate([sum_in.finish(), sum_out.finish()], axis=1)
    scatter_in.begin(1, half_in)
    flight.add(scatter_down)
    flight.add(scatter_in)

    pairs = width // PAIR
    count = pairs // 2
    found = []
    moved = []
    for first in range(0, pairs, count):
        grad_query, grad_kv, grad_rel = attend_back(
            kept["qkv"],
            kept["other_kv"],
            grad_mixed,
            kept["prob"],
            kept["rel_key"],
            kept["rel_query"],
            lookups,
            first,
            count,
        )
        grad_query, grad_kv, grad_rel, grad_mixed = flight.tick(
            (grad_query, grad_kv, grad_rel, grad_mixed)
        )
        moved.append(home.give_back([grad_kv[chunk] for chunk in range(1, grad_kv.shape[0])]))
        found.append((grad_query, grad_kv[0], grad_rel))

    own = []
    for (_, grad_kv, _), pieces in zip(found, moved):
        total = grad_kv.astype(F32)
        for piece in pieces:
            total = total + piece.astype(F32)
        own.append(total.astype(BF16))
    grad_qkv = jnp.concatenate(
        [item[0] for item in found] + [item[0] for item in own] + [item[1] for item in own], axis=1
    )
    rel_both = [jnp.concatenate([item[2][kind] for item in found], axis=1) for kind in range(2)]
    tables = weights["tables"]
    grad_tables = dot(weights["qkv"][:, :width], rel_both[0], 1, 1) + dot(
        weights["qkv"][:, width : 2 * width], rel_both[1], 1, 1
    )
    bias_sums = jnp.sum(grad_qkv.astype(F32), axis=0).reshape(3, width)
    small = jnp.concatenate(
        [
            grad_gain_one[None],
            grad_gain_two[None],
            bias_sums,
            jnp.sum(grad_att.astype(F32), axis=0)[None],
            jnp.sum(grad_down.astype(F32), axis=0)[None],
            grad_offset_one[None],
            grad_offset_two[None],
            jnp.sum(grad_hidden.astype(F32), axis=0).reshape(parts, width),
        ],
        axis=0,
    ).T
    total_cols = 2 * BUCKETS + small.shape[1]
    small = jnp.concatenate([grad_tables, small], axis=1)
    small = jnp.pad(small, ((0, 0), (0, pad_lanes(total_cols) - total_cols)))
    split = small.astype(BF16).reshape(home.doc_size // 2, 2, -1, small.shape[1])
    core = lax.axis_index("doc") % 2
    small_sent = lax.dynamic_index_in_dim(split, 1 - core, 1, keepdims=False)
    small_kept = lax.dynamic_index_in_dim(split, core, 1, keepdims=False)
    small_got = lax.ppermute(small_sent, "doc", flips(home.doc_size, 1))
    rows_turned = kept["rows_low"]
    sum_qk = CoreSum(
        home,
        [
            (rows_turned, grad_qkv[:, : 2 * width]),
            (tables.T, jnp.concatenate(rel_both, axis=1)),
        ],
    )
    sum_v = CoreSum(home, [(rows_turned, grad_qkv[:, 2 * width :])])
    grad_rows = grad_first + dot(grad_qkv, weights["qkv"], 1, 1)
    grad_rows, sum_qk.got, sum_v.got, small_got = flight.tick(
        (grad_rows, sum_qk.got, sum_v.got, small_got)
    )
    small_half = (small_kept.astype(F32) + small_got.astype(F32)).astype(BF16)
    half_qk, half_v = sum_qk.finish(), sum_v.finish()
    cut = 7 * width // 4
    scatter_first, scatter_rest = Scatter(shape, 0), Scatter(shape, 1)
    scatter_first.begin(1, half_qk[:, :cut])
    scatter_rest.begin(
        1,
        jnp.concatenate(
            [half_qk[:, cut:], half_v, small_half.reshape(half_qk.shape[0], -1)], axis=1
        ),
    )
    flight.add(scatter_first)
    flight.add(scatter_rest)
    return grad_rows, (scatter_down, scatter_in, scatter_first, scatter_rest)


def collect(home, scatters, width, hidden):
    scatter_down, scatter_in, scatter_first, scatter_rest = scatters
    devices = home.doc_size * home.ctx_size
    down = scatter_down.result()
    shard = down.shape[1]
    down = down.reshape(-1, width)
    both = scatter_in.result()[0]
    grad_in = to_device_order(both[:, :hidden], devices, shard)
    grad_out = both[:, hidden:]
    rest = scatter_rest.result()[0]
    first = scatter_first.result()[0]
    qkv_left = 3 * width - first.shape[1]
    qkv = jnp.concatenate([first, rest[:, :qkv_left]], axis=1)
    small = rest[:, qkv_left:]
    table_cols = 2 * BUCKETS
    tables = small[:, :table_cols].T.reshape(2, BUCKETS, shard)
    rows = small[:, table_cols:].T
    gains, biases = rows[:2], rows[2:9]
    b_in = rows[9 : 9 + hidden // width].reshape(-1)
    return qkv, grad_out, grad_in, down, tables, gains, biases, b_in


def body(
    mesh_shape,
    layer_input,
    text_count,
    coords,
    w_qkv,
    w_out,
    w_in,
    w_down,
    rel_tables,
    ln_gains,
    biases,
    b_in,
    cotangent,
):
    doc_size, ctx_size = mesh_shape["doc"], mesh_shape["ctx"]
    device_count = doc_size * ctx_size
    local_docs, block_rows, width = layer_input.shape
    layer_count = w_qkv.shape[0]
    hidden = w_in.shape[2]
    home = Home(mesh_shape, local_docs, block_rows, width)

    packed = [
        pack_layer(
            device_count,
            w_qkv[layer],
            w_out[layer],
            w_in[layer],
            w_down[layer],
            rel_tables[layer],
            ln_gains[layer],
            biases[layer],
            b_in[layer],
        )
        for layer in range(layer_count)
    ]

    core = lax.axis_index("doc") % 2
    doc_here = lax.axis_index("ctx") // home.span
    facts = jnp.concatenate([coords.reshape(local_docs, -1), text_count[:, None]], axis=1)
    other_facts = lax.ppermute(facts, "doc", flips(doc_size, 1))
    mine = jnp.where(
        doc_here // local_docs == core,
        lax.dynamic_index_in_dim(facts, doc_here % local_docs, 0, keepdims=False),
        lax.dynamic_index_in_dim(other_facts, doc_here % local_docs, 0, keepdims=False),
    )
    place = (jnp.arange(home.seq, dtype=jnp.int32) + home.position() * home.rows) % home.seq

    def turned(values):
        twice = jnp.concatenate([values, values])
        return lax.dynamic_slice_in_dim(twice, home.position() * home.rows, home.seq)

    lookups = make_lookups(
        turned(mine[: home.seq]),
        turned(mine[home.seq : 2 * home.seq]),
        mine[2 * home.seq],
        place,
        home.rows,
    )

    rows_low = home.to_home(layer_input)
    current = rows_low.astype(F32)
    all_weights = []
    gathered = None
    for layer in range(layer_count):
        shard = packed[layer]
        if gathered is not None:
            shard, gathered = lax.optimization_barrier((shard, gathered))
            all_weights[-1] = unpack_layer(gathered)
        gathered = lax.all_gather(shard, BOTH, axis=0, tiled=True)
        all_weights.append(unpack_layer(gathered))
    kept_all = []
    outputs = []
    for layer in range(layer_count):
        current, kept = layer_forward(home, current, rows_low, all_weights[layer], lookups)
        rows_low = current.astype(BF16)
        outputs.append(home.from_home(rows_low).astype(F32))
        kept_all.append(kept)
    grad_rows = home.to_home(cotangent).astype(F32)
    scatters = [None] * layer_count
    flight = Flight()
    for layer in reversed(range(layer_count)):
        grad_rows, scatters[layer] = layer_backward(
            home, flight, grad_rows, kept_all[layer], all_weights[layer], lookups
        )
    grad_input = home.from_home(grad_rows.astype(BF16)).astype(F32)
    while flight.moving:
        flight.tick(())
    totals = [collect(home, item, width, hidden) for item in scatters]

    def stack(member):
        return jnp.stack([totals[layer][member] for layer in range(layer_count)])

    return (outputs[0], outputs[-1], grad_input) + tuple(stack(member) for member in range(8))


def solution(mesh):
    placed = (
        P("doc", "ctx", None),
        P("doc"),
        P("doc", None, None),
        P(None, BOTH, None),
        P(None, BOTH, None),
        P(None, BOTH, None),
        P(None, BOTH, None),
        P(None, None, None, BOTH),
        P(None, None, BOTH),
        P(None, None, BOTH),
        P(None, BOTH),
        P("doc", "ctx", None),
    )
    return jax.shard_map(
        functools.partial(body, dict(mesh.shape)),
        mesh=mesh,
        in_specs=placed,
        out_specs=(
            P("doc", "ctx", None),
            P("doc", "ctx", None),
            P("doc", "ctx", None),
            P(None, BOTH, None),
            P(None, BOTH, None),
            P(None, BOTH, None),
            P(None, BOTH, None),
            P(None, None, None, BOTH),
            P(None, None, BOTH),
            P(None, None, BOTH),
            P(None, BOTH),
        ),
        check_vma=False,
    )
```

time: 1840 us -> 1100 us (0.60)
  Pallas kernels: 771 us -> 269 us
  waiting for transfers between devices: 441 us -> 247 us
  local copies, waits for them, and re-layouts: 199 us -> 130 us
  starting transfers between devices: 119 us -> 82.3 us
  matrix products: 186 us -> 215 us
  other arithmetic: 102 us -> 129 us
    pallas_call x2 -> x4, Pallas kernels: 515 us -> 191 us  [attend_back(): pl.pallas_call(functools.partial(attend_back_kernel, chunks), grid=(count...]
    ppermute x71 -> x45, waiting for transfers between devices: 278 us -> 39.8 us  [the longest x32 39.8 us: send(): self.got = lax.ppermute(sent, axis_name, flips(size, bit))]
    pallas_call x2, Pallas kernels: 255 us -> 78.3 us  [attend(): pl.pallas_call(functools.partial(attend_kernel, chunks), grid=(pairs,), i...]
    ppermute x71 -> x45, starting transfers between devices: 77.5 us -> 41.1 us  [the longest x32 34.9 us: send(): self.got = lax.ppermute(sent, axis_name, flips(size, bit))]
    convert_element_type x18 -> x0, local copies, waits for them, and re-layouts: 33 us -> none  [halve(): return (kept, send(sent.astype(BF16)))]
    dot_general x34 -> x58, matrix products: 186 us -> 215 us  [dot(): lax.dot_general(left, right, (((left_axis,), (right_axis,)), ((), ())), p...]
    all_gather x2, waiting for transfers between devices: 161 us -> 185 us  [body(): gathered = lax.all_gather(shard, BOTH, axis=0, tiled=True)]
    ppermute x6, waiting for transfers between devices: 1.5 us -> 22.1 us  [from_home(): pieces.append(lax.ppermute(piece, BOTH, back))]
  transfers between devices with their start and end apart: 87 -> 63, of which waited for: 44 -> 11; matrix products, arithmetic and copies ran while one was open for 21% -> 37% of each run, Pallas kernels for 21% -> 25%
where the time goes in v2:
time: 1100 us; the launch traced here: 1090 us
  Pallas kernels  269 us (24%)
  waiting for transfers between devices  247 us (22%)
  matrix products  215 us (20%)
  local copies, waits for them, and re-layouts  130 us (12%)
  other arithmetic  129 us (12%)
  starting transfers between devices  82.3 us (7%)
  between operations  18.4 us (2%)
    dot_general x58, matrix products, dot(): lax.dot_general(left, right, (((left_axis,), (right_axis,)), ((), ())), p...  215 us
    pallas_call x4, Pallas kernels, attend_back(): pl.pallas_call(functools.partial(attend_back_kernel, chunks), grid=(count...  191 us
    all_gather x2, waiting for transfers between devices, body(): gathered = lax.all_gather(shard, BOTH, axis=0, tiled=True)  185 us
    pallas_call x2, Pallas kernels, attend(): pl.pallas_call(functools.partial(attend_kernel, chunks), grid=(pairs,), i...  78.3 us
    ppermute x32, waiting for transfers between devices, send(): self.got = lax.ppermute(sent, axis_name, flips(size, bit))  39.8 us
    unnamed x470, local copies, waits for them, and re-layouts  36.2 us
    ppermute x32, starting transfers between devices, send(): self.got = lax.ppermute(sent, axis_name, flips(size, bit))  34.9 us
    convert_element_type x24, other arithmetic, advance(): self.value = total.astype(BF16)  30 us
  transfers between devices with their start and end apart: 63, of which 11 were waited for; matrix products, arithmetic and copies ran while one was open for 37% of the time, Pallas kernels for 25%

profile of v2, /device:TPU:0, one launch (start us, length us, event | category | flops | bytes accessed | tf_op | source)
XLA Modules:
  0.0 1090.7 jit_solution(4648420337379545011)
XLA Ops:
  24.6 160.1 %all-gather.3.cloned.1.call-done = bf16[1024,12672]{1,0:T(8,128)(2,1)} async-done(((bf16[32,12672]{1,0:T(8,128)(2,1)}), bf16[1024,12672]{1,0:T(8,128)(2,1)}) %all-gather.3.cloned.1.call-update) | async-done | bytes 25952272 | tf_op jit(solution)/shard_map/all_gather | solution.py:930
  214.3 5.0 fusion.51.q_ref.refs_0_.refs_2_
  220.6 20.3 %collective-permute-start.2 = (bf16[288,2048]{1,0:T(8,128)(2,1)}, bf16[288,2048]{1,0:T(8,128)(2,1)}, u32[]{:S(2)}, u32[]{:S(2)}) collective-permute-start(bf16[288,2048]{1,0:T(8,128)(2,1)} %slice.1268), channel_id=1, source_target_pairs={{0,4},{1,5},{2,6},{3,7},{4,0},{5,1},{6,2},{7,3},{8,12},{9,13},{10,... | collective-permute-start | bytes 3538952 | tf_op jit(solution)/shard_map/ppermute | solution.py:532
  243.4 3.9 slice_reduce_fusion.7
  249.3 3.6 fusion.56
  254.6 39.1 %attend.2 = (bf16[288,1024]{1,0:T(8,128)(2,1)S(1)}, bf16[16,288,640]{2,1,0:T(8,128)(2,1)S(1)}) custom-call(bf16[288,3072]{1,0:T(8,128)(2,1)S(1)} %fusion.51.q_ref.refs_0_.refs_2_, bf16[288,3072]{1,0:T(8,128)(2,1)S(1)} %fusion.51.q_ref.refs_0_.refs_2_, bf16[288,2048]{1,0:T(8,128)(2,1)} %collective-permute-done.2.refs_1_.refs_3_, ...), custom_call_target="tpu_custom_call" | custom-call | flops 3397386240 | bytes 8257536 | tf_op jit(solution)/shard_map/attend/pallas_call | solution.py:167
  293.8 4.1 fusion.442
  298.6 16.7 %multiply_convert_fusion.1 = (bf16[288,4096]{1,0:T(8,128)(2,1)S(1)}, f32[288,4096]{1,0:T(8,128)}, f32[288,4096]{1,0:T(8,128)}) fusion(f32[4096]{0:T(1024)S(1)} %bitcast.515, bf16[288,1024]{1,0:T(8,128)(2,1)S(1)} %fusion.201, bf16[1024,12672]{1,0:T(8,128)(2,1)} %all-gather.3.cloned.1.call-done), kind=kOutput, calls=%fused_computation.51 | convolution fusion | flops 2493775872 | bytes 20791296 | tf_op jit(solution)/shard_map/dot_general | solution.py:43
  315.3 3.2 fusion.102
  327.5 4.0 collective-permute-start.4
  331.5 3.9 collective-permute-start.5
  340.4 25.3 %all-gather.5.cloned.1.call-done = bf16[1024,12672]{1,0:T(8,128)(2,1)} async-done(((bf16[32,12672]{1,0:T(8,128)(2,1)}), bf16[1024,12672]{1,0:T(8,128)(2,1)}) %all-gather.5.cloned.1.call-update) | async-done | bytes 25952272 | tf_op jit(solution)/shard_map/all_gather | solution.py:930
  368.5 4.9 fusion.48.q_ref.refs_0_.refs_2_
  381.7 4.2 slice_reduce_fusion.1
  385.8 3.6 fusion.59
  391.2 39.2 %attend.3 = (bf16[288,1024]{1,0:T(8,128)(2,1)S(1)}, bf16[16,288,640]{2,1,0:T(8,128)(2,1)S(1)}) custom-call(bf16[288,3072]{1,0:T(8,128)(2,1)S(1)} %fusion.48.q_ref.refs_0_.refs_2_, bf16[288,3072]{1,0:T(8,128)(2,1)S(1)} %fusion.48.q_ref.refs_0_.refs_2_, bf16[288,2048]{1,0:T(8,128)(2,1)} %collective-permute-done.6.refs_1_.refs_3_, ...), custom_call_target="tpu_custom_call" | custom-call | flops 3397386240 | bytes 8257536 | tf_op jit(solution)/shard_map/attend/pallas_call | solution.py:167
  430.5 4.1 fusion.444
  435.2 15.2 %multiply_convert_fusion = (bf16[288,4096]{1,0:T(8,128)(2,1)S(1)}, f32[288,4096]{1,0:T(8,128)S(1)}, f32[288,4096]{1,0:T(8,128)S(1)}) fusion(f32[4096]{0:T(1024)S(1)} %bitcast.516, bf16[288,1024]{1,0:T(8,128)(2,1)S(1)} %fusion.203, bf16[1024,12672]{1,0:T(8,128)(2,1)} %all-gather.5.cloned.1.call-done), kind=kOutput, calls=%fused_computation.38 | convolution fusion | flops 2493775872 | bytes 20791296 | tf_op jit(solution)/shard_map/dot_general | solution.py:43
  462.9 4.4 convolution_convert_fusion.3
  488.6 4.5 convolution_convert_fusion.1
  498.3 6.2 multiply_reduce_fusion.4
  507.1 3.2 fusion.182.refs_4_
  510.4 3.8 add_convert_fusion.3
  514.2 8.9 add_convert_fusion.2
  543.4 6.8 collective-permute-done.7
  554.8 47.7 %attend_back.4 = (bf16[288,512]{1,0:T(8,128)(2,1)}, bf16[2,2,288,512]{3,2,1,0:T(8,128)(2,1)}, bf16[2,256,512]{2,1,0:T(8,128)(2,1)}) custom-call(bf16[288,3072]{1,0:T(8,128)(2,1)} %copy-done.2, bf16[288,3072]{1,0:T(8,128)(2,1)} %copy-done.2, bf16[288,2048]{1,0:T(8,128)(2,1)} %collective-permute-done.6.refs_1_.refs_3_, bf16[288,3072]{1,0:T(8,128)(2,1)} %copy-done.2, ...), custom_call_target="tpu_custom_call" | custom-call | flops 6794772480 | bytes 6488064 | tf_op jit(solution)/shard_map/attend_back/pallas_call | solution.py:340
  612.3 3.9 collective-permute-start.18
  616.3 48.1 %attend_back.5 = (bf16[288,512]{1,0:T(8,128)(2,1)}, bf16[2,2,288,512]{3,2,1,0:T(8,128)(2,1)}, bf16[2,256,512]{2,1,0:T(8,128)(2,1)}) custom-call(bf16[288,3072]{1,0:T(8,128)(2,1)} %copy-done.2, bf16[288,3072]{1,0:T(8,128)(2,1)} %copy-done.2, bf16[288,2048]{1,0:T(8,128)(2,1)} %collective-permute-done.6.refs_1_.refs_3_, bf16[288,3072]{1,0:T(8,128)(2,1)} %copy-done.2, ...), custom_call_target="tpu_custom_call" | custom-call | flops 6794772480 | bytes 6488064 | tf_op jit(solution)/shard_map/attend_back/pallas_call | solution.py:340
  677.5 3.2 fusion.187
  700.9 6.4 fusion.176
  711.0 11.1 %collective-permute-done.23 = bf16[4,2,32,1024]{3,2,0,1:T(8,128)(2,1)} collective-permute-done((bf16[4,2,32,1024]{3,2,0,1:T(8,128)(2,1)}, bf16[4,2,32,1024]{3,2,0,1:T(8,128)(2,1)}, u32[]{:S(2)}, u32[]{:S(2)}) %collective-permute-start.23) | collective-permute-done | bytes 524320 | tf_op jit(solution)/shard_map/ppermute | solution.py:629
  734.4 5.6 convolution_convert_fusion.2
  758.3 3.6 fusion.447
  769.3 4.5 convolution_convert_fusion
  773.8 5.8 multiply_reduce_fusion.1
  783.7 3.8 add_convert_fusion.1
  787.6 5.0 fusion.179.refs_4_
  792.7 4.6 add_convert_fusion
  819.2 4.7 stack_reshape.19
  830.1 47.8 %attend_back.6 = (bf16[288,512]{1,0:T(8,128)(2,1)}, bf16[2,2,288,512]{3,2,1,0:T(8,128)(2,1)}, bf16[2,256,512]{2,1,0:T(8,128)(2,1)}) custom-call(bf16[288,3072]{1,0:T(8,128)(2,1)} %copy-done.1, bf16[288,3072]{1,0:T(8,128)(2,1)} %copy-done.1, bf16[288,2048]{1,0:T(8,128)(2,1)} %collective-permute-done.2.refs_1_.refs_3_, bf16[288,3072]{1,0:T(8,128)(2,1)} %copy-done.1, ...), custom_call_target="tpu_custom_call" | custom-call | flops 6794772480 | bytes 6488064 | tf_op jit(solution)/shard_map/attend_back/pallas_call | solution.py:340
  893.2 47.6 %attend_back.7 = (bf16[288,512]{1,0:T(8,128)(2,1)}, bf16[2,2,288,512]{3,2,1,0:T(8,128)(2,1)}, bf16[2,256,512]{2,1,0:T(8,128)(2,1)}) custom-call(bf16[288,3072]{1,0:T(8,128)(2,1)} %copy-done.1, bf16[288,3072]{1,0:T(8,128)(2,1)} %copy-done.1, bf16[288,2048]{1,0:T(8,128)(2,1)} %collective-permute-done.2.refs_1_.refs_3_, bf16[288,3072]{1,0:T(8,128)(2,1)} %copy-done.1, ...), custom_call_target="tpu_custom_call" | custom-call | flops 6794772480 | bytes 6488064 | tf_op jit(solution)/shard_map/attend_back/pallas_call | solution.py:340
  955.7 3.2 fusion.190
  985.0 6.4 fusion.173
  994.8 6.3 collective-permute-done.47
  1015.9 15.2 %collective-permute-done.49 = bf16[144,1024]{1,0:T(8,128)(2,1)S(1)} collective-permute-done((bf16[144,1024]{1,0:T(8,128)(2,1)S(1)}, bf16[144,1024]{1,0:T(8,128)(2,1)S(1)}, u32[]{:S(2)}, u32[]{:S(2)}) %collective-permute-start.49) | collective-permute-done | bytes 294944 | tf_op jit(solution)/shard_map/ppermute | solution.py:494
  1032.3 5.2 collective-permute-done.51
  1047.5 3.7 stack_reshape.18
  1059.6 10.6 collective-permute-done.58
  (958 shorter events, 370.0 us)
Async XLA Ops:
  7.2 177.5 %all-gather.3.cloned.1.call-start = ((), (), s32[]{:S(2)}) async-start(), calls=%async_computation | async-start | bytes 26763264 | tf_op jit(solution)/shard_map/all_gather | solution.py:930
  23.4 342.3 %all-gather.5.cloned.1.call-start = ((), (), s32[]{:S(2)}) async-start(), calls=%async_computation.1 | async-start | bytes 26763264 | tf_op jit(solution)/shard_map/all_gather | solution.py:930
  184.8 24.2 %collective-permute-start = (bf16[144,1024]{1,0:T(8,128)(2,1)S(1)}, bf16[144,1024]{1,0:T(8,128)(2,1)S(1)}, u32[]{:S(2)}, u32[]{:S(2)}) collective-permute-start(bf16[144,1024]{1,0:T(8,128)(2,1)S(1)} %get-tuple-element.427), channel_id=1, source_target_pairs={{0,1},{1,0},{2,5},{3,4},{4,3},{5,2},{6,7},{7,6},{8,9},{9,8},{10,13... | collective-permute-start | bytes 884744 | tf_op jit(solution)/shard_map/ppermute | solution.py:480
  184.8 24.1 %collective-permute-start.1 = (bf16[144,1024]{1,0:T(8,128)(2,1)S(1)}, bf16[144,1024]{1,0:T(8,128)(2,1)S(1)}, u32[]{:S(2)}, u32[]{:S(2)}) collective-permute-start(bf16[144,1024]{1,0:T(8,128)(2,1)S(1)} %get-tuple-element.428), channel_id=1, source_target_pairs={{0,0},{1,1},{2,4},{3,5},{4,2},{5,3},{6,6},{7,7},{8,8},{9,9},{10,12... | collective-permute-start | bytes 884744 | tf_op jit(solution)/shard_map/ppermute | solution.py:480
  189.4 17.9 %collective-permute-start.10 = (bf16[144,1024]{1,0:T(8,128)(2,1)}, bf16[144,1024]{1,0:T(8,128)(2,1)S(1)}, u32[]{:S(2)}, u32[]{:S(2)}) collective-permute-start(bf16[144,1024]{1,0:T(8,128)(2,1)} %get-tuple-element.416), channel_id=1, source_target_pairs={{0,0},{1,1},{2,4},{3,5},{4,2},{5,3},{6,6},{7,7},{8,8},{9,9},{10,12... | collective-permute-start | bytes 884744 | tf_op jit(solution)/shard_map/ppermute | solution.py:480
  220.6 32.5 %collective-permute-start.2 = (bf16[288,2048]{1,0:T(8,128)(2,1)}, bf16[288,2048]{1,0:T(8,128)(2,1)}, u32[]{:S(2)}, u32[]{:S(2)}) collective-permute-start(bf16[288,2048]{1,0:T(8,128)(2,1)} %slice.1268), channel_id=1, source_target_pairs={{0,4},{1,5},{2,6},{3,7},{4,0},{5,1},{6,2},{7,3},{8,12},{9,13},{10,... | collective-permute-start | bytes 3538952 | tf_op jit(solution)/shard_map/ppermute | solution.py:532
  327.5 210.4 %collective-permute-start.4 = (bf16[144,1024]{1,0:T(8,128)(2,1)}, bf16[144,1024]{1,0:T(8,128)(2,1)}, u32[]{:S(2)}, u32[]{:S(2)}) collective-permute-start(bf16[144,1024]{1,0:T(8,128)(2,1)} %get-tuple-element.423), channel_id=1, source_target_pairs={{1,0},{0,1},{5,2},{4,3},{3,4},{2,5},{7,6},{6,7},{9,8},{8,9},{13,10... | collective-permute-start | bytes 884744 | tf_op jit(solution)/shard_map/ppermute | solution.py:494
  331.5 206.4 %collective-permute-start.5 = (bf16[144,1024]{1,0:T(8,128)(2,1)}, bf16[144,1024]{1,0:T(8,128)(2,1)}, u32[]{:S(2)}, u32[]{:S(2)}) collective-permute-start(bf16[144,1024]{1,0:T(8,128)(2,1)} %get-tuple-element.424), channel_id=1, source_target_pairs={{0,0},{1,1},{4,2},{5,3},{2,4},{3,5},{6,6},{7,7},{8,8},{9,9},{12,10... | collective-permute-start | bytes 884744 | tf_op jit(solution)/shard_map/ppermute | solution.py:494
  467.3 21.3 %collective-permute-start.11 = (bf16[2048,1024]{1,0:T(8,128)(2,1)}, bf16[2048,1024]{1,0:T(8,128)(2,1)S(1)}, u32[]{:S(2)}, u32[]{:S(2)}) collective-permute-start(bf16[2048,1024]{1,0:T(8,128)(2,1)} %convolution_convert_fusion.3), channel_id=1, source_target_pairs={{0,4},{4,0},{8,12},{12,8},{16,20},{20,16},{24,28},{28,24},{1,5},{5... | collective-permute-start | bytes 12582920 | tf_op jit(solution)/shard_map/ppermute | solution.py:703
  493.1 21.1 %collective-permute-start.12 = (bf16[512,4096]{1,0:T(8,128)(2,1)}, bf16[512,4096]{1,0:T(8,128)(2,1)}, u32[]{:S(2)}, u32[]{:S(2)}) collective-permute-start(bf16[512,4096]{1,0:T(8,128)(2,1)} %convolution_convert_fusion.1), channel_id=1, source_target_pairs={{0,4},{4,0},{8,12},{12,8},{16,20},{20,16},{24,28},{28,24},{1,5},{5... | collective-permute-start | bytes 12582920 | tf_op jit(solution)/shard_map/ppermute | solution.py:703
  530.9 71.6 %collective-permute-start.15 = (bf16[1,2,4,32,5120]{4,3,2,1,0:T(8,128)(2,1)}, bf16[1,2,4,32,5120]{4,3,2,1,0:T(8,128)(2,1)}, u32[]{:S(2)}, u32[]{:S(2)}) collective-permute-start(bf16[1,2,4,32,5120]{4,3,2,1,0:T(8,128)(2,1)} %dynamic-slice_bitcast_fusion.1), channel_id=1, source_target_pairs={{0,8},{4,12},{8,0},{12,4},{16,24},{20,28},{24,16},{28,20},{1,9},{5... | collective-permute-start | bytes 7864328 | tf_op jit(solution)/shard_map/ppermute | solution.py:629
  535.5 67.0 %collective-permute-start.14 = (bf16[4,2,4,32,1024]{4,3,2,1,0:T(8,128)(2,1)}, bf16[4,2,4,32,1024]{4,3,2,1,0:T(8,128)(2,1)}, u32[]{:S(2)}, u32[]{:S(2)}) collective-permute-start(bf16[4,2,4,32,1024]{4,3,2,1,0:T(8,128)(2,1)} %dynamic-slice_bitcast_fusion.3), channel_id=1, source_target_pairs={{0,16},{4,20},{8,24},{12,28},{16,0},{20,4},{24,8},{28,12},{1,17},{... | collective-permute-start | bytes 6291464 | tf_op jit(solution)/shard_map/ppermute | solution.py:629
  605.6 60.9 %collective-permute-start.17 = (bf16[1,4,32,5120]{3,2,1,0:T(8,128)(2,1)S(1)}, bf16[1,4,32,5120]{3,2,1,0:T(8,128)(2,1)S(1)}, u32[]{:S(2)}, u32[]{:S(2)}) collective-permute-start(bf16[1,4,32,5120]{3,2,1,0:T(8,128)(2,1)S(1)} %dynamic-slice_bitcast_fusion.5), channel_id=1, source_target_pairs={{0,16},{4,20},{8,24},{12,28},{16,0},{20,4},{24,8},{28,12},{1,17},{... | collective-permute-start | bytes 3932168 | tf_op jit(solution)/shard_map/ppermute | solution.py:629
  610.6 55.9 %collective-permute-start.16 = (bf16[4,4,32,1024]{3,2,1,0:T(8,128)(2,1)}, bf16[4,4,32,1024]{3,2,1,0:T(8,128)(2,1)}, u32[]{:S(2)}, u32[]{:S(2)}) collective-permute-start(bf16[4,4,32,1024]{3,2,1,0:T(8,128)(2,1)} %dynamic-slice_bitcast_fusion.7), channel_id=1, source_target_pairs={{0,8},{4,12},{8,0},{12,4},{16,24},{20,28},{24,16},{28,20},{1,9},{5... | collective-permute-start | bytes 3145736 | tf_op jit(solution)/shard_map/ppermute | solution.py:629
  612.3 52.0 %collective-permute-start.18 = (bf16[2,288,512]{2,1,0:T(8,128)(2,1)}, bf16[2,288,512]{2,1,0:T(8,128)(2,1)S(1)}, u32[]{:S(2)}, u32[]{:S(2)}) collective-permute-start(bf16[2,288,512]{2,1,0:T(8,128)(2,1)} %slice_bitcast_fusion.3), channel_id=1, source_target_pairs={{0,4},{1,5},{2,6},{3,7},{4,0},{5,1},{6,2},{7,3},{8,12},{9,13},{10,... | collective-permute-start | bytes 1769480 | tf_op jit(solution)/shard_map/ppermute | solution.py:537
  667.8 54.4 %collective-permute-start.24 = (bf16[1,2,32,5120]{3,2,1,0:T(8,128)(2,1)}, bf16[1,2,32,5120]{3,2,1,0:T(8,128)(2,1)}, u32[]{:S(2)}, u32[]{:S(2)}) collective-permute-start(bf16[1,2,32,5120]{3,2,1,0:T(8,128)(2,1)} %dynamic-slice_bitcast_fusion.13), channel_id=1, source_target_pairs={{0,2},{1,3},{2,0},{3,1},{4,6},{5,7},{6,4},{7,5},{8,10},{9,11},{10,... | collective-permute-start | bytes 1966088 | tf_op jit(solution)/shard_map/ppermute | solution.py:629
  671.3 50.8 %collective-permute-start.23 = (bf16[4,2,32,1024]{3,2,0,1:T(8,128)(2,1)}, bf16[4,2,32,1024]{3,2,0,1:T(8,128)(2,1)}, u32[]{:S(2)}, u32[]{:S(2)}) collective-permute-start(bf16[4,2,32,1024]{3,2,0,1:T(8,128)(2,1)} %bitcast.428), channel_id=1, source_target_pairs={{0,2},{1,3},{2,0},{3,1},{4,6},{5,7},{6,4},{7,5},{8,10},{9,11},{10,... | collective-permute-start | bytes 1572872 | tf_op jit(solution)/shard_map/ppermute | solution.py:629
  684.5 37.7 %collective-permute-start.20 = (bf16[512,2048]{1,0:T(8,128)(2,1)}, bf16[512,2048]{1,0:T(8,128)(2,1)}, u32[]{:S(2)}, u32[]{:S(2)}) collective-permute-start(bf16[512,2048]{1,0:T(8,128)(2,1)} %add_convert_fusion.9), channel_id=1, source_target_pairs={{0,4},{4,0},{8,12},{12,8},{16,20},{20,16},{24,28},{28,24},{1,5},{5... | collective-permute-start | bytes 6291464 | tf_op jit(solution)/shard_map/ppermute | solution.py:703
  694.7 27.5 %collective-permute-start.21 = (bf16[512,1024]{1,0:T(8,128)(2,1)}, bf16[512,1024]{1,0:T(8,128)(2,1)}, u32[]{:S(2)}, u32[]{:S(2)}) collective-permute-start(bf16[512,1024]{1,0:T(8,128)(2,1)} %convolution_convert_fusion.6), channel_id=1, source_target_pairs={{0,4},{4,0},{8,12},{12,8},{16,20},{20,16},{24,28},{28,24},{1,5},{5... | collective-permute-start | bytes 3145736 | tf_op jit(solution)/shard_map/ppermute | solution.py:703
  700.4 21.8 %collective-permute-start.22 = (bf16[4,128,384]{2,1,0:T(8,128)(2,1)}, bf16[4,128,384]{2,1,0:T(8,128)(2,1)}, u32[]{:S(2)}, u32[]{:S(2)}) collective-permute-start(bf16[4,128,384]{2,1,0:T(8,128)(2,1)} %bitcast.498), channel_id=1, source_target_pairs={{0,4},{4,0},{8,12},{12,8},{16,20},{20,16},{24,28},{28,24},{1,5},{5... | collective-permute-start | bytes 1179656 | tf_op jit(solution)/shard_map/ppermute | solution.py:809
  730.3 31.7 %collective-permute-start.29 = (bf16[1,2,4,32,1664]{4,3,2,1,0:T(8,128)(2,1)}, bf16[1,2,4,32,1664]{4,3,2,1,0:T(8,128)(2,1)}, u32[]{:S(2)}, u32[]{:S(2)}) collective-permute-start(bf16[1,2,4,32,1664]{4,3,2,1,0:T(8,128)(2,1)} %dynamic-slice_bitcast_fusion.11), channel_id=1, source_target_pairs={{0,8},{4,12},{8,0},{12,4},{16,24},{20,28},{24,16},{28,20},{1,9},{5... | collective-permute-start | bytes 2555912 | tf_op jit(solution)/shard_map/ppermute | solution.py:629
  732.2 29.8 %collective-permute-start.28 = (bf16[1,2,4,32,1792]{4,3,2,1,0:T(8,128)(2,1)}, bf16[1,2,4,32,1792]{4,3,2,1,0:T(8,128)(2,1)}, u32[]{:S(2)}, u32[]{:S(2)}) collective-permute-start(bf16[1,2,4,32,1792]{4,3,2,1,0:T(8,128)(2,1)} %dynamic-slice_bitcast_fusion.9), channel_id=1, source_target_pairs={{0,16},{4,20},{8,24},{12,28},{16,0},{20,4},{24,8},{28,12},{1,17},{... | collective-permute-start | bytes 2752520 | tf_op jit(solution)/shard_map/ppermute | solution.py:629
  740.0 22.0 %collective-permute-start.25 = (bf16[2048,1024]{1,0:T(8,128)(2,1)}, bf16[2048,1024]{1,0:T(8,128)(2,1)S(1)}, u32[]{:S(2)}, u32[]{:S(2)}) collective-permute-start(bf16[2048,1024]{1,0:T(8,128)(2,1)} %convolution_convert_fusion.2), channel_id=1, source_target_pairs={{0,4},{4,0},{8,12},{12,8},{16,20},{20,16},{24,28},{28,24},{1,5},{5... | collective-permute-start | bytes 12582920 | tf_op jit(solution)/shard_map/ppermute | solution.py:703
  741.4 20.6 %collective-permute-start.27 = (bf16[1,1,32,5120]{3,2,1,0:T(8,128)(2,1)S(1)}, bf16[1,1,32,5120]{3,2,1,0:T(8,128)(2,1)S(1)}, u32[]{:S(2)}, u32[]{:S(2)}) collective-permute-start(bf16[1,1,32,5120]{3,2,1,0:T(8,128)(2,1)S(1)} %constant_dynamic-slice_fusion.12), channel_id=1, source_target_pairs={{0,1},{1,0},{2,3},{3,2},{4,5},{5,4},{6,7},{7,6},{8,9},{9,8},{10,11... | collective-permute-start | bytes 983048 | tf_op jit(solution)/shard_map/ppermute | solution.py:629
  742.9 19.1 %collective-permute-start.26 = (bf16[4,1,32,1024]{3,2,0,1:T(8,128)(2,1)S(1)}, bf16[4,1,32,1024]{3,2,0,1:T(8,128)(2,1)S(1)}, u32[]{:S(2)}, u32[]{:S(2)}) collective-permute-start(bf16[4,1,32,1024]{3,2,0,1:T(8,128)(2,1)S(1)} %constant_dynamic-slice_fusion.13), channel_id=1, source_target_pairs={{0,1},{1,0},{2,3},{3,2},{4,5},{5,4},{6,7},{7,6},{8,9},{9,8},{10,11... | collective-permute-start | bytes 786440 | tf_op jit(solution)/shard_map/ppermute | solution.py:629
  764.9 27.7 %collective-permute-start.33 = (bf16[1,4,32,1664]{3,2,1,0:T(8,128)(2,1)}, bf16[1,4,32,1664]{3,2,1,0:T(8,128)(2,1)}, u32[]{:S(2)}, u32[]{:S(2)}) collective-permute-start(bf16[1,4,32,1664]{3,2,1,0:T(8,128)(2,1)} %dynamic-slice_bitcast_fusion.17), channel_id=1, source_target_pairs={{0,16},{4,20},{8,24},{12,28},{16,0},{20,4},{24,8},{28,12},{1,17},{... | collective-permute-start | bytes 1277960 | tf_op jit(solution)/shard_map/ppermute | solution.py:629
  768.2 24.4 %collective-permute-start.32 = (bf16[1,4,32,1792]{3,2,1,0:T(8,128)(2,1)}, bf16[1,4,32,1792]{3,2,1,0:T(8,128)(2,1)}, u32[]{:S(2)}, u32[]{:S(2)}) collective-permute-start(bf16[1,4,32,1792]{3,2,1,0:T(8,128)(2,1)} %dynamic-slice_bitcast_fusion.15), channel_id=1, source_target_pairs={{0,8},{4,12},{8,0},{12,4},{16,24},{20,28},{24,16},{28,20},{1,9},{5... | collective-permute-start | bytes 1376264 | tf_op jit(solution)/shard_map/ppermute | solution.py:629
  773.8 18.8 %collective-permute-start.30 = (bf16[512,4096]{1,0:T(8,128)(2,1)}, bf16[512,4096]{1,0:T(8,128)(2,1)}, u32[]{:S(2)}, u32[]{:S(2)}) collective-permute-start(bf16[512,4096]{1,0:T(8,128)(2,1)} %convolution_convert_fusion), channel_id=1, source_target_pairs={{0,4},{4,0},{8,12},{12,8},{16,20},{20,16},{24,28},{28,24},{1,5},{5... | collective-permute-start | bytes 12582920 | tf_op jit(solution)/shard_map/ppermute | solution.py:703
  805.1 72.9 %collective-permute-start.37 = (bf16[1,2,4,32,5120]{4,3,2,1,0:T(8,128)(2,1)}, bf16[1,2,4,32,5120]{4,3,2,1,0:T(8,128)(2,1)}, u32[]{:S(2)}, u32[]{:S(2)}) collective-permute-start(bf16[1,2,4,32,5120]{4,3,2,1,0:T(8,128)(2,1)} %dynamic-slice_bitcast_fusion), channel_id=1, source_target_pairs={{0,8},{4,12},{8,0},{12,4},{16,24},{20,28},{24,16},{28,20},{1,9},{5... | collective-permute-start | bytes 7864328 | tf_op jit(solution)/shard_map/ppermute | solution.py:629
  808.5 69.5 %collective-permute-start.36 = (bf16[4,2,4,32,1024]{4,3,2,1,0:T(8,128)(2,1)}, bf16[4,2,4,32,1024]{4,3,2,1,0:T(8,128)(2,1)}, u32[]{:S(2)}, u32[]{:S(2)}) collective-permute-start(bf16[4,2,4,32,1024]{4,3,2,1,0:T(8,128)(2,1)} %dynamic-slice_bitcast_fusion.2), channel_id=1, source_target_pairs={{0,16},{4,20},{8,24},{12,28},{16,0},{20,4},{24,8},{28,12},{1,17},{... | collective-permute-start | bytes 6291464 | tf_op jit(solution)/shard_map/ppermute | solution.py:629
  825.8 52.1 %collective-permute-start.35 = (bf16[1,2,32,1664]{3,2,1,0:T(8,128)(2,1)S(1)}, bf16[1,2,32,1664]{3,2,1,0:T(8,128)(2,1)S(1)}, u32[]{:S(2)}, u32[]{:S(2)}) collective-permute-start(bf16[1,2,32,1664]{3,2,1,0:T(8,128)(2,1)S(1)} %dynamic-slice_bitcast_fusion.31), channel_id=1, source_target_pairs={{0,2},{1,3},{2,0},{3,1},{4,6},{5,7},{6,4},{7,5},{8,10},{9,11},{10,... | collective-permute-start | bytes 638984 | tf_op jit(solution)/shard_map/ppermute | solution.py:629
  827.3 50.6 %collective-permute-start.34 = (bf16[1,2,32,1792]{3,2,1,0:T(8,128)(2,1)S(1)}, bf16[1,2,32,1792]{3,2,1,0:T(8,128)(2,1)S(1)}, u32[]{:S(2)}, u32[]{:S(2)}) collective-permute-start(bf16[1,2,32,1792]{3,2,1,0:T(8,128)(2,1)S(1)} %dynamic-slice_bitcast_fusion.29), channel_id=1, source_target_pairs={{0,2},{1,3},{2,0},{3,1},{4,6},{5,7},{6,4},{7,5},{8,10},{9,11},{10,... | collective-permute-start | bytes 688136 | tf_op jit(solution)/shard_map/ppermute | solution.py:629
  882.7 60.3 %collective-permute-start.41 = (bf16[1,4,32,5120]{3,2,1,0:T(8,128)(2,1)}, bf16[1,4,32,5120]{3,2,1,0:T(8,128)(2,1)S(1)}, u32[]{:S(2)}, u32[]{:S(2)}) collective-permute-start(bf16[1,4,32,5120]{3,2,1,0:T(8,128)(2,1)} %dynamic-slice_bitcast_fusion.4), channel_id=1, source_target_pairs={{0,16},{4,20},{8,24},{12,28},{16,0},{20,4},{24,8},{28,12},{1,17},{... | collective-permute-start | bytes 3932168 | tf_op jit(solution)/shard_map/ppermute | solution.py:629
  887.4 55.5 %collective-permute-start.40 = (bf16[4,4,32,1024]{3,2,1,0:T(8,128)(2,1)}, bf16[4,4,32,1024]{3,2,1,0:T(8,128)(2,1)}, u32[]{:S(2)}, u32[]{:S(2)}) collective-permute-start(bf16[4,4,32,1024]{3,2,1,0:T(8,128)(2,1)} %dynamic-slice_bitcast_fusion.6), channel_id=1, source_target_pairs={{0,8},{4,12},{8,0},{12,4},{16,24},{20,28},{24,16},{28,20},{1,9},{5... | collective-permute-start | bytes 3145736 | tf_op jit(solution)/shard_map/ppermute | solution.py:629
  889.2 53.7 %collective-permute-start.39 = (bf16[1,1,32,1664]{3,2,1,0:T(8,128)(2,1)}, bf16[1,1,32,1664]{3,2,1,0:T(8,128)(2,1)}, u32[]{:S(2)}, u32[]{:S(2)}) collective-permute-start(bf16[1,1,32,1664]{3,2,1,0:T(8,128)(2,1)} %constant_dynamic-slice_fusion.9), channel_id=1, source_target_pairs={{0,1},{1,0},{2,3},{3,2},{4,5},{5,4},{6,7},{7,6},{8,9},{9,8},{10,11... | collective-permute-start | bytes 319496 | tf_op jit(solution)/shard_map/ppermute | solution.py:629
  889.5 53.5 %collective-permute-start.38 = (bf16[1,1,32,1792]{3,2,1,0:T(8,128)(2,1)S(1)}, bf16[1,1,32,1792]{3,2,1,0:T(8,128)(2,1)S(1)}, u32[]{:S(2)}, u32[]{:S(2)}) collective-permute-start(bf16[1,1,32,1792]{3,2,1,0:T(8,128)(2,1)S(1)} %constant_dynamic-slice_fusion.10), channel_id=1, source_target_pairs={{0,1},{1,0},{2,3},{3,2},{4,5},{5,4},{6,7},{7,6},{8,9},{9,8},{10,11... | collective-permute-start | bytes 344072 | tf_op jit(solution)/shard_map/ppermute | solution.py:629
  892.3 48.5 %collective-permute-start.42 = (bf16[2,288,512]{2,1,0:T(8,128)(2,1)}, bf16[2,288,512]{2,1,0:T(8,128)(2,1)}, u32[]{:S(2)}, u32[]{:S(2)}) collective-permute-start(bf16[2,288,512]{2,1,0:T(8,128)(2,1)} %slice_bitcast_fusion.1), channel_id=1, source_target_pairs={{0,4},{1,5},{2,6},{3,7},{4,0},{5,1},{6,2},{7,3},{8,12},{9,13},{10,... | collective-permute-start | bytes 1769480 | tf_op jit(solution)/shard_map/ppermute | solution.py:537
  946.7 54.4 %collective-permute-start.48 = (bf16[1,2,32,5120]{3,2,1,0:T(8,128)(2,1)}, bf16[1,2,32,5120]{3,2,1,0:T(8,128)(2,1)}, u32[]{:S(2)}, u32[]{:S(2)}) collective-permute-start(bf16[1,2,32,5120]{3,2,1,0:T(8,128)(2,1)} %dynamic-slice_bitcast_fusion.12), channel_id=1, source_target_pairs={{0,2},{1,3},{2,0},{3,1},{4,6},{5,7},{6,4},{7,5},{8,10},{9,11},{10,... | collective-permute-start | bytes 1966088 | tf_op jit(solution)/shard_map/ppermute | solution.py:629
  950.3 50.8 %collective-permute-start.47 = (bf16[4,2,32,1024]{3,2,0,1:T(8,128)(2,1)}, bf16[4,2,32,1024]{3,2,0,1:T(8,128)(2,1)}, u32[]{:S(2)}, u32[]{:S(2)}) collective-permute-start(bf16[4,2,32,1024]{3,2,0,1:T(8,128)(2,1)} %bitcast.427), channel_id=1, source_target_pairs={{0,2},{1,3},{2,0},{3,1},{4,6},{5,7},{6,4},{7,5},{8,10},{9,11},{10,... | collective-permute-start | bytes 1572872 | tf_op jit(solution)/shard_map/ppermute | solution.py:629
  966.0 35.2 %collective-permute-start.44 = (bf16[512,2048]{1,0:T(8,128)(2,1)}, bf16[512,2048]{1,0:T(8,128)(2,1)}, u32[]{:S(2)}, u32[]{:S(2)}) collective-permute-start(bf16[512,2048]{1,0:T(8,128)(2,1)} %add_convert_fusion.7), channel_id=1, source_target_pairs={{0,4},{4,0},{8,12},{12,8},{16,20},{20,16},{24,28},{28,24},{1,5},{5... | collective-permute-start | bytes 6291464 | tf_op jit(solution)/shard_map/ppermute | solution.py:703
  979.0 22.1 %collective-permute-start.45 = (bf16[512,1024]{1,0:T(8,128)(2,1)}, bf16[512,1024]{1,0:T(8,128)(2,1)}, u32[]{:S(2)}, u32[]{:S(2)}) collective-permute-start(bf16[512,1024]{1,0:T(8,128)(2,1)} %convolution_convert_fusion.4), channel_id=1, source_target_pairs={{0,4},{4,0},{8,12},{12,8},{16,20},{20,16},{24,28},{28,24},{1,5},{5... | collective-permute-start | bytes 3145736 | tf_op jit(solution)/shard_map/ppermute | solution.py:703
  984.5 16.7 %collective-permute-start.46 = (bf16[4,128,384]{2,1,0:T(8,128)(2,1)}, bf16[4,128,384]{2,1,0:T(8,128)(2,1)}, u32[]{:S(2)}, u32[]{:S(2)}) collective-permute-start(bf16[4,128,384]{2,1,0:T(8,128)(2,1)} %bitcast.121), channel_id=1, source_target_pairs={{0,4},{4,0},{8,12},{12,8},{16,20},{20,16},{24,28},{28,24},{1,5},{5... | collective-permute-start | bytes 1179656 | tf_op jit(solution)/shard_map/ppermute | solution.py:809
  1008.3 29.2 %collective-permute-start.54 = (bf16[1,2,4,32,1664]{4,3,2,1,0:T(8,128)(2,1)S(1)}, bf16[1,2,4,32,1664]{4,3,2,1,0:T(8,128)(2,1)S(1)}, u32[]{:S(2)}, u32[]{:S(2)}) collective-permute-start(bf16[1,2,4,32,1664]{4,3,2,1,0:T(8,128)(2,1)S(1)} %dynamic-slice_bitcast_fusion.10), channel_id=1, source_target_pairs={{0,8},{4,12},{8,0},{12,4},{16,24},{20,28},{24,16},{28,20},{1,9},{5... | collective-permute-start | bytes 2555912 | tf_op jit(solution)/shard_map/ppermute | solution.py:629
  1009.4 28.2 %collective-permute-start.53 = (bf16[1,2,4,32,1792]{4,3,2,1,0:T(8,128)(2,1)S(1)}, bf16[1,2,4,32,1792]{4,3,2,1,0:T(8,128)(2,1)S(1)}, u32[]{:S(2)}, u32[]{:S(2)}) collective-permute-start(bf16[1,2,4,32,1792]{4,3,2,1,0:T(8,128)(2,1)S(1)} %dynamic-slice_bitcast_fusion.8), channel_id=1, source_target_pairs={{0,16},{4,20},{8,24},{12,28},{16,0},{20,4},{24,8},{28,12},{1,17},{... | collective-permute-start | bytes 2752520 | tf_op jit(solution)/shard_map/ppermute | solution.py:629
  1011.8 25.8 %collective-permute-start.52 = (bf16[1,1,32,5120]{3,2,1,0:T(8,128)(2,1)S(1)}, bf16[1,1,32,5120]{3,2,1,0:T(8,128)(2,1)S(1)}, u32[]{:S(2)}, u32[]{:S(2)}) collective-permute-start(bf16[1,1,32,5120]{3,2,1,0:T(8,128)(2,1)S(1)} %constant_dynamic-slice_fusion.4), channel_id=1, source_target_pairs={{0,1},{1,0},{2,3},{3,2},{4,5},{5,4},{6,7},{7,6},{8,9},{9,8},{10,11... | collective-permute-start | bytes 983048 | tf_op jit(solution)/shard_map/ppermute | solution.py:629
  1011.9 19.3 %collective-permute-start.49 = (bf16[144,1024]{1,0:T(8,128)(2,1)S(1)}, bf16[144,1024]{1,0:T(8,128)(2,1)S(1)}, u32[]{:S(2)}, u32[]{:S(2)}) collective-permute-start(bf16[144,1024]{1,0:T(8,128)(2,1)S(1)} %get-tuple-element.354), channel_id=1, source_target_pairs={{1,0},{0,1},{5,2},{4,3},{3,4},{2,5},{7,6},{6,7},{9,8},{8,9},{13,10... | collective-permute-start | bytes 884744 | tf_op jit(solution)/shard_map/ppermute | solution.py:494
  1014.0 17.2 %collective-permute-start.50 = (bf16[144,1024]{1,0:T(8,128)(2,1)S(1)}, bf16[144,1024]{1,0:T(8,128)(2,1)S(1)}, u32[]{:S(2)}, u32[]{:S(2)}) collective-permute-start(bf16[144,1024]{1,0:T(8,128)(2,1)S(1)} %get-tuple-element.355), channel_id=1, source_target_pairs={{0,0},{1,1},{4,2},{5,3},{2,4},{3,5},{6,6},{7,7},{8,8},{9,9},{12,10... | collective-permute-start | bytes 884744 | tf_op jit(solution)/shard_map/ppermute | solution.py:494
  1055.7 17.0 %collective-permute-start.57 = (bf16[1,2,32,1792]{3,2,1,0:T(8,128)(2,1)S(1)}, bf16[1,2,32,1792]{3,2,1,0:T(8,128)(2,1)S(1)}, u32[]{:S(2)}, u32[]{:S(2)}) collective-permute-start(bf16[1,2,32,1792]{3,2,1,0:T(8,128)(2,1)S(1)} %dynamic-slice_bitcast_fusion.28), channel_id=1, source_target_pairs={{0,2},{1,3},{2,0},{3,1},{4,6},{5,7},{6,4},{7,5},{8,10},{9,11},{10,... | collective-permute-start | bytes 688136 | tf_op jit(solution)/shard_map/ppermute | solution.py:629
  (239 other events, 3361.4 us)
Sparse Core Ops, SparseCore 0:
  23.5 161.0 all-gather.2
  188.0 177.5 all-gather.4

commit v3 on v2

--- a/solution.py
+++ b/solution.py
@@ -35,8 +35,17 @@
     return centered * lax.rsqrt(spread + NORM_EPSILON) * scale_gain + offset
 
 
+def below(values_in):
+    return 0.5 * lax.erf(values_in * (0.5**0.5)) + 0.5
+
+
 def exact_gelu(values_in):
-    return jax.nn.gelu(values_in, approximate=False)
+    return values_in * below(values_in)
+
+
+def gelu_slope(values_in):
+    bell = jnp.exp(-0.5 * values_in * values_in) * ((0.5 / jnp.pi) ** 0.5)
+    return below(values_in) + values_in * bell
 
 
 def dot(left, right, left_axis, right_axis):
@@ -442,6 +451,195 @@
     return out
 
 
+def split_kernel(block, core_ref, values_ref, mine_ref, other_ref):
+    first_core = core_ref[0] == 0
+    mine, other = [], []
+    for start in range(0, values_ref.shape[1], 2 * block):
+        first = values_ref[:, start : start + block]
+        second = values_ref[:, start + block : start + 2 * block]
+        mine.append(jnp.where(first_core, first, second))
+        other.append(jnp.where(first_core, second, first))
+    mine_ref[...] = jnp.concatenate(mine, axis=1)
+    other_ref[...] = jnp.concatenate(other, axis=1)
+
+
+def split_cores(values, block, core):
+    rows, columns = values.shape
+    step = min(columns, 8 * max(block, LANES))
+    half = jax.ShapeDtypeStruct((rows, columns // 2), values.dtype)
+    return pl.pallas_call(
+        functools.partial(split_kernel, block),
+        grid=(columns // step,),
+        in_specs=[
+            pl.BlockSpec(memory_space=pltpu.SMEM),
+            pl.BlockSpec((rows, step), lambda at: (0, at)),
+        ],
+        out_specs=[pl.BlockSpec((rows, step // 2), lambda at: (0, at))] * 2,
+        out_shape=[half, half],
+        cost_estimate=pl.CostEstimate(
+            flops=0, bytes_accessed=4 * rows * columns, transcendentals=0
+        ),
+        name="split_cores",
+    )(core.reshape(1), values)
+
+
+def product_kernel(left_count, grad_count, steps, own, *refs):
+    picks_ref = refs[0]
+    lefts = refs[1 : 1 + left_count]
+    grads = refs[1 + left_count : 1 + left_count + grad_count]
+    outs = refs[1 + left_count + grad_count :]
+    del picks_ref
+    at = pl.program_id(0)
+    for lead in range(left_count * grad_count):
+        found = dot(lefts[lead % left_count][...], grads[lead % grad_count][...], 0, 0)
+        if not own:
+            outs[0][lead, 0] = found.astype(BF16)
+            continue
+        got_ref, sent_ref, kept_ref = outs
+        total = (found + got_ref[lead, 0].astype(F32)).astype(BF16)
+
+        @pl.when(at < steps // 2)
+        def _():
+            sent_ref[lead, 0] = total
+
+        @pl.when(at >= steps // 2)
+        def _():
+            kept_ref[lead, 0] = total
+
+
+def half_product(home, lefts, grads, got=None, place=None):
+    count = lefts[0].shape[0]
+    columns = grads[0].shape[1]
+    leading = len(lefts) * len(grads)
+    chips = home.doc_size // 2
+    block = home.width // home.doc_size
+    own = got is not None
+    doc = lax.axis_index("doc")
+    core = doc % 2
+    mine = (doc >> (1 + place)) & 1 if own else core
+    picks = jnp.stack([core if own else 1 - core, mine]).astype(jnp.int32)
+
+    def chip(at, picks_ref):
+        if not own:
+            return at
+        half = chips // 2
+        inner = jnp.where(at < half, at, at - half)
+        bit = jnp.where(at < half, 1 - picks_ref[1], picks_ref[1])
+        low = inner & ((1 << place) - 1)
+        return ((inner >> place) << (place + 1)) | (bit << place) | low
+
+    left_spec = pl.BlockSpec(
+        (count, block), lambda at, picks_ref: (0, chip(at, picks_ref) * 2 + picks_ref[0])
+    )
+    piece = (leading, 1, block, columns)
+    in_specs = [left_spec] * len(lefts) + [
+        pl.BlockSpec(item.shape, lambda at, picks_ref: (0, 0)) for item in grads
+    ]
+    operands = [*lefts, *grads]
+    if own:
+        in_specs.append(pl.BlockSpec(piece, lambda at, picks_ref: (0, chip(at, picks_ref), 0, 0)))
+        operands.append(got)
+        half = chips // 2
+        out_specs = [
+            pl.BlockSpec(piece, lambda at, picks_ref: (0, jnp.minimum(at, half - 1), 0, 0)),
+            pl.BlockSpec(piece, lambda at, picks_ref: (0, jnp.maximum(at - half, 0), 0, 0)),
+        ]
+        out_shape = [jax.ShapeDtypeStruct((leading, half, block, columns), BF16)] * 2
+    else:
+        out_specs = pl.BlockSpec(piece, lambda at, picks_ref: (0, at, 0, 0))
+        out_shape = jax.ShapeDtypeStruct((leading, chips, block, columns), BF16)
+    return pl.pallas_call(
+        functools.partial(product_kernel, len(lefts), len(grads), chips, own),
+        grid_spec=pltpu.PrefetchScalarGridSpec(
+            num_scalar_prefetch=1, grid=(chips,), in_specs=in_specs, out_specs=out_specs
+        ),
+        out_shape=out_shape,
+        compiler_params=pltpu.CompilerParams(vmem_limit_bytes=40 << 20),
+        cost_estimate=pl.CostEstimate(
+            flops=2 * leading * chips * block * count * columns,
+            bytes_accessed=(6 if own else 2) * leading * chips * block * columns,
+            transcendentals=0,
+        ),
+        name="half_product",
+    )(picks, *operands)
+
+
+def panels_kernel(picks, left_count, *refs):
+    lefts, grads, out_ref = refs[:left_count], refs[left_count:-1], refs[-1]
+    for panel, (left, right) in enumerate(picks):
+
+        @pl.when(pl.program_id(0) == panel)
+        def _():
+            out_ref[...] = dot(lefts[left][...], grads[right][...], 0, 0).astype(BF16)
+
+
+def panel_products(lefts, grads, picks):
+    width, columns = lefts[0].shape[1], grads[0].shape[1]
+    count = lefts[0].shape[0]
+    return pl.pallas_call(
+        functools.partial(panels_kernel, picks, len(lefts)),
+        grid=(len(picks),),
+        in_specs=[
+            pl.BlockSpec(item.shape, lambda at: (0, 0), pipeline_mode=pl.Buffered(1))
+            for item in (*lefts, *grads)
+        ],
+        out_specs=pl.BlockSpec((width, columns), lambda at: (0, at)),
+        out_shape=jax.ShapeDtypeStruct((width, columns * len(picks)), BF16),
+        compiler_params=pltpu.CompilerParams(vmem_limit_bytes=48 << 20),
+        cost_estimate=pl.CostEstimate(
+            flops=2 * len(picks) * width * count * columns,
+            bytes_accessed=2 * len(picks) * width * columns,
+            transcendentals=0,
+        ),
+        name="panel_products",
+    )(*lefts, *grads)
+
+
+def join_kernel(block, core_ref, mine_ref, other_ref, plus_ref, out_ref):
+    first_core = core_ref[0] == 0
+    pieces = []
+    for start in range(0, mine_ref.shape[1], block):
+        mine, other = mine_ref[:, start : start + block], other_ref[:, start : start + block]
+        pieces.append(jnp.where(first_core, mine, other))
+        pieces.append(jnp.where(first_core, other, mine))
+    out_ref[...] = jnp.concatenate(pieces, axis=1) + plus_ref[...]
+
+
+def join_cores(mine, other, plus, block, core):
+    rows, columns = plus.shape
+    step = min(columns, 4 * max(block, LANES))
+    half = pl.BlockSpec((rows, step // 2), lambda at: (0, at))
+    whole = pl.BlockSpec((rows, step), lambda at: (0, at))
+    return pl.pallas_call(
+        functools.partial(join_kernel, block),
+        grid=(columns // step,),
+        in_specs=[pl.BlockSpec(memory_space=pltpu.SMEM), half, half, whole],
+        out_specs=whole,
+        out_shape=jax.ShapeDtypeStruct(plus.shape, F32),
+        cost_estimate=pl.CostEstimate(
+            flops=0, bytes_accessed=12 * rows * columns, transcendentals=0
+        ),
+        name="join_cores",
+    )(core.reshape(1), mine, other, plus)
+
+
+class Move:
+    def __init__(self, got, join, hold=0):
+        self.hold = hold
+        self.got = got
+        self.join = join
+        self.value = None
+
+    def advance(self):
+        self.value = self.join(self.got)
+        self.got = None
+
+    def result(self):
+        if self.got is not None:
+            self.advance()
+        return self.value
+
+
 class Home:
     def __init__(self, mesh_shape, local_docs, block_rows, width):
         self.width = width
@@ -473,37 +671,57 @@
 
     def to_home(self, local):
         ctx = lax.axis_index("ctx")
-        doc_here = ctx // self.span
+        swap = ((ctx // self.span) % 2) == 1
         pieces = []
         for turn in range(2):
             piece = lax.dynamic_index_in_dim(local, (ctx + turn) % 2, 0, keepdims=False)
             pieces.append(lax.ppermute(piece, BOTH, self.move_pairs(turn)))
-        swap = (doc_here % 2) == 1
-        low_half = jnp.where(swap, pieces[1], pieces[0])
-        high_half = jnp.where(swap, pieces[0], pieces[1])
-        return jnp.concatenate([low_half, high_half], axis=0)
+
+        def join(got):
+            low_half = jnp.where(swap, got[1], got[0])
+            high_half = jnp.where(swap, got[0], got[1])
+            return jnp.concatenate([low_half, high_half], axis=0)
+
+        return Move(pieces, join)
 
     def from_home(self, rows):
         ctx = lax.axis_index("ctx")
         doc_here = ctx // self.span
+        swap = (ctx % 2) == 1
         halves = rows.reshape(2, self.block, rows.shape[1])
         pieces = []
         for turn in range(2):
             piece = lax.dynamic_index_in_dim(halves, (doc_here + turn) % 2, 0, keepdims=False)
             back = [(target, source) for source, target in self.move_pairs(turn)]
             pieces.append(lax.ppermute(piece, BOTH, back))
-        swap = (ctx % 2) == 1
-        first = jnp.where(swap, pieces[1], pieces[0])
-        second = jnp.where(swap, pieces[0], pieces[1])
-        return jnp.stack([first, second])
-
-    def core_half(self, values, core):
+
+        def join(got):
+            first = jnp.where(swap, got[1], got[0])
+            second = jnp.where(swap, got[0], got[1])
+            return jnp.stack([first, second]).astype(F32)
+
+        return Move(pieces, join)
+
+    def halves(self, values):
+        core = lax.axis_index("doc") % 2
+        return split_cores(values, self.width // self.doc_size, core)
+
+    def join_rows(self, mine, other):
+        core = lax.axis_index("doc") % 2
+        columns = mine.shape[1]
+        mine, other = (item.reshape(self.doc_size // 2, 1, -1, columns) for item in (mine, other))
+        both = jnp.concatenate(
+            [jnp.where(core == 0, mine, other), jnp.where(core == 0, other, mine)], axis=1
+        )
+        return both.reshape(-1, columns)
+
+    def core_join(self, mine, other, core):
         block = self.width // self.doc_size
         pieces = []
-        for start in range(0, values.shape[1], 2 * block):
-            first = values[:, start : start + block]
-            second = values[:, start + block : start + 2 * block]
+        for start in range(0, mine.shape[1], block):
+            first, second = mine[:, start : start + block], other[:, start : start + block]
             pieces.append(jnp.where(core == 0, first, second))
+            pieces.append(jnp.where(core == 0, second, first))
         return jnp.concatenate(pieces, axis=1)
 
     def position(self):
@@ -539,48 +757,173 @@
         ]
 
 
-def to_part_order(columns, devices, shard):
-    rows, hidden = columns.shape
-    split = columns.reshape(rows, devices, hidden // (devices * shard), shard)
-    return split.transpose(0, 2, 1, 3).reshape(rows, hidden)
-
-
 def to_device_order(columns, devices, shard):
     rows, hidden = columns.shape
     split = columns.reshape(rows, hidden // (devices * shard), devices, shard)
     return split.transpose(0, 2, 1, 3).reshape(rows, hidden)
 
 
-def pack_layer(devices, w_qkv, w_out, w_in, w_down, tables, gains, biases, b_in):
+def pack_first(w_qkv, tables, gains, biases, b_in):
     shard = w_qkv.shape[0]
-    down = w_down.reshape(-1, shard, w_down.shape[1])
-    down = [down[part] for part in range(down.shape[0])]
     small = jnp.concatenate(
         [tables.reshape(-1, shard).T, gains.T, biases.T, b_in.reshape(-1, shard).T], axis=1
     )
     small = jnp.pad(small, ((0, 0), (0, pad_lanes(small.shape[1]) - small.shape[1])))
+    return jnp.concatenate([w_qkv, small], axis=1)
+
+
+def pack_rest(devices, w_out, w_in, w_down):
+    shard, width = w_out.shape
+    split = w_in.reshape(shard, devices, -1, shard).transpose(2, 0, 1, 3)
     return jnp.concatenate(
-        [w_qkv, w_out, to_part_order(w_in, devices, shard), *down, small], axis=1
-    )
-
-
-def unpack_layer(packed):
-    width = packed.shape[0]
-    hidden = ((packed.shape[1] - 4 * width) // (2 * width)) * width
-    start = 4 * width + hidden
-    small = packed[:, start + hidden :]
-    table_cols = 2 * BUCKETS
-    rows = small[:, table_cols:].astype(F32).T
+        [w_out[None], split.reshape(-1, shard, width), w_down.reshape(-1, shard, width)]
+    )
+
+
+def unpack_rest(packed):
+    parts = (packed.shape[0] - 1) // 2
     return dict(
-        qkv=packed[:, : 3 * width],
-        out=packed[:, 3 * width : 4 * width],
-        w_in=packed[:, 4 * width : start],
-        down=[packed[:, start + at : start + at + width] for at in range(0, hidden, width)],
-        tables=small[:, :table_cols],
-        gains=rows[:2],
-        biases=rows[2:9],
-        b_in=rows[9 : 9 + hidden // width].reshape(hidden),
-    )
+        out=packed[0],
+        w_in=[packed[1 + part] for part in range(parts)],
+        down=[packed[1 + parts + part] for part in range(parts)],
+    )
+
+
+class Gather:
+    def __init__(self, home, block, cut):
+        self.home = home
+        self.hold = 0
+        self.values = [block[None]]
+        self.cut = cut
+        high = [1 << at for at in range(1, home.doc_size.bit_length() - 1)]
+        self.high = high
+        self.orders = [list(high), list(reversed(high))]
+        self.seen = [[], []]
+        self.steps = [("ctx", 0)] + [("doc", at) for at in range(len(high))] + [("core", 0)]
+        self.send()
+
+    def send(self):
+        kind, at = self.step = self.steps.pop(0)
+        if kind == "doc" and len(self.values) == 1:
+            value = self.values[0]
+            self.values = [value[:, :, : self.cut], value[:, :, self.cut :]]
+        doc_size = self.home.doc_size
+        if kind == "ctx":
+            size = self.home.ctx_size
+            self.got = [
+                lax.ppermute(self.values[0], "ctx", flips(size, far)) for far in range(1, size)
+            ]
+            return
+        if kind == "doc":
+            pairs = [("doc", flips(doc_size, order[at])) for order in self.orders]
+        else:
+            pairs = [("doc", flips(doc_size, 1))] * 2
+        self.got = [
+            lax.ppermute(value, *pair) for value, pair in zip(self.values, pairs)
+        ]
+
+    def joined(self, own, got, mine, axis):
+        return jnp.stack(
+            [jnp.where(mine == 0, own, got), jnp.where(mine == 0, got, own)], axis=axis
+        )
+
+    def advance(self):
+        kind, at = self.step
+        if kind == "ctx":
+            mine = lax.axis_index("ctx")
+            near = self.values + self.got
+            size = self.home.ctx_size
+            rows = []
+            for place in range(size):
+                found = near[place]
+                for here in range(1, size):
+                    found = jnp.where(mine == here, near[place ^ here], found)
+                rows.append(found)
+            self.values = [jnp.concatenate(rows, axis=0)]
+        elif kind == "doc":
+            values = []
+            for color in range(2):
+                bit = self.orders[color][at]
+                mine = (lax.axis_index("doc") // bit) % 2
+                axis = sum(1 for other in self.seen[color] if other > bit)
+                self.seen[color].append(bit)
+                values.append(self.joined(self.values[color], self.got[color], mine, axis))
+            self.values = values
+        else:
+            self.other = [self.flat(value) for value in self.got]
+            self.mine = [self.flat(value) for value in self.values]
+            self.got = None
+            return
+        self.send()
+
+    def flat(self, value):
+        return value.reshape(-1, value.shape[-1])
+
+    def finish(self):
+        while self.got is not None:
+            self.advance()
+        return First(self)
+
+
+class First:
+    def __init__(self, gather):
+        home = self.home = gather.home
+        self.core = lax.axis_index("doc") % 2
+        width = home.width
+        cut = gather.cut
+        self.cut = cut
+        left = 3 * width - cut
+        self.weights = [
+            (half[0], half[1][:, :left]) for half in (gather.mine, gather.other)
+        ]
+        small = [half[1][:, left:] for half in (gather.mine, gather.other)]
+        table_cols = 2 * BUCKETS
+        self.tables = [half[:, :table_cols] for half in small]
+        rows = [half[:, table_cols:].astype(F32).T for half in small]
+        rows = home.core_join(rows[0], rows[1], self.core)
+        self.gains = rows[:2]
+        self.biases = rows[2:9]
+        self.b_in = rows[9:]
+
+    def project(self, rows):
+        mine, other = rows
+        return jnp.concatenate(
+            [
+                dot(mine, first, 1, 0) + dot(other, second, 1, 0)
+                for first, second in zip(*self.weights)
+            ],
+            axis=1,
+        )
+
+    def relative(self):
+        width = self.home.width
+        cut = self.cut
+        mine, other = self.weights
+        wanted = 2 * width - cut
+        return jnp.concatenate(
+            [
+                dot(self.tables[0], mine[0], 0, 0) + dot(self.tables[1], other[0], 0, 0),
+                dot(self.tables[0], mine[1][:, :wanted], 0, 0)
+                + dot(self.tables[1], other[1][:, :wanted], 0, 0),
+            ],
+            axis=1,
+        )
+
+    def back(self, grads, plus):
+        first, second = grads[:, : self.cut], grads[:, self.cut :]
+        mine, other = [
+            dot(first, half[0], 1, 1) + dot(second, half[1], 1, 1) for half in self.weights
+        ]
+        block = self.home.width // self.home.doc_size
+        return join_cores(mine, other, plus, block, self.core)
+
+    def tables_back(self, which, query_part, key_part):
+        width = self.home.width
+        grads = jnp.concatenate([query_part, key_part], axis=1)
+        half = self.weights[which]
+        return dot(half[0], grads[:, : self.cut], 1, 1) + dot(
+            half[1][:, : 2 * width - self.cut], grads[:, self.cut :], 1, 1
+        )
 
 
 def flips(size, bit):
@@ -588,96 +931,158 @@
 
 
 class Scatter:
-    def __init__(self, shape, order):
-        self.doc_size, self.ctx_size = shape
-        self.order = order
-        self.bits = [1 << at for at in range(self.doc_size.bit_length() - 2, 0, -1)]
-        self.value = None
-        self.got = None
-        self.steps = None
-
-    def begin(self, leading, half):
-        columns = half.shape[-1]
-        block = half.size // (columns * leading * (self.doc_size // 2) * self.ctx_size)
-        self.value = half.reshape((leading,) + (2,) * len(self.bits) + (self.ctx_size, block, columns))
-        self.left = list(self.bits)
-        steps = [("doc", bit) for bit in (self.bits if self.order == 0 else reversed(self.bits))]
-        size = self.ctx_size // 2
-        while size:
-            steps.append(("ctx", size))
-            size //= 2
-        self.steps = steps
+    def __init__(self, home, colors, apart):
+        self.home = home
+        self.apart = apart
+        self.hold = 0
+        self.done = []
+        places = list(range(home.doc_size.bit_length() - 2))
+        self.orders = [places[::-1], places]
+        self.left = [places[::-1], places[::-1]]
+        self.kept, self.got = [], []
+        for color, pieces in enumerate(colors):
+            place = self.next_place(color)
+            self.kept.append([kept for _, kept in pieces])
+            self.got.append([self.exchange(sent, place) for sent, _ in pieces])
+
+    def next_place(self, color):
+        place = self.orders[color].pop(0)
+        self.left[color] = [item for item in self.left[color] if item != place]
+        return place
+
+    def exchange(self, sent, place):
+        return lax.ppermute(sent, "doc", flips(self.home.doc_size, 2 << place))
+
+    def send(self):
+        ctx = lax.axis_index("ctx")
+        self.kept, self.got = [], []
+        if self.orders[0]:
+            for color, value in enumerate(self.values):
+                leading, chips, block, columns = value.shape
+                before = self.left[color]
+                place = self.next_place(color)
+                axis = before.index(place)
+                split = value.reshape(leading, 1 << axis, 2, -1, block, columns)
+                mine = (lax.axis_index("doc") >> (1 + place)) & 1
+                shape = (leading, chips // 2, block, columns)
+                kept = lax.dynamic_index_in_dim(split, mine, 2, keepdims=False)
+                sent = lax.dynamic_index_in_dim(split, 1 - mine, 2, keepdims=False)
+                self.kept.append([kept.reshape(shape)])
+                self.got.append([self.exchange(sent.reshape(shape), place)])
+            return
+        count = 1 if self.apart else len(self.values)
+        now, self.values = self.values[:count], self.values[count:]
+        size = self.home.ctx_size
+        wide = jnp.concatenate(
+            [value[at, 0] for value in now for at in range(value.shape[0])], axis=-1
+        )
+        wide = wide.reshape(size, wide.shape[0] // size, wide.shape[1])
+        self.last = lax.dynamic_index_in_dim(wide, ctx, 0, keepdims=False)
+        for far in range(1, size):
+            sent = lax.dynamic_index_in_dim(wide, ctx ^ far, 0, keepdims=False)
+            self.got.append(lax.ppermute(sent, "ctx", flips(size, far)))
+
+    def advance(self):
+        if not self.kept:
+            total = self.last.astype(F32)
+            for piece in self.got:
+                total = total + piece.astype(F32)
+            self.done.append(total)
+            self.got = None
+            if self.values:
+                self.send()
+            return
+        self.values = [
+            jnp.concatenate(
+                [
+                    (kept.astype(F32) + got.astype(F32)).astype(BF16)
+                    for kept, got in zip(keeps, gots)
+                ],
+                axis=0,
+            )
+            for keeps, gots in zip(self.kept, self.got)
+        ]
         self.send()
 
-    def send(self):
-        self.kept = self.got = None
-        if not self.steps:
-            return
-        axis_name, bit = self.steps.pop(0)
-        value = self.value
-        if axis_name == "doc":
-            axis = 1 + self.left.index(bit)
-            self.left.remove(bit)
-            size = self.doc_size
-        else:
-            axis = 1
-            value = value.reshape((value.shape[0], 2, value.shape[1] // 2) + value.shape[2:])
-            size = self.ctx_size
-        mine = (lax.axis_index(axis_name) // bit) % 2
-        self.kept = lax.dynamic_index_in_dim(value, mine, axis, keepdims=False)
-        sent = lax.dynamic_index_in_dim(value, 1 - mine, axis, keepdims=False)
-        self.got = lax.ppermute(sent, axis_name, flips(size, bit))
-
-    def advance(self):
-        total = self.kept.astype(F32) + self.got.astype(F32)
-        self.value = total.astype(BF16)
-        if not self.steps:
-            self.value = total
-        self.send()
-
     def result(self):
-        value = self.value
-        return value.reshape((value.shape[0],) + value.shape[-2:])
+        return self.done[0] if len(self.done) == 1 else jnp.concatenate(self.done, axis=1)
+
+
+class Offload:
+    def __init__(self, packed, axis, after=None):
+        self.axis = axis
+        self.packed = packed
+        self.after = after
+        if after is None:
+            self.start()
+
+    def start(self, values=()):
+        if self.after is not None:
+            self.packed, self.after.value, values = lax.optimization_barrier(
+                (self.packed, self.after.value, values)
+            )
+        self.value = lax.psum_scatter(
+            self.packed, BOTH, scatter_dimension=self.axis, tiled=True
+        )
+        return values
+
+    def result(self):
+        return self.value.astype(F32)
 
 
 class Flight:
     def __init__(self):
         self.moving = []
+        self.waiting = []
 
     def add(self, scatter):
         self.moving.append(scatter)
 
     def tick(self, values):
-        got = [item.got for item in self.moving]
+        self.moving = [item for item in self.moving if item.got is not None]
+        ready = [item for item in self.moving if item.hold <= 0]
+        got = [item.got for item in ready]
         values, got = lax.optimization_barrier((values, got))
-        for item, piece in zip(self.moving, got):
+        for item in self.moving:
+            item.hold -= 1
+        for item, piece in zip(ready, got):
             item.got = piece
             item.advance()
         self.moving = [item for item in self.moving if item.got is not None]
         return values
 
 
-def layer_forward(home, rows_in, rows_low, weights, lookups):
+def layer_forward(home, flight, rows_in, rows_low, first, rest, fetch_next, lookups):
     width = rows_in.shape[1]
-    gains, biases = weights["gains"], weights["biases"]
-    qkv = (dot(rows_low, weights["qkv"], 1, 0) + biases[:3].reshape(1, -1)).astype(BF16)
+    gains, biases = first.gains, first.biases
+    row_halves = home.halves(rows_low)
+    qkv = (first.project(row_halves) + biases[:3].reshape(1, -1)).astype(BF16)
+    qkv = fetch_next(flight.tick(qkv))
     other_kv = home.fetch(qkv[:, width:])
-    rel_both = dot(weights["tables"], weights["qkv"][:, : 2 * width], 0, 0).astype(BF16)
+    rel_both = first.relative().astype(BF16)
     rel_query = rel_both[:, :width].reshape(2, BUCKETS, width)
     rel_key = rel_both[:, width:].reshape(2, BUCKETS, width)
     mixed, prob = attend(qkv, other_kv, rel_key, rel_query, lookups)
-    first_sum = rows_in + (dot(mixed, weights["out"], 1, 0) + biases[3])
+    mixed = flight.tick(mixed)
+    rest = unpack_rest(rest)
+    first_sum = rows_in + (dot(mixed, rest["out"], 1, 0) + biases[3])
     first_norm = norm_rows(first_sum, gains[0], biases[5])
     norm_low = first_norm.astype(BF16)
-    hidden_pre = dot(norm_low, weights["w_in"], 1, 0) + weights["b_in"]
-    active = exact_gelu(hidden_pre).astype(BF16)
+    hidden_pre = [
+        dot(norm_low, panel, 1, 0) + first.b_in[part : part + 1]
+        for part, panel in enumerate(rest["w_in"])
+    ]
+    active = [exact_gelu(item).astype(BF16) for item in hidden_pre]
+    active = flight.tick(active)
     down_rows = biases[4]
-    for part, panel in enumerate(weights["down"]):
-        down_rows = down_rows + dot(active[:, part * width : (part + 1) * width], panel, 1, 0)
+    for item, panel in zip(active, rest["down"]):
+        down_rows = down_rows + dot(item, panel, 1, 0)
     second_sum = first_norm + down_rows
     result = norm_rows(second_sum, gains[1], biases[6])
+    result = flight.tick(result)
     kept = dict(
         rows_low=rows_low,
+        row_halves=row_halves,
         qkv=qkv,
         other_kv=other_kv,
         rel_key=rel_key,
@@ -690,70 +1095,114 @@
         active=active,
         second_sum=second_sum,
     )
-    return result, kept
+    return result, kept, rest
+
+
+class WholeSum:
+    def __init__(self, home, lefts, grads, place):
+        self.home, self.lefts, self.grads = home, lefts, grads
+        self.place = place
+        self.block = home.width // home.doc_size
+        self.core = lax.axis_index("doc") % 2
+        self.direct = self.block % LANES == 0
+        if self.direct:
+            sent = half_product(home, lefts, grads)
+        else:
+            whole = jnp.stack(
+                [dot(left, item, 0, 0).astype(BF16) for left in lefts for item in grads]
+            )
+            self.whole = whole.reshape(
+                whole.shape[0], home.doc_size // 2, 2, self.block, whole.shape[2]
+            )
+            sent = lax.dynamic_index_in_dim(self.whole, 1 - self.core, 2, keepdims=False)
+        self.got = lax.ppermute(sent, "doc", flips(home.doc_size, 1))
+
+    def finish(self):
+        if self.direct:
+            return half_product(self.home, self.lefts, self.grads, self.got, self.place)
+        kept = lax.dynamic_index_in_dim(self.whole, self.core, 2, keepdims=False)
+        return split_chips((kept.astype(F32) + self.got.astype(F32)).astype(BF16), self.place)
+
+
+def split_chips(total, place):
+    leading, chips, block, columns = total.shape
+    split = total.reshape(leading, chips >> (place + 1), 2, 1 << place, block, columns)
+    mine = (lax.axis_index("doc") >> (1 + place)) & 1
+    sent = lax.dynamic_index_in_dim(split, 1 - mine, 2, keepdims=False)
+    kept = lax.dynamic_index_in_dim(split, mine, 2, keepdims=False)
+    shape = (leading, chips // 2, block, columns)
+    return sent.reshape(shape), kept.reshape(shape)
 
 
 class CoreSum:
     def __init__(self, home, terms):
-        self.home = home
         self.terms = terms
-        core = lax.axis_index("doc") % 2
-        self.core = core
-        sent = self.product(1 - core).astype(BF16)
-        self.got = lax.ppermute(sent, "doc", flips(home.doc_size, 1))
-
-    def product(self, core):
+        self.got = lax.ppermute(self.product(1).astype(BF16), "doc", flips(home.doc_size, 1))
+
+    def product(self, which):
         total = None
-        for left, right in self.terms:
-            piece = dot(self.home.core_half(left, core), right, 0, 0)
+        for halves, grads, axis in self.terms:
+            piece = dot(halves[which], grads, axis, 0)
             total = piece if total is None else total + piece
         return total
 
     def finish(self):
-        return (self.product(self.core) + self.got.astype(F32)).astype(BF16)
-
-
-def layer_backward(home, flight, grad_out, kept, weights, lookups):
+        return (self.product(0) + self.got.astype(F32)).astype(BF16)
+
+
+def layer_backward(home, flight, grad_out, kept, first_weights, weights, lookups, offload):
     width = grad_out.shape[1]
-    shape = (home.doc_size, home.ctx_size)
-    gains, biases = weights["gains"], weights["biases"]
-    rows = grad_out.shape[0]
-    parts = len(weights["down"])
+    gains, biases = first_weights.gains, first_weights.biases
+    top = home.doc_size.bit_length() - 3
 
     _, second_pull = jax.vjp(norm_rows, kept["second_sum"], gains[1], biases[6])
     grad_second, grad_gain_two, grad_offset_two = second_pull(grad_out)
     grad_down = grad_second.astype(BF16)
-    sum_down = CoreSum(home, [(kept["active"], grad_down)])
-    grad_active = jnp.concatenate(
-        [dot(grad_down, panel, 1, 1) for panel in weights["down"]], axis=1
-    )
-    _, gelu_pull = jax.vjp(exact_gelu, kept["hidden_pre"])
-    grad_hidden = gelu_pull(grad_active)[0].astype(BF16)
-    grad_hidden, grad_down, sum_down.got = flight.tick((grad_hidden, grad_down, sum_down.got))
-
-    sum_in = CoreSum(home, [(kept["norm_low"], grad_hidden)])
-    grad_first_norm = grad_second + dot(grad_hidden, weights["w_in"], 1, 1)
+    if not offload:
+        sum_down = WholeSum(home, kept["active"], [grad_down], top)
+    grad_hidden = [
+        (dot(grad_down, panel, 1, 1) * gelu_slope(item)).astype(BF16)
+        for panel, item in zip(weights["down"], kept["hidden_pre"])
+    ]
+    if offload:
+        grad_hidden, grad_down = flight.tick((grad_hidden, grad_down))
+    else:
+        grad_hidden, grad_down, sum_down.got = flight.tick((grad_hidden, grad_down, sum_down.got))
+        sum_in = WholeSum(home, [kept["norm_low"]], grad_hidden, 0)
+    grad_first_norm = grad_second
+    for item, panel in zip(grad_hidden, weights["w_in"]):
+        grad_first_norm = grad_first_norm + dot(item, panel, 1, 1)
     _, first_pull = jax.vjp(norm_rows, kept["first_sum"], gains[0], biases[5])
     grad_first, grad_gain_one, grad_offset_one = first_pull(grad_first_norm)
     grad_att = grad_first.astype(BF16)
-    sum_out = CoreSum(home, [(kept["mixed"], grad_att)])
     grad_mixed = dot(grad_att, weights["out"], 1, 1).astype(BF16)
-    half_down = sum_down.finish()
-    grad_mixed, half_down, sum_in.got, sum_out.got = flight.tick(
-        (grad_mixed, half_down, sum_in.got, sum_out.got)
-    )
-    scatter_down, scatter_in = Scatter(shape, 0), Scatter(shape, 1)
-    scatter_down.begin(parts, half_down)
-    half_in = jnp.concatenate([sum_in.finish(), sum_out.finish()], axis=1)
-    scatter_in.begin(1, half_in)
-    flight.add(scatter_down)
-    flight.add(scatter_in)
+    if offload:
+        parts = len(grad_hidden)
+        panels = panel_products(
+            [*kept["active"], kept["norm_low"], kept["mixed"]],
+            [grad_down, *grad_hidden, grad_att],
+            [(part, 0) for part in range(parts)]
+            + [(parts, 1 + part) for part in range(parts)]
+            + [(parts + 1, parts + 1)],
+        )
+        early = Offload(panels, 0)
+        grad_mixed = flight.tick(grad_mixed)
+    else:
+        sum_out = WholeSum(home, [kept["mixed"]], [grad_att], 0)
+        halves_down = sum_down.finish()
+        grad_mixed, halves_down, sum_in.got, sum_out.got = flight.tick(
+            (grad_mixed, halves_down, sum_in.got, sum_out.got)
+        )
+        while flight.waiting:
+            grad_mixed = flight.waiting.pop(0).start(grad_mixed)
+        early = Scatter(home, [[halves_down], [sum_in.finish(), sum_out.finish()]], True)
+        flight.add(early)
 
     pairs = width // PAIR
-    count = pairs // 2
     found = []
     moved = []
-    for first in range(0, pairs, count):
+    cuts = [0, pairs] if offload else [0, pairs // 2, 3 * pairs // 4, pairs]
+    for first, count in zip(cuts, [after - at for at, after in zip(cuts, cuts[1:])]):
         grad_query, grad_kv, grad_rel = attend_back(
             kept["qkv"],
             kept["other_kv"],
@@ -781,10 +1230,6 @@
         [item[0] for item in found] + [item[0] for item in own] + [item[1] for item in own], axis=1
     )
     rel_both = [jnp.concatenate([item[2][kind] for item in found], axis=1) for kind in range(2)]
-    tables = weights["tables"]
-    grad_tables = dot(weights["qkv"][:, :width], rel_both[0], 1, 1) + dot(
-        weights["qkv"][:, width : 2 * width], rel_both[1], 1, 1
-    )
     bias_sums = jnp.sum(grad_qkv.astype(F32), axis=0).reshape(3, width)
     small = jnp.concatenate(
         [
@@ -795,61 +1240,78 @@
             jnp.sum(grad_down.astype(F32), axis=0)[None],
             grad_offset_one[None],
             grad_offset_two[None],
-            jnp.sum(grad_hidden.astype(F32), axis=0).reshape(parts, width),
+            *[jnp.sum(item.astype(F32), axis=0)[None] for item in grad_hidden],
         ],
         axis=0,
-    ).T
-    total_cols = 2 * BUCKETS + small.shape[1]
-    small = jnp.concatenate([grad_tables, small], axis=1)
-    small = jnp.pad(small, ((0, 0), (0, pad_lanes(total_cols) - total_cols)))
-    split = small.astype(BF16).reshape(home.doc_size // 2, 2, -1, small.shape[1])
-    core = lax.axis_index("doc") % 2
-    small_sent = lax.dynamic_index_in_dim(split, 1 - core, 1, keepdims=False)
-    small_kept = lax.dynamic_index_in_dim(split, core, 1, keepdims=False)
-    small_got = lax.ppermute(small_sent, "doc", flips(home.doc_size, 1))
-    rows_turned = kept["rows_low"]
+    )
+    small_rows = small.shape[0]
+    small = jnp.pad(small, ((0, pad_lanes(small_rows) - small_rows), (0, 0))).astype(BF16)
+
+    if offload:
+        rel_wide = jnp.concatenate(rel_both, axis=1)
+        grad_qk = dot(kept["rows_low"], grad_qkv[:, : 2 * width], 0, 0) + dot(
+            home.join_rows(*first_weights.tables), rel_wide, 1, 0
+        )
+        grad_v = dot(kept["rows_low"], grad_qkv[:, 2 * width :], 0, 0)
+        found_tables = home.join_rows(
+            *[first_weights.tables_back(which, *rel_both).astype(BF16) for which in range(2)]
+        )
+        late = Offload(
+            jnp.concatenate(
+                [grad_qk.astype(BF16), grad_v.astype(BF16), found_tables, small.T], axis=1
+            ),
+            0,
+            early,
+        )
+        flight.waiting.append(late)
+        grad_rows = flight.tick(first_weights.back(grad_qkv, grad_first))
+        return grad_rows, (early, late)
+    small_halves = home.halves(small)
+
+    def small_half(which):
+        found_tables = first_weights.tables_back(which, rel_both[0], rel_both[1])
+        return jnp.concatenate([found_tables, small_halves[which].astype(F32).T], axis=1)
+
+    small_got = lax.ppermute(small_half(1).astype(BF16), "doc", flips(home.doc_size, 1))
+    row_halves = kept["row_halves"]
     sum_qk = CoreSum(
         home,
         [
-            (rows_turned, grad_qkv[:, : 2 * width]),
-            (tables.T, jnp.concatenate(rel_both, axis=1)),
+            (row_halves, grad_qkv[:, : 2 * width], 0),
+            (first_weights.tables, jnp.concatenate(rel_both, axis=1), 1),
         ],
     )
-    sum_v = CoreSum(home, [(rows_turned, grad_qkv[:, 2 * width :])])
-    grad_rows = grad_first + dot(grad_qkv, weights["qkv"], 1, 1)
+    sum_v = CoreSum(home, [(row_halves, grad_qkv[:, 2 * width :], 0)])
+    grad_rows = first_weights.back(grad_qkv, grad_first)
     grad_rows, sum_qk.got, sum_v.got, small_got = flight.tick(
         (grad_rows, sum_qk.got, sum_v.got, small_got)
     )
-    small_half = (small_kept.astype(F32) + small_got.astype(F32)).astype(BF16)
+    small_sum = (small_half(0) + small_got.astype(F32)).astype(BF16)
     half_qk, half_v = sum_qk.finish(), sum_v.finish()
     cut = 7 * width // 4
-    scatter_first, scatter_rest = Scatter(shape, 0), Scatter(shape, 1)
-    scatter_first.begin(1, half_qk[:, :cut])
-    scatter_rest.begin(
-        1,
-        jnp.concatenate(
-            [half_qk[:, cut:], half_v, small_half.reshape(half_qk.shape[0], -1)], axis=1
-        ),
-    )
-    flight.add(scatter_first)
-    flight.add(scatter_rest)
-    return grad_rows, (scatter_down, scatter_in, scatter_first, scatter_rest)
+    half_rest = jnp.concatenate([half_qk[:, cut:], half_v, small_sum], axis=1)
+
+    def by_chip(half):
+        return half.reshape(1, home.doc_size // 2, -1, half.shape[1])
+
+    late = Scatter(
+        home,
+        [[split_chips(by_chip(half_qk[:, :cut]), top)], [split_chips(by_chip(half_rest), 0)]],
+        False,
+    )
+    flight.add(late)
+    return grad_rows, (early, late)
 
 
 def collect(home, scatters, width, hidden):
-    scatter_down, scatter_in, scatter_first, scatter_rest = scatters
     devices = home.doc_size * home.ctx_size
-    down = scatter_down.result()
-    shard = down.shape[1]
-    down = down.reshape(-1, width)
-    both = scatter_in.result()[0]
-    grad_in = to_device_order(both[:, :hidden], devices, shard)
-    grad_out = both[:, hidden:]
-    rest = scatter_rest.result()[0]
-    first = scatter_first.result()[0]
-    qkv_left = 3 * width - first.shape[1]
-    qkv = jnp.concatenate([first, rest[:, :qkv_left]], axis=1)
-    small = rest[:, qkv_left:]
+    early, late = (item.result() for item in scatters)
+    shard = early.shape[0]
+    down = jnp.concatenate([early[:, at : at + width] for at in range(0, hidden, width)], axis=0)
+    grad_in = to_device_order(early[:, hidden : 2 * hidden], devices, shard)
+    grad_out = early[:, 2 * hidden :]
+    qkv = late[:, : 3 * width]
+    small = late[:, 3 * width :]
     table_cols = 2 * BUCKETS
     tables = small[:, :table_cols].T.reshape(2, BUCKETS, shard)
     rows = small[:, table_cols:].T
@@ -880,18 +1342,13 @@
     hidden = w_in.shape[2]
     home = Home(mesh_shape, local_docs, block_rows, width)
 
+    cut = 3 * width // 2
+    firsts = [
+        pack_first(w_qkv[layer], rel_tables[layer], ln_gains[layer], biases[layer], b_in[layer])
+        for layer in range(layer_count)
+    ]
     packed = [
-        pack_layer(
-            device_count,
-            w_qkv[layer],
-            w_out[layer],
-            w_in[layer],
-            w_down[layer],
-            rel_tables[layer],
-            ln_gains[layer],
-            biases[layer],
-            b_in[layer],
-        )
+        pack_rest(device_count, w_out[layer], w_in[layer], w_down[layer])
         for layer in range(layer_count)
     ]
 
@@ -918,32 +1375,69 @@
         home.rows,
     )
 
-    rows_low = home.to_home(layer_input)
-    current = rows_low.astype(F32)
-    all_weights = []
-    gathered = None
-    for layer in range(layer_count):
-        shard = packed[layer]
-        if gathered is not None:
-            shard, gathered = lax.optimization_barrier((shard, gathered))
-            all_weights[-1] = unpack_layer(gathered)
-        gathered = lax.all_gather(shard, BOTH, axis=0, tiled=True)
-        all_weights.append(unpack_layer(gathered))
+    arriving = home.to_home(layer_input)
+    rests = [lax.all_gather(packed[0], BOTH, axis=1, tiled=True)]
+
+    ahead = []
+
+    def fetch_next(values):
+        if len(rests) < layer_count:
+            shard, block, values = lax.optimization_barrier(
+                (packed[len(rests)], firsts[len(rests)], values)
+            )
+            rests.append(lax.all_gather(shard, BOTH, axis=1, tiled=True))
+            ahead.append(Gather(home, block, cut))
+        else:
+            own, values = lax.optimization_barrier((cotangent, values))
+            ahead.append(home.to_home(own))
+        flight.add(ahead[-1])
+        return values
+
+    first_weights = []
+    rest_weights = []
     kept_all = []
     outputs = []
+    flight = Flight()
+    ahead.append(Gather(home, firsts[0], cut))
+    gather = ahead[0]
+    arriving.got, gather.got, lookups = lax.optimization_barrier(
+        (arriving.got, gather.got, lookups)
+    )
+    rows_low = arriving.result()
+    current = rows_low.astype(F32)
     for layer in range(layer_count):
-        current, kept = layer_forward(home, current, rows_low, all_weights[layer], lookups)
+        first_weights.append(ahead[layer].finish())
+        current, kept, rest = layer_forward(
+            home,
+            flight,
+            current,
+            rows_low,
+            first_weights[layer],
+            rests[layer],
+            fetch_next,
+            lookups,
+        )
+        rest_weights.append(rest)
         rows_low = current.astype(BF16)
-        outputs.append(home.from_home(rows_low).astype(F32))
+        outputs.append(home.from_home(rows_low))
+        outputs[-1].hold = 1 if layer + 1 < layer_count else 2
+        flight.add(outputs[-1])
         kept_all.append(kept)
-    grad_rows = home.to_home(cotangent).astype(F32)
+    grad_rows = ahead[-1].result().astype(F32)
     scatters = [None] * layer_count
-    flight = Flight()
     for layer in reversed(range(layer_count)):
         grad_rows, scatters[layer] = layer_backward(
-            home, flight, grad_rows, kept_all[layer], all_weights[layer], lookups
-        )
-    grad_input = home.from_home(grad_rows.astype(BF16)).astype(F32)
+            home,
+            flight,
+            grad_rows,
+            kept_all[layer],
+            first_weights[layer],
+            rest_weights[layer],
+            lookups,
+            layer > 0,
+        )
+    grad_input = home.from_home(grad_rows.astype(BF16))
+    flight.add(grad_input)
     while flight.moving:
         flight.tick(())
     totals = [collect(home, item, width, hidden) for item in scatters]
@@ -951,7 +1445,7 @@
     def stack(member):
         return jnp.stack([totals[layer][member] for layer in range(layer_count)])
 
-    return (outputs[0], outputs[-1], grad_input) + tuple(stack(member) for member in range(8))
+    return tuple(item.result() for item in (outputs[0], outputs[-1], grad_input)) + tuple(stack(member) for member in range(8))
 
 
 def solution(mesh):

time: 1100 us -> 965 us (0.88)
  waiting for transfers between devices: 247 us -> 126 us
  matrix products: 215 us -> 152 us
  Pallas kernels: 269 us -> 331 us
  other arithmetic: 129 us -> 103 us
    all_gather x2, waiting for transfers between devices: 185 us -> 9.31 us  [the longest x1 9.31 us: fetch_next(): rests.append(lax.all_gather(shard, BOTH, axis=1, tiled=True))]
    ppermute x34 -> x39, waiting for transfers between devices: 39.8 us -> 104 us  [the longest x12 53.5 us: send(): lax.ppermute(value, *pair)]
    dot_general x58 -> x77, matrix products: 215 us -> 152 us  [dot(): lax.dot_general(left, right, (((left_axis,), (right_axis,)), ((), ())), p...]
    pallas_call x0 -> x12, Pallas kernels: none -> 61.4 us  [the longest x6 35.4 us: half_product(): pl.pallas_call(functools.partial(product_kernel, len(lefts), len(grads),...]
    convert_element_type x35 -> x19, other arithmetic: 52.8 us -> 22 us  [the longest x9 11.8 us: advance(): (kept.astype(F32) + got.astype(F32)).astype(BF16)]
    ppermute x34 -> x39, starting transfers between devices: 36 us -> 60.5 us  [the longest x12 23.9 us: send(): lax.ppermute(value, *pair)]
    ppermute x6, waiting for transfers between devices: 22.1 us -> 0.56 us  [from_home(): pieces.append(lax.ppermute(piece, BOTH, back))]
    ppermute x2, starting transfers between devices: 20.6 us -> 0.21 us  [fetch(): lax.ppermute(values, BOTH, self.ring_pairs(-shift))]
  transfers between devices with their start and end apart: 63 -> 63, of which waited for: 11 -> 18; matrix products, arithmetic and copies ran while one was open for 37% -> 32% of each run, Pallas kernels for 25% -> 33%
where the time goes in v3:
time: 965 us; the launch traced here: 958 us
  Pallas kernels  331 us (34%)
  matrix products  152 us (16%)
  local copies, waits for them, and re-layouts  135 us (14%)
  waiting for transfers between devices  126 us (13%)
  other arithmetic  103 us (11%)
  starting transfers between devices  92.7 us (10%)
  between operations  17.8 us (2%)
    pallas_call x4, Pallas kernels, attend_back(): pl.pallas_call(functools.partial(attend_back_kernel, chunks), grid=(count...  192 us
    dot_general x77, matrix products, dot(): lax.dot_general(left, right, (((left_axis,), (right_axis,)), ((), ())), p...  152 us
    pallas_call x2, Pallas kernels, attend(): pl.pallas_call(functools.partial(attend_kernel, chunks), grid=(pairs,), i...  77.9 us
    ppermute x12, waiting for transfers between devices, send(): lax.ppermute(value, *pair)  53.5 us
    unnamed x455, local copies, waits for them, and re-layouts  42.5 us
    ppermute x9, waiting for transfers between devices, send(): self.got.append(lax.ppermute(sent, 'ctx', flips(size, far)))  35.7 us
    pallas_call x6, Pallas kernels, half_product(): pl.pallas_call(functools.partial(product_kernel, len(lefts), len(grads),...  35.4 us
    ppermute x12, starting transfers between devices, send(): lax.ppermute(value, *pair)  23.9 us
  transfers between devices with their start and end apart: 63, of which 18 were waited for; matrix products, arithmetic and copies ran while one was open for 32% of the time, Pallas kernels for 33%

profile of v3, /device:TPU:0, one launch (start us, length us, event | category | flops | bytes accessed | tf_op | source)
XLA Modules:
  0.0 957.7 jit_solution(595703337307283911)
XLA Ops:
  42.4 8.4 collective-permute-done.1
  56.1 4.3 collective-permute-done.6
  73.8 17.0 %collective-permute-done.7 = bf16[2,4,32,1536]{3,2,1,0:T(8,128)(2,1)} collective-permute-done((bf16[2,4,32,1536]{3,2,1,0:T(8,128)(2,1)}, bf16[2,4,32,1536]{3,2,1,0:T(8,128)(2,1)}, u32[]{:S(2)}, u32[]{:S(2)}) %collective-permute-start.7) | collective-permute-done | bytes 786464 | tf_op jit(solution)/shard_map/ppermute | solution.py:822
  92.2 6.6 collective-permute-start.8
  104.8 6.4 collective-permute-start.11
  120.9 3.3 convolution_add_fusion.3
  137.3 3.2 collective-permute-start.13
  150.3 39.1 %attend.2 = (bf16[288,1024]{1,0:T(8,128)(2,1)S(1)}, bf16[16,288,640]{2,1,0:T(8,128)(2,1)S(1)}) custom-call(bf16[288,3072]{1,0:T(8,128)(2,1)S(1)} %fusion.q_ref.refs_0_.refs_2_, bf16[288,3072]{1,0:T(8,128)(2,1)S(1)} %fusion.q_ref.refs_0_.refs_2_, bf16[288,2048]{1,0:T(8,128)(2,1)S(1)} %collective-permute-done.12.refs_1_.refs_3_, ...), custom_call_target="tpu_custom_call" | custom-call | flops 3397386240 | bytes 8257536 | tf_op jit(solution)/shard_map/attend/pallas_call | solution.py:176
  200.2 4.6 multiply_convert_fusion.4
  220.2 22.6 %collective-permute-done.18 = bf16[2,4,32,1536]{3,2,1,0:T(8,128)(2,1)S(1)} collective-permute-done((bf16[2,4,32,1536]{3,2,1,0:T(8,128)(2,1)S(1)}, bf16[2,4,32,1536]{3,2,1,0:T(8,128)(2,1)S(1)}, u32[]{:S(2)}, u32[]{:S(2)}) %collective-permute-start.18) | collective-permute-done | bytes 786464 | tf_op jit(solution)/shard_map/ppermute | solution.py:822
  242.9 6.6 collective-permute-done.19
  262.2 3.3 fusion.214
  269.6 3.8 convolution_add_fusion.1
  293.6 38.9 %attend.3 = (bf16[288,1024]{1,0:T(8,128)(2,1)S(1)}, bf16[16,288,640]{2,1,0:T(8,128)(2,1)S(1)}) custom-call(bf16[288,3072]{1,0:T(8,128)(2,1)S(1)} %fusion.1.q_ref.refs_0_.refs_2_, bf16[288,3072]{1,0:T(8,128)(2,1)S(1)} %fusion.1.q_ref.refs_0_.refs_2_, bf16[288,2048]{1,0:T(8,128)(2,1)S(1)} %collective-permute-done.22.refs_1_.refs_3_, ...), custom_call_target="tpu_custom_call" | custom-call | flops 3397386240 | bytes 8257536 | tf_op jit(solution)/shard_map/attend/pallas_call | solution.py:176
  338.0 9.3 all-gather.5.cloned.1.call-done
  350.9 3.2 multiply_convert_fusion
  376.9 14.8 %panel_products.1 = bf16[1024,9216]{1,0:T(8,128)(2,1)} custom-call(bf16[288,1024]{1,0:T(8,128)(2,1)S(1)} %get-tuple-element.180.refs_0_, bf16[288,1024]{1,0:T(8,128)(2,1)S(1)} %get-tuple-element.181.refs_1_, bf16[288,1024]{1,0:T(8,128)(2,1)S(1)} %get-tuple-element.182.refs_2_, bf16[288,1024]{1,0:T(8,128)(2,1)S(1)} %get-tuple-element.183.refs_3_, ...), custom_call_target="tpu_custom_call" | custom-call | flops 5435817984 | bytes 18874368 | tf_op jit(solution)/shard_map/panel_products/pallas_call | solution.py:579
  395.1 3.2 fusion.105.refs_4_
  398.3 91.8 %attend_back.4 = (bf16[288,1024]{1,0:T(8,128)(2,1)}, bf16[2,2,288,1024]{3,2,1,0:T(8,128)(2,1)}, bf16[2,256,1024]{2,1,0:T(8,128)(2,1)}) custom-call(bf16[288,3072]{1,0:T(8,128)(2,1)} %copy-done.12, bf16[288,3072]{1,0:T(8,128)(2,1)} %copy-done.12, bf16[288,2048]{1,0:T(8,128)(2,1)} %copy-done.39, bf16[288,3072]{1,0:T(8,128)(2,1)} %copy-done.12, ...), custom_call_target="tpu_custom_call" | custom-call | flops 13589544960 | bytes 12976128 | tf_op jit(solution)/shard_map/attend_back/pallas_call | solution.py:349
  492.4 5.2 collective-permute-start.29
  508.3 3.1 convolution_add_fusion.8.other_ref
  521.0 5.1 half_product.6
  557.1 5.3 half_product.8
  563.8 4.6 fusion.155
  575.9 3.6 multiply_reduce_fusion.1
  581.8 3.1 half_product.9
  593.7 4.0 convolution_convert_fusion
  597.7 9.4 half_product.7
  607.2 4.0 fusion.106.refs_4_
  611.3 8.8 half_product.10
  627.1 3.4 pad_maximum_fusion
  637.1 3.7 half_product.11
  641.4 47.6 %attend_back.5 = (bf16[288,512]{1,0:T(8,128)(2,1)}, bf16[2,2,288,512]{3,2,1,0:T(8,128)(2,1)}, bf16[2,256,512]{2,1,0:T(8,128)(2,1)}) custom-call(bf16[288,3072]{1,0:T(8,128)(2,1)} %copy-done, bf16[288,3072]{1,0:T(8,128)(2,1)} %copy-done, bf16[288,2048]{1,0:T(8,128)(2,1)} %copy-done.2, bf16[288,3072]{1,0:T(8,128)(2,1)} %copy-done, ...), custom_call_target="tpu_custom_call" | custom-call | flops 6794772480 | bytes 6488064 | tf_op jit(solution)/shard_map/attend_back/pallas_call | solution.py:349
  709.9 3.1 reshape.575
  713.0 4.8 copy.139
  717.8 4.5 stack_reshape.19
  723.9 26.1 %attend_back.6 = (bf16[288,256]{1,0:T(8,128)(2,1)}, bf16[2,2,288,256]{3,2,1,0:T(8,128)(2,1)}, bf16[2,256,256]{2,1,0:T(8,128)(2,1)}) custom-call(bf16[288,3072]{1,0:T(8,128)(2,1)} %copy-done, bf16[288,3072]{1,0:T(8,128)(2,1)} %copy-done, bf16[288,2048]{1,0:T(8,128)(2,1)} %copy-done.2, bf16[288,3072]{1,0:T(8,128)(2,1)} %copy-done, ...), custom_call_target="tpu_custom_call" | custom-call | flops 3397386240 | bytes 3244032 | tf_op jit(solution)/shard_map/attend_back/pallas_call | solution.py:349
  764.7 26.2 %attend_back.7 = (bf16[288,256]{1,0:T(8,128)(2,1)}, bf16[2,2,288,256]{3,2,1,0:T(8,128)(2,1)}, bf16[2,256,256]{2,1,0:T(8,128)(2,1)}) custom-call(bf16[288,3072]{1,0:T(8,128)(2,1)} %copy-done, bf16[288,3072]{1,0:T(8,128)(2,1)} %copy-done, bf16[288,2048]{1,0:T(8,128)(2,1)} %copy-done.2, bf16[288,3072]{1,0:T(8,128)(2,1)} %copy-done, ...), custom_call_target="tpu_custom_call" | custom-call | flops 3397386240 | bytes 3244032 | tf_op jit(solution)/shard_map/attend_back/pallas_call | solution.py:349
  791.8 10.2 %collective-permute-done.38 = bf16[32,4096]{1,0:T(8,128)(2,1)S(1)} collective-permute-done((bf16[32,4096]{1,0:T(8,128)(2,1)S(1)}, bf16[32,4096]{1,0:T(8,128)(2,1)S(1)}, u32[]{:S(2)}, u32[]{:S(2)}) %collective-permute-start.38) | collective-permute-done | bytes 262176 | tf_op jit(solution)/shard_map/ppermute | solution.py:983
  802.0 6.8 collective-permute-done.40
  860.2 7.2 collective-permute-done.49
  881.5 4.0 collective-permute-start.52
  885.5 13.7 %collective-permute-start.53 = (bf16[144,1024]{1,0:T(8,128)(2,1)}, bf16[144,1024]{1,0:T(8,128)(2,1)}, u32[]{:S(2)}, u32[]{:S(2)}) collective-permute-start(bf16[144,1024]{1,0:T(8,128)(2,1)} %get-tuple-element.404), channel_id=1, source_target_pairs={{1,0},{0,1},{5,2},{4,3},{3,4},{2,5},{7,6},{6,7},{9,8},{8,9},{13,10... | collective-permute-start | bytes 884744 | tf_op jit(solution)/shard_map/ppermute | solution.py:696
  901.2 3.1 copy.138
  904.3 3.7 stack_reshape.18
  914.2 7.9 collective-permute-done.55
  924.7 4.4 collective-permute-start.56
  936.4 8.9 collective-permute-done.57
  (952 shorter events, 404.1 us)
Async XLA Ops:
  7.2 189.6 %all-gather.3.cloned.1.call-start = ((), (), s32[]{:S(2)}) async-start(), calls=%async_computation.2 | async-start | bytes 19464192 | tf_op jit(solution)/shard_map/all_gather | solution.py:1379
  12.9 334.5 %all-gather.5.cloned.1.call-start = ((), (), s32[]{:S(2)}) async-start(), calls=%async_computation.3 | async-start | bytes 19464192 | tf_op jit(solution)/shard_map/all_gather | solution.py:1388
  15.0 22.6 %collective-permute-start.2 = (bf16[1,32,3456]{2,1,0:T(8,128)(2,1)}, bf16[1,32,3456]{2,1,0:T(8,128)(2,1)}, u32[]{:S(2)}, u32[]{:S(2)}) collective-permute-start(bf16[1,32,3456]{2,1,0:T(8,128)(2,1)} %maximum_bitcast_fusion.2), channel_id=1, source_target_pairs={{0,1},{1,0},{2,3},{3,2},{4,5},{5,4},{6,7},{7,6},{8,9},{9,8},{10,11... | collective-permute-start | bytes 663560 | tf_op jit(solution)/shard_map/ppermute | solution.py:814
  18.0 22.4 %collective-permute-start.3 = (bf16[1,32,3456]{2,1,0:T(8,128)(2,1)}, bf16[1,32,3456]{2,1,0:T(8,128)(2,1)}, u32[]{:S(2)}, u32[]{:S(2)}) collective-permute-start(bf16[1,32,3456]{2,1,0:T(8,128)(2,1)} %maximum_bitcast_fusion.2), channel_id=1, source_target_pairs={{0,2},{1,3},{2,0},{3,1},{4,6},{5,7},{6,4},{7,5},{8,10},{9,11},{10,... | collective-permute-start | bytes 663560 | tf_op jit(solution)/shard_map/ppermute | solution.py:814
  20.6 21.8 %collective-permute-start.4 = (bf16[1,32,3456]{2,1,0:T(8,128)(2,1)}, bf16[1,32,3456]{2,1,0:T(8,128)(2,1)}, u32[]{:S(2)}, u32[]{:S(2)}) collective-permute-start(bf16[1,32,3456]{2,1,0:T(8,128)(2,1)} %maximum_bitcast_fusion.2), channel_id=1, source_target_pairs={{0,3},{1,2},{2,1},{3,0},{4,7},{5,6},{6,5},{7,4},{8,11},{9,10},{10,... | collective-permute-start | bytes 663560 | tf_op jit(solution)/shard_map/ppermute | solution.py:814
  21.6 20.8 %collective-permute-start = (bf16[144,1024]{1,0:T(8,128)(2,1)}, bf16[144,1024]{1,0:T(8,128)(2,1)S(1)}, u32[]{:S(2)}, u32[]{:S(2)}) collective-permute-start(bf16[144,1024]{1,0:T(8,128)(2,1)} %get-tuple-element.426), channel_id=1, source_target_pairs={{0,0},{1,1},{2,4},{3,5},{4,2},{5,3},{6,6},{7,7},{8,8},{9,9},{10,12... | collective-permute-start | bytes 884744 | tf_op jit(solution)/shard_map/ppermute | solution.py:678
  23.5 27.3 %collective-permute-start.1 = (bf16[144,1024]{1,0:T(8,128)(2,1)S(1)}, bf16[144,1024]{1,0:T(8,128)(2,1)S(1)}, u32[]{:S(2)}, u32[]{:S(2)}) collective-permute-start(bf16[144,1024]{1,0:T(8,128)(2,1)S(1)} %get-tuple-element.425), channel_id=1, source_target_pairs={{0,1},{1,0},{2,5},{3,4},{4,3},{5,2},{6,7},{7,6},{8,9},{9,8},{10,13... | collective-permute-start | bytes 884744 | tf_op jit(solution)/shard_map/ppermute | solution.py:678
  62.5 28.2 %collective-permute-start.7 = (bf16[2,4,32,1536]{3,2,1,0:T(8,128)(2,1)}, bf16[2,4,32,1536]{3,2,1,0:T(8,128)(2,1)}, u32[]{:S(2)}, u32[]{:S(2)}) collective-permute-start(bf16[2,4,32,1536]{3,2,1,0:T(8,128)(2,1)} %pad_maximum_fusion.15), channel_id=1, source_target_pairs={{0,16},{4,20},{8,24},{12,28},{16,0},{20,4},{24,8},{28,12},{1,17},{... | collective-permute-start | bytes 2359304 | tf_op jit(solution)/shard_map/ppermute | solution.py:822
  66.1 35.7 %collective-permute-start.10 = (bf16[2,4,32,1920]{3,2,1,0:T(8,128)(2,1)}, bf16[2,4,32,1920]{3,2,1,0:T(8,128)(2,1)}, u32[]{:S(2)}, u32[]{:S(2)}) collective-permute-start(bf16[2,4,32,1920]{3,2,1,0:T(8,128)(2,1)} %pad_maximum_fusion.9), channel_id=1, source_target_pairs={{0,8},{4,12},{8,0},{12,4},{16,24},{20,28},{24,16},{28,20},{1,9},{5... | collective-permute-start | bytes 2949128 | tf_op jit(solution)/shard_map/ppermute | solution.py:822
  92.2 28.7 %collective-permute-start.8 = (bf16[2,2,4,32,1536]{4,3,2,1,0:T(8,128)(2,1)S(1)}, bf16[2,2,4,32,1536]{4,3,2,1,0:T(8,128)(2,1)}, u32[]{:S(2)}, u32[]{:S(2)}) collective-permute-start(bf16[2,2,4,32,1536]{4,3,2,1,0:T(8,128)(2,1)S(1)} %pad_maximum_fusion.4), channel_id=1, source_target_pairs={{0,4},{4,0},{8,12},{12,8},{16,20},{20,16},{24,28},{28,24},{1,5},{5... | collective-permute-start | bytes 4718600 | tf_op jit(solution)/shard_map/ppermute | solution.py:822
  104.8 19.4 %collective-permute-start.11 = (bf16[2,2,4,32,1920]{4,3,2,0,1:T(8,128)(2,1)}, bf16[2,2,4,32,1920]{4,3,2,0,1:T(8,128)(2,1)}, u32[]{:S(2)}, u32[]{:S(2)}) collective-permute-start(bf16[2,2,4,32,1920]{4,3,2,0,1:T(8,128)(2,1)} %pad_maximum_fusion.1), channel_id=1, source_target_pairs={{0,4},{4,0},{8,12},{12,8},{16,20},{20,16},{24,28},{28,24},{1,5},{5... | collective-permute-start | bytes 5898248 | tf_op jit(solution)/shard_map/ppermute | solution.py:822
  132.9 508.5 %reduce-scatter.3.cloned.1.call-start = ((), (), s32[]{:S(2)}) async-start(), calls=%async_computation.4 | async-start | bytes 19464192 | tf_op jit(solution)/shard_map/reduce_scatter | solution.py:1024
  137.3 54.7 %collective-permute-start.13 = (bf16[1,32,3456]{2,1,0:T(8,128)(2,1)S(1)}, bf16[1,32,3456]{2,1,0:T(8,128)(2,1)S(1)}, u32[]{:S(2)}, u32[]{:S(2)}) collective-permute-start(bf16[1,32,3456]{2,1,0:T(8,128)(2,1)S(1)} %bitcast.702), channel_id=1, source_target_pairs={{0,1},{1,0},{2,3},{3,2},{4,5},{5,4},{6,7},{7,6},{8,9},{9,8},{10,11... | collective-permute-start | bytes 663560 | tf_op jit(solution)/shard_map/ppermute | solution.py:814
  140.6 51.4 %collective-permute-start.14 = (bf16[1,32,3456]{2,1,0:T(8,128)(2,1)S(1)}, bf16[1,32,3456]{2,1,0:T(8,128)(2,1)S(1)}, u32[]{:S(2)}, u32[]{:S(2)}) collective-permute-start(bf16[1,32,3456]{2,1,0:T(8,128)(2,1)S(1)} %bitcast.703), channel_id=1, source_target_pairs={{0,2},{1,3},{2,0},{3,1},{4,6},{5,7},{6,4},{7,5},{8,10},{9,11},{10,... | collective-permute-start | bytes 663560 | tf_op jit(solution)/shard_map/ppermute | solution.py:814
  141.5 50.6 %collective-permute-start.15 = (bf16[1,32,3456]{2,1,0:T(8,128)(2,1)S(1)}, bf16[1,32,3456]{2,1,0:T(8,128)(2,1)S(1)}, u32[]{:S(2)}, u32[]{:S(2)}) collective-permute-start(bf16[1,32,3456]{2,1,0:T(8,128)(2,1)S(1)} %bitcast.704), channel_id=1, source_target_pairs={{0,3},{1,2},{2,1},{3,0},{4,7},{5,6},{6,5},{7,4},{8,11},{9,10},{10,... | collective-permute-start | bytes 663560 | tf_op jit(solution)/shard_map/ppermute | solution.py:814
  193.0 19.1 %collective-permute-start.17 = (bf16[4,32,1920]{2,1,0:T(8,128)(2,1)}, bf16[4,32,1920]{2,1,0:T(8,128)(2,1)}, u32[]{:S(2)}, u32[]{:S(2)}) collective-permute-start(bf16[4,32,1920]{2,1,0:T(8,128)(2,1)} %pad_maximum_fusion.28), channel_id=1, source_target_pairs={{0,16},{4,20},{8,24},{12,28},{16,0},{20,4},{24,8},{28,12},{1,17},{... | collective-permute-start | bytes 1474568 | tf_op jit(solution)/shard_map/ppermute | solution.py:822
  213.5 36.0 %collective-permute-start.19 = (bf16[2,4,32,1920]{3,2,1,0:T(8,128)(2,1)S(1)}, bf16[2,4,32,1920]{3,2,1,0:T(8,128)(2,1)S(1)}, u32[]{:S(2)}, u32[]{:S(2)}) collective-permute-start(bf16[2,4,32,1920]{3,2,1,0:T(8,128)(2,1)S(1)} %pad_maximum_fusion.10), channel_id=1, source_target_pairs={{0,8},{4,12},{8,0},{12,4},{16,24},{20,28},{24,16},{28,20},{1,9},{5... | collective-permute-start | bytes 2949128 | tf_op jit(solution)/shard_map/ppermute | solution.py:822
  215.5 27.3 %collective-permute-start.18 = (bf16[2,4,32,1536]{3,2,1,0:T(8,128)(2,1)S(1)}, bf16[2,4,32,1536]{3,2,1,0:T(8,128)(2,1)S(1)}, u32[]{:S(2)}, u32[]{:S(2)}) collective-permute-start(bf16[2,4,32,1536]{3,2,1,0:T(8,128)(2,1)S(1)} %pad_maximum_fusion.16), channel_id=1, source_target_pairs={{0,16},{4,20},{8,24},{12,28},{16,0},{20,4},{24,8},{28,12},{1,17},{... | collective-permute-start | bytes 2359304 | tf_op jit(solution)/shard_map/ppermute | solution.py:822
  251.2 22.2 %collective-permute-start.21 = (bf16[2,2,4,32,1920]{4,3,2,0,1:T(8,128)(2,1)}, bf16[2,2,4,32,1920]{4,3,2,0,1:T(8,128)(2,1)}, u32[]{:S(2)}, u32[]{:S(2)}) collective-permute-start(bf16[2,2,4,32,1920]{4,3,2,0,1:T(8,128)(2,1)} %pad_maximum_fusion.2), channel_id=1, source_target_pairs={{0,4},{4,0},{8,12},{12,8},{16,20},{20,16},{24,28},{28,24},{1,5},{5... | collective-permute-start | bytes 5898248 | tf_op jit(solution)/shard_map/ppermute | solution.py:822
  281.7 53.4 %collective-permute-start.23 = (bf16[144,1024]{1,0:T(8,128)(2,1)S(1)}, bf16[144,1024]{1,0:T(8,128)(2,1)S(1)}, u32[]{:S(2)}, u32[]{:S(2)}) collective-permute-start(bf16[144,1024]{1,0:T(8,128)(2,1)S(1)} %get-tuple-element.422), channel_id=1, source_target_pairs={{0,0},{1,1},{4,2},{5,3},{2,4},{3,5},{6,6},{7,7},{8,8},{9,9},{12,10... | collective-permute-start | bytes 884744 | tf_op jit(solution)/shard_map/ppermute | solution.py:696
  282.4 53.5 %collective-permute-start.24 = (bf16[144,1024]{1,0:T(8,128)(2,1)S(1)}, bf16[144,1024]{1,0:T(8,128)(2,1)S(1)}, u32[]{:S(2)}, u32[]{:S(2)}) collective-permute-start(bf16[144,1024]{1,0:T(8,128)(2,1)S(1)} %get-tuple-element.421), channel_id=1, source_target_pairs={{1,0},{0,1},{5,2},{4,3},{3,4},{2,5},{7,6},{6,7},{9,8},{8,9},{13,10... | collective-permute-start | bytes 884744 | tf_op jit(solution)/shard_map/ppermute | solution.py:696
  283.0 53.6 %collective-permute-start.25 = (bf16[144,1024]{1,0:T(8,128)(2,1)S(1)}, bf16[144,1024]{1,0:T(8,128)(2,1)S(1)}, u32[]{:S(2)}, u32[]{:S(2)}) collective-permute-start(bf16[144,1024]{1,0:T(8,128)(2,1)S(1)} %get-tuple-element.420), channel_id=1, source_target_pairs={{0,0},{1,1},{2,4},{3,5},{4,2},{5,3},{6,6},{7,7},{8,8},{9,9},{10,12... | collective-permute-start | bytes 884744 | tf_op jit(solution)/shard_map/ppermute | solution.py:678
  283.7 53.6 %collective-permute-start.26 = (bf16[144,1024]{1,0:T(8,128)(2,1)S(1)}, bf16[144,1024]{1,0:T(8,128)(2,1)S(1)}, u32[]{:S(2)}, u32[]{:S(2)}) collective-permute-start(bf16[144,1024]{1,0:T(8,128)(2,1)S(1)} %get-tuple-element.419), channel_id=1, source_target_pairs={{0,1},{1,0},{2,5},{3,4},{4,3},{5,2},{6,7},{7,6},{8,9},{9,8},{10,13... | collective-permute-start | bytes 884744 | tf_op jit(solution)/shard_map/ppermute | solution.py:678
  391.7 554.3 %reduce-scatter.5.cloned.1.call-start = ((), (), s32[]{:S(2)}) async-start(), calls=%async_computation.5 | async-start | bytes 7299072 | tf_op jit(solution)/shard_map/reduce_scatter | solution.py:1024
  393.5 96.6 %collective-permute-start.27 = (bf16[144,1024]{1,0:T(8,128)(2,1)S(1)}, bf16[144,1024]{1,0:T(8,128)(2,1)}, u32[]{:S(2)}, u32[]{:S(2)}) collective-permute-start(bf16[144,1024]{1,0:T(8,128)(2,1)S(1)} %get-tuple-element.414), channel_id=1, source_target_pairs={{0,0},{1,1},{4,2},{5,3},{2,4},{3,5},{6,6},{7,7},{8,8},{9,9},{12,10... | collective-permute-start | bytes 884744 | tf_op jit(solution)/shard_map/ppermute | solution.py:696
  395.0 95.1 %collective-permute-start.28 = (bf16[144,1024]{1,0:T(8,128)(2,1)S(1)}, bf16[144,1024]{1,0:T(8,128)(2,1)}, u32[]{:S(2)}, u32[]{:S(2)}) collective-permute-start(bf16[144,1024]{1,0:T(8,128)(2,1)S(1)} %get-tuple-element.413), channel_id=1, source_target_pairs={{1,0},{0,1},{5,2},{4,3},{3,4},{2,5},{7,6},{6,7},{9,8},{8,9},{13,10... | collective-permute-start | bytes 884744 | tf_op jit(solution)/shard_map/ppermute | solution.py:696
  526.1 31.0 %collective-permute-start.30 = (bf16[4,4,128,1024]{3,2,1,0:T(8,128)(2,1)}, bf16[4,4,128,1024]{3,2,1,0:T(8,128)(2,1)}, u32[]{:S(2)}, u32[]{:S(2)}) collective-permute-start(bf16[4,4,128,1024]{3,2,1,0:T(8,128)(2,1)} %half_product.6), channel_id=1, source_target_pairs={{0,4},{4,0},{8,12},{12,8},{16,20},{20,16},{24,28},{28,24},{1,5},{5... | collective-permute-start | bytes 12582920 | tf_op jit(solution)/shard_map/ppermute | solution.py:1118
  562.4 48.8 %collective-permute-start.31 = (bf16[4,4,128,1024]{3,2,1,0:T(8,128)(2,1)}, bf16[4,4,128,1024]{3,2,1,0:T(8,128)(2,1)}, u32[]{:S(2)}, u32[]{:S(2)}) collective-permute-start(bf16[4,4,128,1024]{3,2,1,0:T(8,128)(2,1)} %half_product.8), channel_id=1, source_target_pairs={{0,4},{4,0},{8,12},{12,8},{16,20},{20,16},{24,28},{28,24},{1,5},{5... | collective-permute-start | bytes 12582920 | tf_op jit(solution)/shard_map/ppermute | solution.py:1118
  584.9 26.3 %collective-permute-start.32 = (bf16[1,4,128,1024]{3,2,1,0:T(8,128)(2,1)}, bf16[1,4,128,1024]{3,2,1,0:T(8,128)(2,1)}, u32[]{:S(2)}, u32[]{:S(2)}) collective-permute-start(bf16[1,4,128,1024]{3,2,1,0:T(8,128)(2,1)} %half_product.9), channel_id=1, source_target_pairs={{0,4},{4,0},{8,12},{12,8},{16,20},{20,16},{24,28},{28,24},{1,5},{5... | collective-permute-start | bytes 3145736 | tf_op jit(solution)/shard_map/ppermute | solution.py:1118
  620.1 68.9 %collective-permute-start.34 = (bf16[4,2,128,1024]{3,2,1,0:T(8,128)(2,1)}, bf16[4,2,128,1024]{3,2,1,0:T(8,128)(2,1)}, u32[]{:S(2)}, u32[]{:S(2)}) collective-permute-start(bf16[4,2,128,1024]{3,2,1,0:T(8,128)(2,1)} %get-tuple-element.219), channel_id=1, source_target_pairs={{0,8},{4,12},{8,0},{12,4},{16,24},{20,28},{24,16},{28,20},{1,9},{5... | collective-permute-start | bytes 6291464 | tf_op jit(solution)/shard_map/ppermute | solution.py:954
  621.7 67.3 %collective-permute-start.33 = (bf16[4,2,128,1024]{3,2,1,0:T(8,128)(2,1)}, bf16[4,2,128,1024]{3,2,1,0:T(8,128)(2,1)}, u32[]{:S(2)}, u32[]{:S(2)}) collective-permute-start(bf16[4,2,128,1024]{3,2,1,0:T(8,128)(2,1)} %get-tuple-element.217), channel_id=1, source_target_pairs={{0,16},{4,20},{8,24},{12,28},{16,0},{20,4},{24,8},{28,12},{1,17},{... | collective-permute-start | bytes 6291464 | tf_op jit(solution)/shard_map/ppermute | solution.py:954
  640.8 48.3 %collective-permute-start.35 = (bf16[1,2,128,1024]{3,2,1,0:T(8,128)(2,1)S(1)}, bf16[1,2,128,1024]{3,2,1,0:T(8,128)(2,1)S(1)}, u32[]{:S(2)}, u32[]{:S(2)}) collective-permute-start(bf16[1,2,128,1024]{3,2,1,0:T(8,128)(2,1)S(1)} %get-tuple-element.221), channel_id=1, source_target_pairs={{0,8},{4,12},{8,0},{12,4},{16,24},{20,28},{24,16},{28,20},{1,9},{5... | collective-permute-start | bytes 1572872 | tf_op jit(solution)/shard_map/ppermute | solution.py:954
  698.5 53.7 %collective-permute-start.37 = (bf16[5,1,128,1024]{3,2,1,0:T(8,128)(2,1)}, bf16[5,1,128,1024]{3,2,1,0:T(8,128)(2,1)}, u32[]{:S(2)}, u32[]{:S(2)}) collective-permute-start(bf16[5,1,128,1024]{3,2,1,0:T(8,128)(2,1)} %fusion.108), channel_id=1, source_target_pairs={{0,16},{4,20},{8,24},{12,28},{16,0},{20,4},{24,8},{28,12},{1,17},{... | collective-permute-start | bytes 3932168 | tf_op jit(solution)/shard_map/ppermute | solution.py:954
  703.0 49.2 %collective-permute-start.36 = (bf16[4,1,128,1024]{3,2,1,0:T(8,128)(2,1)}, bf16[4,1,128,1024]{3,2,1,0:T(8,128)(2,1)}, u32[]{:S(2)}, u32[]{:S(2)}) collective-permute-start(bf16[4,1,128,1024]{3,2,1,0:T(8,128)(2,1)} %constant_dynamic-slice_fusion.3), channel_id=1, source_target_pairs={{0,8},{4,12},{8,0},{12,4},{16,24},{20,28},{24,16},{28,20},{1,9},{5... | collective-permute-start | bytes 3145736 | tf_op jit(solution)/shard_map/ppermute | solution.py:954
  705.3 44.7 %collective-permute-start.41 = (bf16[2,288,512]{2,1,0:T(8,128)(2,1)}, bf16[2,288,512]{2,1,0:T(8,128)(2,1)}, u32[]{:S(2)}, u32[]{:S(2)}) collective-permute-start(bf16[2,288,512]{2,1,0:T(8,128)(2,1)} %slice_bitcast_fusion.153), channel_id=1, source_target_pairs={{0,4},{1,5},{2,6},{3,7},{4,0},{5,1},{6,2},{7,3},{8,12},{9,13},{10,... | collective-permute-start | bytes 1769480 | tf_op jit(solution)/shard_map/ppermute | solution.py:755
  755.3 100.5 %collective-permute-start.47 = (bf16[32,5120]{1,0:T(8,128)(2,1)}, bf16[32,5120]{1,0:T(8,128)(2,1)}, u32[]{:S(2)}, u32[]{:S(2)}) collective-permute-start(bf16[32,5120]{1,0:T(8,128)(2,1)} %get-tuple-element.358), channel_id=1, source_target_pairs={{0,1},{1,0},{2,3},{3,2},{4,5},{5,4},{6,7},{7,6},{8,9},{9,8},{10,11... | collective-permute-start | bytes 983048 | tf_op jit(solution)/shard_map/ppermute | solution.py:983
  755.7 104.5 %collective-permute-start.48 = (bf16[32,5120]{1,0:T(8,128)(2,1)}, bf16[32,5120]{1,0:T(8,128)(2,1)}, u32[]{:S(2)}, u32[]{:S(2)}) collective-permute-start(bf16[32,5120]{1,0:T(8,128)(2,1)} %get-tuple-element.357), channel_id=1, source_target_pairs={{0,2},{1,3},{2,0},{3,1},{4,6},{5,7},{6,4},{7,5},{8,10},{9,11},{10,... | collective-permute-start | bytes 983048 | tf_op jit(solution)/shard_map/ppermute | solution.py:983
  759.5 42.4 %collective-permute-start.38 = (bf16[32,4096]{1,0:T(8,128)(2,1)S(1)}, bf16[32,4096]{1,0:T(8,128)(2,1)S(1)}, u32[]{:S(2)}, u32[]{:S(2)}) collective-permute-start(bf16[32,4096]{1,0:T(8,128)(2,1)S(1)} %get-tuple-element.368), channel_id=1, source_target_pairs={{0,1},{1,0},{2,3},{3,2},{4,5},{5,4},{6,7},{7,6},{8,9},{9,8},{10,11... | collective-permute-start | bytes 786440 | tf_op jit(solution)/shard_map/ppermute | solution.py:983
  760.1 41.9 %collective-permute-start.39 = (bf16[32,4096]{1,0:T(8,128)(2,1)S(1)}, bf16[32,4096]{1,0:T(8,128)(2,1)S(1)}, u32[]{:S(2)}, u32[]{:S(2)}) collective-permute-start(bf16[32,4096]{1,0:T(8,128)(2,1)S(1)} %get-tuple-element.367), channel_id=1, source_target_pairs={{0,2},{1,3},{2,0},{3,1},{4,6},{5,7},{6,4},{7,5},{8,10},{9,11},{10,... | collective-permute-start | bytes 786440 | tf_op jit(solution)/shard_map/ppermute | solution.py:983
  762.2 46.5 %collective-permute-start.40 = (bf16[32,4096]{1,0:T(8,128)(2,1)S(1)}, bf16[32,4096]{1,0:T(8,128)(2,1)S(1)}, u32[]{:S(2)}, u32[]{:S(2)}) collective-permute-start(bf16[32,4096]{1,0:T(8,128)(2,1)S(1)} %get-tuple-element.366), channel_id=1, source_target_pairs={{0,3},{1,2},{2,1},{3,0},{4,7},{5,6},{6,5},{7,4},{8,11},{9,10},{10,... | collective-permute-start | bytes 786440 | tf_op jit(solution)/shard_map/ppermute | solution.py:983
  801.9 20.9 %collective-permute-start.42 = (bf16[2,288,256]{2,1,0:T(8,128)(2,1)S(1)}, bf16[2,288,256]{2,1,0:T(8,128)(2,1)S(1)}, u32[]{:S(2)}, u32[]{:S(2)}) collective-permute-start(bf16[2,288,256]{2,1,0:T(8,128)(2,1)S(1)} %slice_bitcast_fusion.161), channel_id=1, source_target_pairs={{0,4},{1,5},{2,6},{3,7},{4,0},{5,1},{6,2},{7,3},{8,12},{9,13},{10,... | collective-permute-start | bytes 884744 | tf_op jit(solution)/shard_map/ppermute | solution.py:755
  843.4 24.0 %collective-permute-start.44 = (bf16[512,2048]{1,0:T(8,128)(2,1)}, bf16[512,2048]{1,0:T(8,128)(2,1)}, u32[]{:S(2)}, u32[]{:S(2)}) collective-permute-start(bf16[512,2048]{1,0:T(8,128)(2,1)} %add_convert_fusion.2), channel_id=1, source_target_pairs={{0,4},{4,0},{8,12},{12,8},{16,20},{20,16},{24,28},{28,24},{1,5},{5... | collective-permute-start | bytes 6291464 | tf_op jit(solution)/shard_map/ppermute | solution.py:1140
  844.6 22.7 %collective-permute-start.46 = (bf16[512,384]{1,0:T(8,128)(2,1)}, bf16[512,384]{1,0:T(8,128)(2,1)}, u32[]{:S(2)}, u32[]{:S(2)}) collective-permute-start(bf16[512,384]{1,0:T(8,128)(2,1)} %pad_maximum_fusion.40), channel_id=1, source_target_pairs={{0,4},{4,0},{8,12},{12,8},{16,20},{20,16},{24,28},{28,24},{1,5},{5... | collective-permute-start | bytes 1179656 | tf_op jit(solution)/shard_map/ppermute | solution.py:1275
  846.4 20.9 %collective-permute-start.45 = (bf16[512,1024]{1,0:T(8,128)(2,1)}, bf16[512,1024]{1,0:T(8,128)(2,1)}, u32[]{:S(2)}, u32[]{:S(2)}) collective-permute-start(bf16[512,1024]{1,0:T(8,128)(2,1)} %convolution_convert_fusion.1), channel_id=1, source_target_pairs={{0,4},{4,0},{8,12},{12,8},{16,20},{20,16},{24,28},{28,24},{1,5},{5... | collective-permute-start | bytes 3145736 | tf_op jit(solution)/shard_map/ppermute | solution.py:1140
  876.7 32.7 %collective-permute-start.51 = (bf16[1,2,128,1664]{3,2,1,0:T(8,128)(2,1)}, bf16[1,2,128,1664]{3,2,1,0:T(8,128)(2,1)}, u32[]{:S(2)}, u32[]{:S(2)}) collective-permute-start(bf16[1,2,128,1664]{3,2,1,0:T(8,128)(2,1)} %dynamic-slice_bitcast_fusion.1), channel_id=1, source_target_pairs={{0,8},{4,12},{8,0},{12,4},{16,24},{20,28},{24,16},{28,20},{1,9},{5... | collective-permute-start | bytes 2555912 | tf_op jit(solution)/shard_map/ppermute | solution.py:954
  879.0 30.4 %collective-permute-start.50 = (bf16[1,2,128,1792]{3,2,1,0:T(8,128)(2,1)}, bf16[1,2,128,1792]{3,2,1,0:T(8,128)(2,1)}, u32[]{:S(2)}, u32[]{:S(2)}) collective-permute-start(bf16[1,2,128,1792]{3,2,1,0:T(8,128)(2,1)} %dynamic-slice_bitcast_fusion), channel_id=1, source_target_pairs={{0,16},{4,20},{8,24},{12,28},{16,0},{20,4},{24,8},{28,12},{1,17},{... | collective-permute-start | bytes 2752520 | tf_op jit(solution)/shard_map/ppermute | solution.py:954
  881.5 27.3 %collective-permute-start.52 = (bf16[144,1024]{1,0:T(8,128)(2,1)}, bf16[144,1024]{1,0:T(8,128)(2,1)}, u32[]{:S(2)}, u32[]{:S(2)}) collective-permute-start(bf16[144,1024]{1,0:T(8,128)(2,1)} %get-tuple-element.405), channel_id=1, source_target_pairs={{0,0},{1,1},{4,2},{5,3},{2,4},{3,5},{6,6},{7,7},{8,8},{9,9},{12,10... | collective-permute-start | bytes 884744 | tf_op jit(solution)/shard_map/ppermute | solution.py:696
  885.5 23.8 %collective-permute-start.53 = (bf16[144,1024]{1,0:T(8,128)(2,1)}, bf16[144,1024]{1,0:T(8,128)(2,1)}, u32[]{:S(2)}, u32[]{:S(2)}) collective-permute-start(bf16[144,1024]{1,0:T(8,128)(2,1)} %get-tuple-element.404), channel_id=1, source_target_pairs={{1,0},{0,1},{5,2},{4,3},{3,4},{2,5},{7,6},{6,7},{9,8},{8,9},{13,10... | collective-permute-start | bytes 884744 | tf_op jit(solution)/shard_map/ppermute | solution.py:696
  (234 other events, 2165.0 us)
Sparse Core Ops, SparseCore 0:
  13.0 175.6 all-gather.2
  192.3 154.9 all-gather.4
  391.8 207.3 reduce-scatter.2
  705.4 136.9 reduce-scatter.4

commit v4 on v3

--- a/solution.py
+++ b/solution.py
@@ -1195,13 +1195,13 @@
         )
         while flight.waiting:
             grad_mixed = flight.waiting.pop(0).start(grad_mixed)
-        early = Scatter(home, [[halves_down], [sum_in.finish(), sum_out.finish()]], True)
+        early = Scatter(home, [[halves_down], [sum_in.finish(), sum_out.finish()]], False)
         flight.add(early)
 
     pairs = width // PAIR
     found = []
     moved = []
-    cuts = [0, pairs] if offload else [0, pairs // 2, 3 * pairs // 4, pairs]
+    cuts = [0, pairs] if offload else [0, pairs // 2, pairs]
     for first, count in zip(cuts, [after - at for at, after in zip(cuts, cuts[1:])]):
         grad_query, grad_kv, grad_rel = attend_back(
             kept["qkv"],

time: 965 us -> 940 us (0.974)
  waiting for transfers between devices: 126 us -> 114 us
    ppermute x9 -> x6, waiting for transfers between devices: 35.7 us -> 24.4 us  [send(): self.got.append(lax.ppermute(sent, 'ctx', flips(size, far)))]
    pallas_call x4 -> x3, Pallas kernels: 192 us -> 188 us  [attend_back(): pl.pallas_call(functools.partial(attend_back_kernel, chunks), grid=(count...]
    unnamed x455 -> x399, local copies, waits for them, and re-layouts: 42.5 us -> 40.1 us
  transfers between devices with their start and end apart: 63 -> 59, of which waited for: 18 -> 17; matrix products, arithmetic and copies ran while one was open for 32% -> 33% of each run, Pallas kernels for 33% -> 33%
where the time goes in v4:
time: 940 us; the launch traced here: 933 us
  Pallas kernels  323 us (34%)
  matrix products  154 us (16%)
  local copies, waits for them, and re-layouts  128 us (14%)
  waiting for transfers between devices  114 us (12%)
  other arithmetic  106 us (11%)
  starting transfers between devices  90.1 us (10%)
  between operations  17.6 us (2%)
    pallas_call x3, Pallas kernels, attend_back(): pl.pallas_call(functools.partial(attend_back_kernel, chunks), grid=(count...  188 us
    dot_general x77, matrix products, dot(): lax.dot_general(left, right, (((left_axis,), (right_axis,)), ((), ())), p...  154 us
    pallas_call x2, Pallas kernels, attend(): pl.pallas_call(functools.partial(attend_kernel, chunks), grid=(pairs,), i...  78.1 us
    ppermute x12, waiting for transfers between devices, send(): lax.ppermute(value, *pair)  54 us
    unnamed x399, local copies, waits for them, and re-layouts  40.1 us
    pallas_call x6, Pallas kernels, half_product(): pl.pallas_call(functools.partial(product_kernel, len(lefts), len(grads),...  31.5 us
    ppermute x12, starting transfers between devices, send(): lax.ppermute(value, *pair)  26 us
    ppermute x6, waiting for transfers between devices, send(): self.got.append(lax.ppermute(sent, 'ctx', flips(size, far)))  24.4 us
  transfers between devices with their start and end apart: 59, of which 17 were waited for; matrix products, arithmetic and copies ran while one was open for 33% of the time, Pallas kernels for 33%

profile of v4, /device:TPU:0, one launch (start us, length us, event | category | flops | bytes accessed | tf_op | source)
XLA Modules:
  0.0 933.0 jit_solution(2106844638705450973)
XLA Ops:
  37.1 3.4 collective-permute-done.3
  43.4 7.7 collective-permute-done.1
  56.1 4.2 collective-permute-done.6
  71.1 17.1 %collective-permute-done.7 = bf16[2,4,32,1536]{3,2,1,0:T(8,128)(2,1)} collective-permute-done((bf16[2,4,32,1536]{3,2,1,0:T(8,128)(2,1)}, bf16[2,4,32,1536]{3,2,1,0:T(8,128)(2,1)}, u32[]{:S(2)}, u32[]{:S(2)}) %collective-permute-start.7) | collective-permute-done | bytes 786464 | tf_op jit(solution)/shard_map/ppermute | solution.py:822
  89.8 8.1 collective-permute-start.8
  97.9 4.4 collective-permute-done.10
  105.2 6.5 collective-permute-start.11
  121.9 3.3 convolution_add_fusion.3
  137.4 3.2 collective-permute-start.13
  150.5 39.2 %attend.2 = (bf16[288,1024]{1,0:T(8,128)(2,1)S(1)}, bf16[16,288,640]{2,1,0:T(8,128)(2,1)S(1)}) custom-call(bf16[288,3072]{1,0:T(8,128)(2,1)S(1)} %fusion.q_ref.refs_0_.refs_2_, bf16[288,3072]{1,0:T(8,128)(2,1)S(1)} %fusion.q_ref.refs_0_.refs_2_, bf16[288,2048]{1,0:T(8,128)(2,1)S(1)} %collective-permute-done.12.refs_1_.refs_3_, ...), custom_call_target="tpu_custom_call" | custom-call | flops 3397386240 | bytes 8257536 | tf_op jit(solution)/shard_map/attend/pallas_call | solution.py:176
  200.6 4.5 multiply_convert_fusion.4
  221.3 21.5 %collective-permute-done.18 = bf16[2,4,32,1536]{3,2,1,0:T(8,128)(2,1)S(1)} collective-permute-done((bf16[2,4,32,1536]{3,2,1,0:T(8,128)(2,1)S(1)}, bf16[2,4,32,1536]{3,2,1,0:T(8,128)(2,1)S(1)}, u32[]{:S(2)}, u32[]{:S(2)}) %collective-permute-start.18) | collective-permute-done | bytes 786464 | tf_op jit(solution)/shard_map/ppermute | solution.py:822
  242.9 6.4 collective-permute-done.19
  252.9 3.1 copy.122
  262.0 3.3 fusion.213
  269.3 3.7 convolution_add_fusion.1
  293.4 38.9 %attend.3 = (bf16[288,1024]{1,0:T(8,128)(2,1)S(1)}, bf16[16,288,640]{2,1,0:T(8,128)(2,1)S(1)}) custom-call(bf16[288,3072]{1,0:T(8,128)(2,1)S(1)} %fusion.1.q_ref.refs_0_.refs_2_, bf16[288,3072]{1,0:T(8,128)(2,1)S(1)} %fusion.1.q_ref.refs_0_.refs_2_, bf16[288,2048]{1,0:T(8,128)(2,1)S(1)} %collective-permute-done.22.refs_1_.refs_3_, ...), custom_call_target="tpu_custom_call" | custom-call | flops 3397386240 | bytes 8257536 | tf_op jit(solution)/shard_map/attend/pallas_call | solution.py:176
  337.1 10.1 %all-gather.5.cloned.1.call-done = bf16[9,1024,1024]{2,1,0:T(8,128)(2,1)} async-done(((bf16[9,32,1024]{2,1,0:T(8,128)(2,1)}), bf16[9,1024,1024]{2,1,0:T(8,128)(2,1)}) %all-gather.5.cloned.1.call-update) | async-done | bytes 18874384 | tf_op jit(solution)/shard_map/all_gather | solution.py:1388
  347.2 3.1 fusion.297
  350.9 3.2 multiply_convert_fusion
  376.8 14.8 %panel_products.1 = bf16[1024,9216]{1,0:T(8,128)(2,1)} custom-call(bf16[288,1024]{1,0:T(8,128)(2,1)S(1)} %get-tuple-element.170.refs_0_, bf16[288,1024]{1,0:T(8,128)(2,1)S(1)} %get-tuple-element.171.refs_1_, bf16[288,1024]{1,0:T(8,128)(2,1)S(1)} %get-tuple-element.172.refs_2_, bf16[288,1024]{1,0:T(8,128)(2,1)S(1)} %get-tuple-element.173.refs_3_, ...), custom_call_target="tpu_custom_call" | custom-call | flops 5435817984 | bytes 18874368 | tf_op jit(solution)/shard_map/panel_products/pallas_call | solution.py:579
  395.5 3.2 fusion.105.refs_4_
  398.8 91.7 %attend_back.3 = (bf16[288,1024]{1,0:T(8,128)(2,1)}, bf16[2,2,288,1024]{3,2,1,0:T(8,128)(2,1)}, bf16[2,256,1024]{2,1,0:T(8,128)(2,1)}) custom-call(bf16[288,3072]{1,0:T(8,128)(2,1)} %copy-done.6, bf16[288,3072]{1,0:T(8,128)(2,1)} %copy-done.6, bf16[288,2048]{1,0:T(8,128)(2,1)} %copy-done.39, bf16[288,3072]{1,0:T(8,128)(2,1)} %copy-done.6, ...), custom_call_target="tpu_custom_call" | custom-call | flops 13589544960 | bytes 12976128 | tf_op jit(solution)/shard_map/attend_back/pallas_call | solution.py:349
  492.9 4.8 collective-permute-start.29
  520.8 5.2 half_product.6
  566.3 4.3 half_product.8
  571.6 4.6 fusion.158
  584.0 3.5 multiply_reduce_fusion.1
  589.9 3.1 half_product.9
  593.4 7.9 add_convert_fusion
  601.4 9.0 half_product.7
  610.3 4.0 fusion.106.refs_4_
  614.4 7.9 half_product.10
  634.4 3.4 pad_maximum_fusion
  652.9 47.7 %attend_back.4 = (bf16[288,512]{1,0:T(8,128)(2,1)}, bf16[2,2,288,512]{3,2,1,0:T(8,128)(2,1)}, bf16[2,256,512]{2,1,0:T(8,128)(2,1)}) custom-call(bf16[288,3072]{1,0:T(8,128)(2,1)} %copy-done.5, bf16[288,3072]{1,0:T(8,128)(2,1)} %copy-done.5, bf16[288,2048]{1,0:T(8,128)(2,1)} %copy-done.38, bf16[288,3072]{1,0:T(8,128)(2,1)} %copy-done.5, ...), custom_call_target="tpu_custom_call" | custom-call | flops 6794772480 | bytes 6488064 | tf_op jit(solution)/shard_map/attend_back/pallas_call | solution.py:349
  716.5 3.2 reshape.570
  719.7 4.8 copy.139
  724.4 3.7 stack_reshape.19
  730.0 48.2 %attend_back.5 = (bf16[288,512]{1,0:T(8,128)(2,1)}, bf16[2,2,288,512]{3,2,1,0:T(8,128)(2,1)}, bf16[2,256,512]{2,1,0:T(8,128)(2,1)}) custom-call(bf16[288,3072]{1,0:T(8,128)(2,1)} %copy-done.5, bf16[288,3072]{1,0:T(8,128)(2,1)} %copy-done.5, bf16[288,2048]{1,0:T(8,128)(2,1)} %copy-done.38, bf16[288,3072]{1,0:T(8,128)(2,1)} %copy-done.5, ...), custom_call_target="tpu_custom_call" | custom-call | flops 6794772480 | bytes 6488064 | tf_op jit(solution)/shard_map/attend_back/pallas_call | solution.py:349
  831.7 9.8 %collective-permute-done.44 = bf16[32,9216]{1,0:T(8,128)(2,1)} collective-permute-done((bf16[32,9216]{1,0:T(8,128)(2,1)}, bf16[32,9216]{1,0:T(8,128)(2,1)}, u32[]{:S(2)}, u32[]{:S(2)}) %collective-permute-start.44) | collective-permute-done | bytes 589856 | tf_op jit(solution)/shard_map/ppermute | solution.py:983
  853.7 3.8 collective-permute-start.48
  857.5 15.6 %collective-permute-start.49 = (bf16[144,1024]{1,0:T(8,128)(2,1)}, bf16[144,1024]{1,0:T(8,128)(2,1)}, u32[]{:S(2)}, u32[]{:S(2)}) collective-permute-start(bf16[144,1024]{1,0:T(8,128)(2,1)} %get-tuple-element.386), channel_id=1, source_target_pairs={{1,0},{0,1},{5,2},{4,3},{3,4},{2,5},{7,6},{6,7},{9,8},{8,9},{13,10... | collective-permute-start | bytes 884744 | tf_op jit(solution)/shard_map/ppermute | solution.py:696
  877.2 3.1 copy.138
  880.3 3.7 stack_reshape.18
  892.7 6.0 collective-permute-done.51
  898.7 3.4 collective-permute-done.50
  909.0 5.1 collective-permute-done.52
  914.1 6.5 collective-permute-done.53
  (876 shorter events, 388.5 us)
Async XLA Ops:
  7.2 190.1 %all-gather.3.cloned.1.call-start = ((), (), s32[]{:S(2)}) async-start(), calls=%async_computation.2 | async-start | bytes 19464192 | tf_op jit(solution)/shard_map/all_gather | solution.py:1379
  13.2 334.0 %all-gather.5.cloned.1.call-start = ((), (), s32[]{:S(2)}) async-start(), calls=%async_computation.3 | async-start | bytes 19464192 | tf_op jit(solution)/shard_map/all_gather | solution.py:1388
  15.2 21.9 %collective-permute-start.2 = (bf16[1,32,3456]{2,1,0:T(8,128)(2,1)}, bf16[1,32,3456]{2,1,0:T(8,128)(2,1)S(1)}, u32[]{:S(2)}, u32[]{:S(2)}) collective-permute-start(bf16[1,32,3456]{2,1,0:T(8,128)(2,1)} %maximum_bitcast_fusion.2), channel_id=1, source_target_pairs={{0,1},{1,0},{2,3},{3,2},{4,5},{5,4},{6,7},{7,6},{8,9},{9,8},{10,11... | collective-permute-start | bytes 663560 | tf_op jit(solution)/shard_map/ppermute | solution.py:814
  18.2 22.3 %collective-permute-start.3 = (bf16[1,32,3456]{2,1,0:T(8,128)(2,1)}, bf16[1,32,3456]{2,1,0:T(8,128)(2,1)}, u32[]{:S(2)}, u32[]{:S(2)}) collective-permute-start(bf16[1,32,3456]{2,1,0:T(8,128)(2,1)} %maximum_bitcast_fusion.2), channel_id=1, source_target_pairs={{0,2},{1,3},{2,0},{3,1},{4,6},{5,7},{6,4},{7,5},{8,10},{9,11},{10,... | collective-permute-start | bytes 663560 | tf_op jit(solution)/shard_map/ppermute | solution.py:814
  20.8 21.8 %collective-permute-start.4 = (bf16[1,32,3456]{2,1,0:T(8,128)(2,1)}, bf16[1,32,3456]{2,1,0:T(8,128)(2,1)}, u32[]{:S(2)}, u32[]{:S(2)}) collective-permute-start(bf16[1,32,3456]{2,1,0:T(8,128)(2,1)} %maximum_bitcast_fusion.2), channel_id=1, source_target_pairs={{0,3},{1,2},{2,1},{3,0},{4,7},{5,6},{6,5},{7,4},{8,11},{9,10},{10,... | collective-permute-start | bytes 663560 | tf_op jit(solution)/shard_map/ppermute | solution.py:814
  21.2 21.5 %collective-permute-start = (bf16[144,1024]{1,0:T(8,128)(2,1)S(1)}, bf16[144,1024]{1,0:T(8,128)(2,1)S(1)}, u32[]{:S(2)}, u32[]{:S(2)}) collective-permute-start(bf16[144,1024]{1,0:T(8,128)(2,1)S(1)} %get-tuple-element.407), channel_id=1, source_target_pairs={{0,0},{1,1},{2,4},{3,5},{4,2},{5,3},{6,6},{7,7},{8,8},{9,9},{10,12... | collective-permute-start | bytes 884744 | tf_op jit(solution)/shard_map/ppermute | solution.py:678
  22.2 28.9 %collective-permute-start.1 = (bf16[144,1024]{1,0:T(8,128)(2,1)S(1)}, bf16[144,1024]{1,0:T(8,128)(2,1)}, u32[]{:S(2)}, u32[]{:S(2)}) collective-permute-start(bf16[144,1024]{1,0:T(8,128)(2,1)S(1)} %get-tuple-element.406), channel_id=1, source_target_pairs={{0,1},{1,0},{2,5},{3,4},{4,3},{5,2},{6,7},{7,6},{8,9},{9,8},{10,13... | collective-permute-start | bytes 884744 | tf_op jit(solution)/shard_map/ppermute | solution.py:678
  61.5 26.8 %collective-permute-start.7 = (bf16[2,4,32,1536]{3,2,1,0:T(8,128)(2,1)}, bf16[2,4,32,1536]{3,2,1,0:T(8,128)(2,1)}, u32[]{:S(2)}, u32[]{:S(2)}) collective-permute-start(bf16[2,4,32,1536]{3,2,1,0:T(8,128)(2,1)} %pad_maximum_fusion.17), channel_id=1, source_target_pairs={{0,16},{4,20},{8,24},{12,28},{16,0},{20,4},{24,8},{28,12},{1,17},{... | collective-permute-start | bytes 2359304 | tf_op jit(solution)/shard_map/ppermute | solution.py:822
  64.7 37.6 %collective-permute-start.10 = (bf16[2,4,32,1920]{3,2,1,0:T(8,128)(2,1)}, bf16[2,4,32,1920]{3,2,1,0:T(8,128)(2,1)}, u32[]{:S(2)}, u32[]{:S(2)}) collective-permute-start(bf16[2,4,32,1920]{3,2,1,0:T(8,128)(2,1)} %pad_maximum_fusion.10), channel_id=1, source_target_pairs={{0,8},{4,12},{8,0},{12,4},{16,24},{20,28},{24,16},{28,20},{1,9},{5... | collective-permute-start | bytes 2949128 | tf_op jit(solution)/shard_map/ppermute | solution.py:822
  89.8 32.1 %collective-permute-start.8 = (bf16[2,2,4,32,1536]{4,3,2,1,0:T(8,128)(2,1)S(1)}, bf16[2,2,4,32,1536]{4,3,2,1,0:T(8,128)(2,1)}, u32[]{:S(2)}, u32[]{:S(2)}) collective-permute-start(bf16[2,2,4,32,1536]{4,3,2,1,0:T(8,128)(2,1)S(1)} %pad_maximum_fusion.4), channel_id=1, source_target_pairs={{0,4},{4,0},{8,12},{12,8},{16,20},{20,16},{24,28},{28,24},{1,5},{5... | collective-permute-start | bytes 4718600 | tf_op jit(solution)/shard_map/ppermute | solution.py:822
  105.2 20.0 %collective-permute-start.11 = (bf16[2,2,4,32,1920]{4,3,2,0,1:T(8,128)(2,1)}, bf16[2,2,4,32,1920]{4,3,2,0,1:T(8,128)(2,1)}, u32[]{:S(2)}, u32[]{:S(2)}) collective-permute-start(bf16[2,2,4,32,1920]{4,3,2,0,1:T(8,128)(2,1)} %pad_maximum_fusion.1), channel_id=1, source_target_pairs={{0,4},{4,0},{8,12},{12,8},{16,20},{20,16},{24,28},{28,24},{1,5},{5... | collective-permute-start | bytes 5898248 | tf_op jit(solution)/shard_map/ppermute | solution.py:822
  133.0 516.7 %reduce-scatter.3.cloned.1.call-start = ((), (), s32[]{:S(2)}) async-start(), calls=%async_computation.4 | async-start | bytes 19464192 | tf_op jit(solution)/shard_map/reduce_scatter | solution.py:1024
  137.4 54.9 %collective-permute-start.13 = (bf16[1,32,3456]{2,1,0:T(8,128)(2,1)S(1)}, bf16[1,32,3456]{2,1,0:T(8,128)(2,1)S(1)}, u32[]{:S(2)}, u32[]{:S(2)}) collective-permute-start(bf16[1,32,3456]{2,1,0:T(8,128)(2,1)S(1)} %bitcast.640), channel_id=1, source_target_pairs={{0,1},{1,0},{2,3},{3,2},{4,5},{5,4},{6,7},{7,6},{8,9},{9,8},{10,11... | collective-permute-start | bytes 663560 | tf_op jit(solution)/shard_map/ppermute | solution.py:814
  140.6 51.8 %collective-permute-start.14 = (bf16[1,32,3456]{2,1,0:T(8,128)(2,1)S(1)}, bf16[1,32,3456]{2,1,0:T(8,128)(2,1)S(1)}, u32[]{:S(2)}, u32[]{:S(2)}) collective-permute-start(bf16[1,32,3456]{2,1,0:T(8,128)(2,1)S(1)} %bitcast.641), channel_id=1, source_target_pairs={{0,2},{1,3},{2,0},{3,1},{4,6},{5,7},{6,4},{7,5},{8,10},{9,11},{10,... | collective-permute-start | bytes 663560 | tf_op jit(solution)/shard_map/ppermute | solution.py:814
  141.2 51.2 %collective-permute-start.15 = (bf16[1,32,3456]{2,1,0:T(8,128)(2,1)S(1)}, bf16[1,32,3456]{2,1,0:T(8,128)(2,1)S(1)}, u32[]{:S(2)}, u32[]{:S(2)}) collective-permute-start(bf16[1,32,3456]{2,1,0:T(8,128)(2,1)S(1)} %bitcast.642), channel_id=1, source_target_pairs={{0,3},{1,2},{2,1},{3,0},{4,7},{5,6},{6,5},{7,4},{8,11},{9,10},{10,... | collective-permute-start | bytes 663560 | tf_op jit(solution)/shard_map/ppermute | solution.py:814
  193.4 18.9 %collective-permute-start.17 = (bf16[4,32,1920]{2,1,0:T(8,128)(2,1)}, bf16[4,32,1920]{2,1,0:T(8,128)(2,1)}, u32[]{:S(2)}, u32[]{:S(2)}) collective-permute-start(bf16[4,32,1920]{2,1,0:T(8,128)(2,1)} %pad_maximum_fusion.30), channel_id=1, source_target_pairs={{0,16},{4,20},{8,24},{12,28},{16,0},{20,4},{24,8},{28,12},{1,17},{... | collective-permute-start | bytes 1474568 | tf_op jit(solution)/shard_map/ppermute | solution.py:822
  195.8 16.5 %collective-permute-start.16 = (bf16[4,32,1536]{2,1,0:T(8,128)(2,1)}, bf16[4,32,1536]{2,1,0:T(8,128)(2,1)}, u32[]{:S(2)}, u32[]{:S(2)}) collective-permute-start(bf16[4,32,1536]{2,1,0:T(8,128)(2,1)} %pad_maximum_fusion.40), channel_id=1, source_target_pairs={{0,8},{4,12},{8,0},{12,4},{16,24},{20,28},{24,16},{28,20},{1,9},{5... | collective-permute-start | bytes 1179656 | tf_op jit(solution)/shard_map/ppermute | solution.py:822
  213.6 35.6 %collective-permute-start.19 = (bf16[2,4,32,1920]{3,2,1,0:T(8,128)(2,1)S(1)}, bf16[2,4,32,1920]{3,2,1,0:T(8,128)(2,1)S(1)}, u32[]{:S(2)}, u32[]{:S(2)}) collective-permute-start(bf16[2,4,32,1920]{3,2,1,0:T(8,128)(2,1)S(1)} %pad_maximum_fusion.11), channel_id=1, source_target_pairs={{0,8},{4,12},{8,0},{12,4},{16,24},{20,28},{24,16},{28,20},{1,9},{5... | collective-permute-start | bytes 2949128 | tf_op jit(solution)/shard_map/ppermute | solution.py:822
  215.5 27.3 %collective-permute-start.18 = (bf16[2,4,32,1536]{3,2,1,0:T(8,128)(2,1)S(1)}, bf16[2,4,32,1536]{3,2,1,0:T(8,128)(2,1)S(1)}, u32[]{:S(2)}, u32[]{:S(2)}) collective-permute-start(bf16[2,4,32,1536]{3,2,1,0:T(8,128)(2,1)S(1)} %pad_maximum_fusion.18), channel_id=1, source_target_pairs={{0,16},{4,20},{8,24},{12,28},{16,0},{20,4},{24,8},{28,12},{1,17},{... | collective-permute-start | bytes 2359304 | tf_op jit(solution)/shard_map/ppermute | solution.py:822
  250.9 22.1 %collective-permute-start.21 = (bf16[2,2,4,32,1920]{4,3,2,0,1:T(8,128)(2,1)}, bf16[2,2,4,32,1920]{4,3,2,0,1:T(8,128)(2,1)}, u32[]{:S(2)}, u32[]{:S(2)}) collective-permute-start(bf16[2,2,4,32,1920]{4,3,2,0,1:T(8,128)(2,1)} %pad_maximum_fusion.2), channel_id=1, source_target_pairs={{0,4},{4,0},{8,12},{12,8},{16,20},{20,16},{24,28},{28,24},{1,5},{5... | collective-permute-start | bytes 5898248 | tf_op jit(solution)/shard_map/ppermute | solution.py:822
  252.4 16.9 %collective-permute-start.20 = (bf16[2,2,4,32,1536]{4,3,2,1,0:T(8,128)(2,1)}, bf16[2,2,4,32,1536]{4,3,2,1,0:T(8,128)(2,1)}, u32[]{:S(2)}, u32[]{:S(2)}) collective-permute-start(bf16[2,2,4,32,1536]{4,3,2,1,0:T(8,128)(2,1)} %pad_maximum_fusion.5), channel_id=1, source_target_pairs={{0,4},{4,0},{8,12},{12,8},{16,20},{20,16},{24,28},{28,24},{1,5},{5... | collective-permute-start | bytes 4718600 | tf_op jit(solution)/shard_map/ppermute | solution.py:822
  281.3 54.3 %collective-permute-start.23 = (bf16[144,1024]{1,0:T(8,128)(2,1)S(1)}, bf16[144,1024]{1,0:T(8,128)(2,1)S(1)}, u32[]{:S(2)}, u32[]{:S(2)}) collective-permute-start(bf16[144,1024]{1,0:T(8,128)(2,1)S(1)} %get-tuple-element.403), channel_id=1, source_target_pairs={{0,0},{1,1},{4,2},{5,3},{2,4},{3,5},{6,6},{7,7},{8,8},{9,9},{12,10... | collective-permute-start | bytes 884744 | tf_op jit(solution)/shard_map/ppermute | solution.py:696
  282.0 54.4 %collective-permute-start.24 = (bf16[144,1024]{1,0:T(8,128)(2,1)S(1)}, bf16[144,1024]{1,0:T(8,128)(2,1)S(1)}, u32[]{:S(2)}, u32[]{:S(2)}) collective-permute-start(bf16[144,1024]{1,0:T(8,128)(2,1)S(1)} %get-tuple-element.402), channel_id=1, source_target_pairs={{1,0},{0,1},{5,2},{4,3},{3,4},{2,5},{7,6},{6,7},{9,8},{8,9},{13,10... | collective-permute-start | bytes 884744 | tf_op jit(solution)/shard_map/ppermute | solution.py:696
  282.4 54.6 %collective-permute-start.25 = (bf16[144,1024]{1,0:T(8,128)(2,1)S(1)}, bf16[144,1024]{1,0:T(8,128)(2,1)S(1)}, u32[]{:S(2)}, u32[]{:S(2)}) collective-permute-start(bf16[144,1024]{1,0:T(8,128)(2,1)S(1)} %get-tuple-element.401), channel_id=1, source_target_pairs={{0,0},{1,1},{2,4},{3,5},{4,2},{5,3},{6,6},{7,7},{8,8},{9,9},{10,12... | collective-permute-start | bytes 884744 | tf_op jit(solution)/shard_map/ppermute | solution.py:678
  283.1 53.9 %collective-permute-start.26 = (bf16[144,1024]{1,0:T(8,128)(2,1)S(1)}, bf16[144,1024]{1,0:T(8,128)(2,1)}, u32[]{:S(2)}, u32[]{:S(2)}) collective-permute-start(bf16[144,1024]{1,0:T(8,128)(2,1)S(1)} %get-tuple-element.400), channel_id=1, source_target_pairs={{0,1},{1,0},{2,5},{3,4},{4,3},{5,2},{6,7},{7,6},{8,9},{9,8},{10,13... | collective-permute-start | bytes 884744 | tf_op jit(solution)/shard_map/ppermute | solution.py:678
  391.7 529.7 %reduce-scatter.5.cloned.1.call-start = ((), (), s32[]{:S(2)}) async-start(), calls=%async_computation.5 | async-start | bytes 7299072 | tf_op jit(solution)/shard_map/reduce_scatter | solution.py:1024
  393.9 96.6 %collective-permute-start.27 = (bf16[144,1024]{1,0:T(8,128)(2,1)S(1)}, bf16[144,1024]{1,0:T(8,128)(2,1)}, u32[]{:S(2)}, u32[]{:S(2)}) collective-permute-start(bf16[144,1024]{1,0:T(8,128)(2,1)S(1)} %get-tuple-element.395), channel_id=1, source_target_pairs={{0,0},{1,1},{4,2},{5,3},{2,4},{3,5},{6,6},{7,7},{8,8},{9,9},{12,10... | collective-permute-start | bytes 884744 | tf_op jit(solution)/shard_map/ppermute | solution.py:696
  395.4 95.0 %collective-permute-start.28 = (bf16[144,1024]{1,0:T(8,128)(2,1)S(1)}, bf16[144,1024]{1,0:T(8,128)(2,1)}, u32[]{:S(2)}, u32[]{:S(2)}) collective-permute-start(bf16[144,1024]{1,0:T(8,128)(2,1)S(1)} %get-tuple-element.394), channel_id=1, source_target_pairs={{1,0},{0,1},{5,2},{4,3},{3,4},{2,5},{7,6},{6,7},{9,8},{8,9},{13,10... | collective-permute-start | bytes 884744 | tf_op jit(solution)/shard_map/ppermute | solution.py:696
  526.0 40.4 %collective-permute-start.30 = (bf16[4,4,128,1024]{3,2,1,0:T(8,128)(2,1)}, bf16[4,4,128,1024]{3,2,1,0:T(8,128)(2,1)}, u32[]{:S(2)}, u32[]{:S(2)}) collective-permute-start(bf16[4,4,128,1024]{3,2,1,0:T(8,128)(2,1)} %half_product.6), channel_id=1, source_target_pairs={{0,4},{4,0},{8,12},{12,8},{16,20},{20,16},{24,28},{28,24},{1,5},{5... | collective-permute-start | bytes 12582920 | tf_op jit(solution)/shard_map/ppermute | solution.py:1118
  570.6 43.7 %collective-permute-start.31 = (bf16[4,4,128,1024]{3,2,1,0:T(8,128)(2,1)S(1)}, bf16[4,4,128,1024]{3,2,1,0:T(8,128)(2,1)S(1)}, u32[]{:S(2)}, u32[]{:S(2)}) collective-permute-start(bf16[4,4,128,1024]{3,2,1,0:T(8,128)(2,1)S(1)} %half_product.8), channel_id=1, source_target_pairs={{0,4},{4,0},{8,12},{12,8},{16,20},{20,16},{24,28},{28,24},{1,5},{5... | collective-permute-start | bytes 12582920 | tf_op jit(solution)/shard_map/ppermute | solution.py:1118
  592.9 21.4 %collective-permute-start.32 = (bf16[1,4,128,1024]{3,2,1,0:T(8,128)(2,1)}, bf16[1,4,128,1024]{3,2,1,0:T(8,128)(2,1)S(1)}, u32[]{:S(2)}, u32[]{:S(2)}) collective-permute-start(bf16[1,4,128,1024]{3,2,1,0:T(8,128)(2,1)} %half_product.9), channel_id=1, source_target_pairs={{0,4},{4,0},{8,12},{12,8},{16,20},{20,16},{24,28},{28,24},{1,5},{5... | collective-permute-start | bytes 3145736 | tf_op jit(solution)/shard_map/ppermute | solution.py:1118
  623.7 76.9 %collective-permute-start.34 = (bf16[4,2,128,1024]{3,2,1,0:T(8,128)(2,1)}, bf16[4,2,128,1024]{3,2,1,0:T(8,128)(2,1)}, u32[]{:S(2)}, u32[]{:S(2)}) collective-permute-start(bf16[4,2,128,1024]{3,2,1,0:T(8,128)(2,1)} %get-tuple-element.209), channel_id=1, source_target_pairs={{0,8},{4,12},{8,0},{12,4},{16,24},{20,28},{24,16},{28,20},{1,9},{5... | collective-permute-start | bytes 6291464 | tf_op jit(solution)/shard_map/ppermute | solution.py:954
  625.1 75.5 %collective-permute-start.33 = (bf16[4,2,128,1024]{3,2,1,0:T(8,128)(2,1)}, bf16[4,2,128,1024]{3,2,1,0:T(8,128)(2,1)}, u32[]{:S(2)}, u32[]{:S(2)}) collective-permute-start(bf16[4,2,128,1024]{3,2,1,0:T(8,128)(2,1)} %get-tuple-element.207), channel_id=1, source_target_pairs={{0,16},{4,20},{8,24},{12,28},{16,0},{20,4},{24,8},{28,12},{1,17},{... | collective-permute-start | bytes 6291464 | tf_op jit(solution)/shard_map/ppermute | solution.py:954
  649.1 51.4 %collective-permute-start.35 = (bf16[1,2,128,1024]{3,2,1,0:T(8,128)(2,1)S(1)}, bf16[1,2,128,1024]{3,2,1,0:T(8,128)(2,1)S(1)}, u32[]{:S(2)}, u32[]{:S(2)}) collective-permute-start(bf16[1,2,128,1024]{3,2,1,0:T(8,128)(2,1)S(1)} %get-tuple-element.211), channel_id=1, source_target_pairs={{0,8},{4,12},{8,0},{12,4},{16,24},{20,28},{24,16},{28,20},{1,9},{5... | collective-permute-start | bytes 1572872 | tf_op jit(solution)/shard_map/ppermute | solution.py:954
  704.6 75.1 %collective-permute-start.37 = (bf16[5,1,128,1024]{3,2,1,0:T(8,128)(2,1)}, bf16[5,1,128,1024]{3,2,1,0:T(8,128)(2,1)}, u32[]{:S(2)}, u32[]{:S(2)}) collective-permute-start(bf16[5,1,128,1024]{3,2,1,0:T(8,128)(2,1)} %fusion.108), channel_id=1, source_target_pairs={{0,16},{4,20},{8,24},{12,28},{16,0},{20,4},{24,8},{28,12},{1,17},{... | collective-permute-start | bytes 3932168 | tf_op jit(solution)/shard_map/ppermute | solution.py:954
  709.1 70.6 %collective-permute-start.36 = (bf16[4,1,128,1024]{3,2,1,0:T(8,128)(2,1)}, bf16[4,1,128,1024]{3,2,1,0:T(8,128)(2,1)}, u32[]{:S(2)}, u32[]{:S(2)}) collective-permute-start(bf16[4,1,128,1024]{3,2,1,0:T(8,128)(2,1)} %constant_dynamic-slice_fusion.3), channel_id=1, source_target_pairs={{0,8},{4,12},{8,0},{12,4},{16,24},{20,28},{24,16},{28,20},{1,9},{5... | collective-permute-start | bytes 3145736 | tf_op jit(solution)/shard_map/ppermute | solution.py:954
  716.5 61.7 %collective-permute-start.38 = (bf16[2,288,512]{2,1,0:T(8,128)(2,1)}, bf16[2,288,512]{2,1,0:T(8,128)(2,1)}, u32[]{:S(2)}, u32[]{:S(2)}) collective-permute-start(bf16[2,288,512]{2,1,0:T(8,128)(2,1)} %slice_bitcast_fusion.154), channel_id=1, source_target_pairs={{0,4},{1,5},{2,6},{3,7},{4,0},{5,1},{6,2},{7,3},{8,12},{9,13},{10,... | collective-permute-start | bytes 1769480 | tf_op jit(solution)/shard_map/ppermute | solution.py:755
  789.3 37.4 %collective-permute-start.43 = (bf16[32,9216]{1,0:T(8,128)(2,1)}, bf16[32,9216]{1,0:T(8,128)(2,1)}, u32[]{:S(2)}, u32[]{:S(2)}) collective-permute-start(bf16[32,9216]{1,0:T(8,128)(2,1)} %get-tuple-element.330), channel_id=1, source_target_pairs={{0,1},{1,0},{2,3},{3,2},{4,5},{5,4},{6,7},{7,6},{8,9},{9,8},{10,11... | collective-permute-start | bytes 1769480 | tf_op jit(solution)/shard_map/ppermute | solution.py:983
  789.4 52.1 %collective-permute-start.44 = (bf16[32,9216]{1,0:T(8,128)(2,1)}, bf16[32,9216]{1,0:T(8,128)(2,1)}, u32[]{:S(2)}, u32[]{:S(2)}) collective-permute-start(bf16[32,9216]{1,0:T(8,128)(2,1)} %get-tuple-element.329), channel_id=1, source_target_pairs={{0,2},{1,3},{2,0},{3,1},{4,6},{5,7},{6,4},{7,5},{8,10},{9,11},{10,... | collective-permute-start | bytes 1769480 | tf_op jit(solution)/shard_map/ppermute | solution.py:983
  791.2 50.2 %collective-permute-start.45 = (bf16[32,9216]{1,0:T(8,128)(2,1)}, bf16[32,9216]{1,0:T(8,128)(2,1)}, u32[]{:S(2)}, u32[]{:S(2)}) collective-permute-start(bf16[32,9216]{1,0:T(8,128)(2,1)} %get-tuple-element.328), channel_id=1, source_target_pairs={{0,3},{1,2},{2,1},{3,0},{4,7},{5,6},{6,5},{7,4},{8,11},{9,10},{10,... | collective-permute-start | bytes 1769480 | tf_op jit(solution)/shard_map/ppermute | solution.py:983
  806.9 35.3 %collective-permute-start.40 = (bf16[512,2048]{1,0:T(8,128)(2,1)}, bf16[512,2048]{1,0:T(8,128)(2,1)}, u32[]{:S(2)}, u32[]{:S(2)}) collective-permute-start(bf16[512,2048]{1,0:T(8,128)(2,1)} %add_convert_fusion.2), channel_id=1, source_target_pairs={{0,4},{4,0},{8,12},{12,8},{16,20},{20,16},{24,28},{28,24},{1,5},{5... | collective-permute-start | bytes 6291464 | tf_op jit(solution)/shard_map/ppermute | solution.py:1140
  809.8 31.7 %collective-permute-start.41 = (bf16[512,1024]{1,0:T(8,128)(2,1)}, bf16[512,1024]{1,0:T(8,128)(2,1)}, u32[]{:S(2)}, u32[]{:S(2)}) collective-permute-start(bf16[512,1024]{1,0:T(8,128)(2,1)} %convolution_convert_fusion.1), channel_id=1, source_target_pairs={{0,4},{4,0},{8,12},{12,8},{16,20},{20,16},{24,28},{28,24},{1,5},{5... | collective-permute-start | bytes 3145736 | tf_op jit(solution)/shard_map/ppermute | solution.py:1140
  849.6 35.5 %collective-permute-start.47 = (bf16[1,2,128,1664]{3,2,1,0:T(8,128)(2,1)}, bf16[1,2,128,1664]{3,2,1,0:T(8,128)(2,1)}, u32[]{:S(2)}, u32[]{:S(2)}) collective-permute-start(bf16[1,2,128,1664]{3,2,1,0:T(8,128)(2,1)} %dynamic-slice_bitcast_fusion.1), channel_id=1, source_target_pairs={{0,8},{4,12},{8,0},{12,4},{16,24},{20,28},{24,16},{28,20},{1,9},{5... | collective-permute-start | bytes 2555912 | tf_op jit(solution)/shard_map/ppermute | solution.py:954
  851.3 33.8 %collective-permute-start.46 = (bf16[1,2,128,1792]{3,2,1,0:T(8,128)(2,1)}, bf16[1,2,128,1792]{3,2,1,0:T(8,128)(2,1)}, u32[]{:S(2)}, u32[]{:S(2)}) collective-permute-start(bf16[1,2,128,1792]{3,2,1,0:T(8,128)(2,1)} %dynamic-slice_bitcast_fusion), channel_id=1, source_target_pairs={{0,16},{4,20},{8,24},{12,28},{16,0},{20,4},{24,8},{28,12},{1,17},{... | collective-permute-start | bytes 2752520 | tf_op jit(solution)/shard_map/ppermute | solution.py:954
  853.7 31.4 %collective-permute-start.48 = (bf16[144,1024]{1,0:T(8,128)(2,1)}, bf16[144,1024]{1,0:T(8,128)(2,1)}, u32[]{:S(2)}, u32[]{:S(2)}) collective-permute-start(bf16[144,1024]{1,0:T(8,128)(2,1)} %get-tuple-element.387), channel_id=1, source_target_pairs={{0,0},{1,1},{4,2},{5,3},{2,4},{3,5},{6,6},{7,7},{8,8},{9,9},{12,10... | collective-permute-start | bytes 884744 | tf_op jit(solution)/shard_map/ppermute | solution.py:696
  857.5 27.6 %collective-permute-start.49 = (bf16[144,1024]{1,0:T(8,128)(2,1)}, bf16[144,1024]{1,0:T(8,128)(2,1)}, u32[]{:S(2)}, u32[]{:S(2)}) collective-permute-start(bf16[144,1024]{1,0:T(8,128)(2,1)} %get-tuple-element.386), channel_id=1, source_target_pairs={{1,0},{0,1},{5,2},{4,3},{3,4},{2,5},{7,6},{6,7},{9,8},{8,9},{13,10... | collective-permute-start | bytes 884744 | tf_op jit(solution)/shard_map/ppermute | solution.py:696
  903.7 16.9 %collective-permute-start.53 = (bf16[32,3456]{1,0:T(8,128)(2,1)S(1)}, bf16[32,3456]{1,0:T(8,128)(2,1)S(1)}, u32[]{:S(2)}, u32[]{:S(2)}) collective-permute-start(bf16[32,3456]{1,0:T(8,128)(2,1)S(1)} %get-tuple-element.363), channel_id=1, source_target_pairs={{0,2},{1,3},{2,0},{3,1},{4,6},{5,7},{6,4},{7,5},{8,10},{9,11},{10,... | collective-permute-start | bytes 663560 | tf_op jit(solution)/shard_map/ppermute | solution.py:983
  904.3 16.4 %collective-permute-start.54 = (bf16[32,3456]{1,0:T(8,128)(2,1)S(1)}, bf16[32,3456]{1,0:T(8,128)(2,1)S(1)}, u32[]{:S(2)}, u32[]{:S(2)}) collective-permute-start(bf16[32,3456]{1,0:T(8,128)(2,1)S(1)} %get-tuple-element.361), channel_id=1, source_target_pairs={{0,3},{1,2},{2,1},{3,0},{4,7},{5,6},{6,5},{7,4},{8,11},{9,10},{10,... | collective-permute-start | bytes 663560 | tf_op jit(solution)/shard_map/ppermute | solution.py:983
  (203 other events, 1835.4 us)
Sparse Core Ops, SparseCore 0:
  13.3 176.8 all-gather.2
  193.2 153.9 all-gather.4
  391.8 207.7 reduce-scatter.2
  712.4 147.4 reduce-scatter.4
